TPU v7x, 512 devices: a whole 4x4x16 slice. The times are simulated.
512 devices in a mesh: lat: 32 (over x, z_lo), lon: 16 (over y, z_hi, core).
Axes of the slice: x: 4, y: 4, z: 16 (z_hi: 2, z_lo: 8; z = z_hi * 8 + z_lo), core: 2. Of those that a mesh axis runs over, the one named last changes fastest.
Arguments:
- state: float32 [4, 2, 768, 2048], P(None, None, 'lat', 'lon'), may hold values from -6 to 6
- zonal_shift: int32 [2, 768], P(None, 'lat'), may hold values from -1024 to 1024, as said below
- zonal_cells: int32 [2, 768, 2048], P(None, 'lat', 'lon'), may hold values from -2 to 2
- zonal_fraction: float32 [2, 768, 2048], P(None, 'lat', 'lon'), may hold values from 0 to 1
- merid_cells: int32 [2, 768, 2048], P(None, 'lat', 'lon'), may hold values from -1 to 1
- merid_fraction: float32 [2, 768, 2048], P(None, 'lat', 'lon'), may hold values from 0 to 1
- coupling: float32 [2, 768, 2048], P(None, 'lat', 'lon'), may hold values from 0.5 to 8
Outputs:
- advanced: float32 [4, 2, 768, 2048], P(None, None, 'lat', 'lon')
Inputs may be any that keep to these rules, and one draw needn't show every extreme that they name: `zonal_shift`: one whole-cell zonal displacement for each level and latitude row; bounded more tightly near the equator than near the poles.
All inputs are finite; a program needn't handle non-finite values.
Results may differ from a plain program's by a relative error of at most 0.00002.
Values sent between devices are 32-bit elements; how exact they have to be, the bound alone decides.
No kernel may reach another device: no remote copies, remote signals or barrier semaphores. Data moves between devices by JAX's collectives and lax.ppermute only.
A program may use at most 128 MiB of HBM per device.

v0:
```python
import jax
import jax.numpy as jnp
from jax import lax
from jax.sharding import PartitionSpec as P

SWEEPS = 4


spare_columns = 7


def from_behind(value, axis, steps):
    count = lax.axis_size(axis)
    pairs = [(source, (source + steps) % count) for source in range(count)]
    return lax.ppermute(value, axis, pairs)


def with_halo(value, sides, width, wrap):
    for axis, dim in sides:
        size, length = (lax.axis_size(axis), value.shape[dim])
        up = [(i, (i + 1) % size) for i in range(size if wrap else size - 1)]
        down = [(j, i) for i, j in up]
        last = lax.slice_in_dim(value, length - width, length, axis=dim)
        leading = lax.slice_in_dim(value, 0, width, axis=dim)
        before = lax.ppermute(last, axis, up)
        after = lax.ppermute(leading, axis, down)
        value = jnp.concatenate([before, value, after], axis=dim)
    return value


def cubic_weights(frac):
    return (
        -frac * (frac - 1.0) * (frac - 2.0) / 6.0,
        (frac + 1.0) * (frac - 1.0) * (frac - 2.0) / 2.0,
        -(frac + 1.0) * frac * (frac - 2.0) / 2.0,
        (frac + 1.0) * frac * (frac - 1.0) / 6.0,
    )


def window_rows(block, starts, length):

    def take_one(piece, begin):
        return lax.dynamic_slice_in_dim(piece, begin, length, 1)

    return jax.vmap(take_one, in_axes=(1, 0), out_axes=1)(block, starts)


def pick_cells(window, weights, cells, width):
    result = jnp.zeros(window.shape[:-1] + (width,), jnp.float32)
    for offset in range(-2, 3):
        part = jnp.zeros(result.shape, jnp.float32)
        for k in range(4):
            begin = k - 1 - offset + 3
            part = part + weights[k] * window[..., begin : begin + width]
        result = jnp.where(cells == offset, part, result)
    return result


def body(state, zonal_shift, zonal_cells, zonal_fraction, merid_cells, merid_fraction, coupling):
    fields, levels, rows, width = state.shape
    sectors = lax.axis_size("lon")
    bands = lax.axis_size("lat")
    circle = width * sectors
    band_index = lax.axis_index("lat")
    count = levels * rows
    moved_shift = jnp.mod(zonal_shift + 3, circle)
    hops = moved_shift // width
    within = moved_shift - hops * width
    current = state
    for bit in range((sectors - 1).bit_length()):
        arrived = from_behind(current, "lon", 2**bit)
        taken = hops // 2**bit % 2 == 1
        current = jnp.where(taken[None, :, :, None], arrived, current)
    prior = from_behind(current, "lon", 1)
    after = from_behind(current[..., :spare_columns], "lon", -1)
    extended = jnp.concatenate([prior, current, after], axis=3)
    starts = (width - within).reshape(count)
    window = window_rows(
        extended.reshape(fields, count, 2 * width + spare_columns), starts, width + spare_columns
    )
    window = window.reshape(fields, levels, rows, width + spare_columns)
    weights = tuple((w[None] for w in cubic_weights(zonal_fraction)))
    zonal = pick_cells(window, weights, zonal_cells[None], width)
    padded = with_halo(zonal, (("lat", 2),), 3, False)
    merid_w = cubic_weights(merid_fraction)
    source = jnp.zeros(state.shape, jnp.float32)
    for offset in range(-1, 2):
        part = jnp.zeros(state.shape, jnp.float32)
        for k in range(4):
            begin = 3 - offset + k - 1
            part = part + merid_w[k][None] * padded[..., begin : begin + rows, :]
        source = jnp.where((merid_cells == offset)[None], part, source)
    rim_rows = jnp.arange(rows + 2, dtype=jnp.int32)
    dropped = (rim_rows == 0) & (band_index == 0) | (rim_rows == rows + 1) & (
        band_index == bands - 1
    )
    rim_keep = jnp.where(dropped, 0.0, 1.0).astype(jnp.float32)[:, None]
    phi = source
    for sweep in range(SWEEPS):
        rimmed = with_halo(phi, (("lat", 2), ("lon", 3)), 1, True)
        rimmed = rimmed * rim_keep
        beside = rimmed[..., :-2, 1:-1] + rimmed[..., 2:, 1:-1]
        beside = beside + rimmed[..., 1:-1, :-2] + rimmed[..., 1:-1, 2:]
        phi = (source + coupling * beside) / (1.0 + 4.0 * coupling)
    return phi


def solution(mesh):
    in_specs = (
        P(None, None, "lat", "lon"),
        P(None, "lat"),
        P(None, "lat", "lon"),
        P(None, "lat", "lon"),
        P(None, "lat", "lon"),
        P(None, "lat", "lon"),
        P(None, "lat", "lon"),
    )
    out_specs = P(None, None, "lat", "lon")
    return jax.shard_map(body, mesh=mesh, in_specs=in_specs, out_specs=out_specs, check_vma=False)
```

profile of v0, /device:TPU:505, one launch (start us, length us, event | category | flops | bytes accessed | tf_op | source)
XLA Modules:
  0.0 278.0 jit_solution(15304844866838023922)
XLA Ops:
  0.0 6.3 %collective-permute-start = (f32[4,2,24,128]{3,2,1,0:T(8,128)}, f32[4,2,24,128]{3,2,1,0:T(8,128)S(1)}, u32[]{:S(2)}, u32[]{:S(2)}) collective-permute-start(f32[4,2,24,128]{3,2,1,0:T(8,128)} %param.7), channel_id=1, source_target_pairs={{0,1},{1,2},{2,3},{3,4},{4,5},{5,6},{6,7},{7,8},{8,9},{9,10},{10,1... | collective-permute-start | bytes 294920 | tf_op jit(solution)/shard_map/ppermute | solution.py:15
  9.2 7.9 %collective-permute-start.1 = (f32[4,2,24,128]{3,2,1,0:T(8,128)S(1)}, f32[4,2,24,128]{3,2,1,0:T(8,128)S(1)}, u32[]{:S(2)}, u32[]{:S(2)}) collective-permute-start(f32[4,2,24,128]{3,2,1,0:T(8,128)S(1)} %broadcast_select_fusion), channel_id=1, source_target_pairs={{0,2},{1,3},{2,4},{3,5},{4,6},{5,7},{6,8},{7,9},{8,10},{9,11},{10,... | collective-permute-start | bytes 294920 | tf_op jit(solution)/shard_map/ppermute | solution.py:15
  18.5 4.7 %collective-permute-done.1 = f32[4,2,24,128]{3,2,1,0:T(8,128)S(1)} collective-permute-done((f32[4,2,24,128]{3,2,1,0:T(8,128)S(1)}, f32[4,2,24,128]{3,2,1,0:T(8,128)S(1)}, u32[]{:S(2)}, u32[]{:S(2)}) %collective-permute-start.1) | collective-permute-done | bytes 98336 | tf_op jit(solution)/shard_map/ppermute | solution.py:15
  23.3 3.2 %collective-permute-start.2 = (f32[4,2,24,128]{3,2,1,0:T(8,128)S(1)}, f32[4,2,24,128]{3,2,1,0:T(8,128)S(1)}, u32[]{:S(2)}, u32[]{:S(2)}) collective-permute-start(f32[4,2,24,128]{3,2,1,0:T(8,128)S(1)} %broadcast_select_fusion.1), channel_id=1, source_target_pairs={{0,4},{1,5},{2,6},{3,7},{4,8},{5,9},{6,10},{7,11},{8,12},{9,13},{1... | collective-permute-start | bytes 294920 | tf_op jit(solution)/shard_map/ppermute | solution.py:15
  28.8 4.1 %collective-permute-start.3 = (f32[4,2,24,128]{3,2,1,0:T(8,128)S(1)}, f32[4,2,24,128]{3,2,1,0:T(8,128)S(1)}, u32[]{:S(2)}, u32[]{:S(2)}) collective-permute-start(f32[4,2,24,128]{3,2,1,0:T(8,128)S(1)} %broadcast_select_fusion.2), channel_id=1, source_target_pairs={{0,8},{1,9},{2,10},{3,11},{4,12},{5,13},{6,14},{7,15},{8,0},{9,1},... | collective-permute-start | bytes 294920 | tf_op jit(solution)/shard_map/ppermute | solution.py:15
  35.8 22.8 %collective-permute-start.4 = (f32[4,2,24,128]{3,2,1,0:T(8,128)S(1)}, f32[4,2,24,128]{3,2,1,0:T(8,128)S(1)}, u32[]{:S(2)}, u32[]{:S(2)}) collective-permute-start(f32[4,2,24,128]{3,2,1,0:T(8,128)S(1)} %broadcast_select_fusion.3), channel_id=1, source_target_pairs={{0,1},{1,2},{2,3},{3,4},{4,5},{5,6},{6,7},{7,8},{8,9},{9,10},{10,1... | collective-permute-start | bytes 294920 | tf_op jit(solution)/shard_map/ppermute | solution.py:15
  60.5 17.1 %collective-permute-done.5 = f32[4,2,24,7]{3,2,1,0:T(8,128)S(1)} collective-permute-done((f32[4,2,24,7]{3,2,1,0:T(8,128)S(1)}, f32[4,2,24,7]{3,2,1,0:T(8,128)S(1)}, u32[]{:S(2)}, u32[]{:S(2)}) %collective-permute-start.5) | collective-permute-done | bytes 5408 | tf_op jit(solution)/shard_map/ppermute | solution.py:15
  77.6 5.4 %copy.8 = f32[4,2,24,263]{0,2,1,3:T(8,128)} copy(f32[4,2,24,263]{3,2,1,0:T(8,128)S(1)} %pad_maximum_fusion) | data formatting | bytes 403968 | tf_op jit(solution)/shard_map/concatenate | solution.py:76
  83.1 7.5 %gather_fusion = f32[48,4,135]{1,0,2:T(8,128)S(1)} fusion(f32[48,4,263]{1,0,2:T(8,128)} %bitcast.10, s32[48]{0:T(128)S(1)} %fusion.49), kind=kCustom, calls=%fused_computation | custom fusion | bytes 207936 | tf_op jit(solution)/shard_map/vmap()/gather | solution.py:43
  90.5 8.5 %fusion.50 = (f32[4,2,24,128]{0,2,1,3:T(8,128)}, f32[4,2,24,128]{0,2,1,3:T(8,128)}, f32[4,2,24,128]{0,2,1,3:T(8,128)}, f32[4,2,24,128]{0,2,1,3:T(8,128)}, f32[4,...) fusion(f32[4,2,24,135]{0,2,1,3:T(8,128)S(1)} %bitcast.9), kind=kLoop, calls=%fused_computation.135 | loop fusion | bytes 1572864 | tf_op jit(solution)/shard_map/slice | solution.py:54
  105.6 3.0 %copy.20 = f32[4,2,24,128]{3,2,1,0:T(8,128)} copy(f32[4,2,24,128]{0,2,1,3:T(8,128)} %get-tuple-element.11) | data formatting | bytes 196608
  110.4 3.2 %copy.22 = f32[4,2,24,128]{3,2,1,0:T(8,128)} copy(f32[4,2,24,128]{0,2,1,3:T(8,128)} %get-tuple-element.9) | data formatting | bytes 196608
  113.6 3.0 %copy.23 = f32[4,2,24,128]{3,2,1,0:T(8,128)} copy(f32[4,2,24,128]{0,2,1,3:T(8,128)} %get-tuple-element.8) | data formatting | bytes 196608
  119.8 2.8 %collective-permute-start.6 = (f32[4,2,3,128]{3,2,1,0:T(4,128)S(1)}, f32[4,2,3,128]{3,2,1,0:T(4,128)S(1)}, u32[]{:S(2)}, u32[]{:S(2)}) collective-permute-start(f32[4,2,3,128]{3,2,1,0:T(4,128)S(1)} %get-tuple-element.32), channel_id=1, source_target_pairs={{0,16},{16,32},{32,48},{48,64},{64,80},{80,96},{96,112},{112,128},... | collective-permute-start | bytes 36872 | tf_op jit(solution)/shard_map/ppermute | solution.py:25
  122.6 3.0 %collective-permute-start.7 = (f32[4,2,3,128]{3,2,1,0:T(4,128)S(1)}, f32[4,2,3,128]{3,2,1,0:T(4,128)S(1)}, u32[]{:S(2)}, u32[]{:S(2)}) collective-permute-start(f32[4,2,3,128]{3,2,1,0:T(4,128)S(1)} %get-tuple-element.31), channel_id=1, source_target_pairs={{16,0},{32,16},{48,32},{64,48},{80,64},{96,80},{112,96},{128,112},... | collective-permute-start | bytes 36872 | tf_op jit(solution)/shard_map/ppermute | solution.py:26
  126.4 8.2 %collective-permute-done.7 = f32[4,2,3,128]{3,2,1,0:T(4,128)S(1)} collective-permute-done((f32[4,2,3,128]{3,2,1,0:T(4,128)S(1)}, f32[4,2,3,128]{3,2,1,0:T(4,128)S(1)}, u32[]{:S(2)}, u32[]{:S(2)}) %collective-permute-start.7) | collective-permute-done | bytes 12320 | tf_op jit(solution)/shard_map/ppermute | solution.py:26
  137.4 3.4 %collective-permute-start.9 = (f32[4,2,1,128]{3,2,1,0:T(1,128)S(1)}, f32[4,2,1,128]{3,2,1,0:T(1,128)S(1)}, u32[]{:S(2)}, u32[]{:S(2)}) collective-permute-start(f32[4,2,1,128]{3,2,1,0:T(1,128)S(1)} %get-tuple-element.30), channel_id=1, source_target_pairs={{16,0},{32,16},{48,32},{64,48},{80,64},{96,80},{112,96},{128,112},... | collective-permute-start | bytes 12296 | tf_op jit(solution)/shard_map/ppermute | solution.py:26
  140.8 8.6 %collective-permute-done.9 = f32[4,2,1,128]{3,2,1,0:T(1,128)S(1)} collective-permute-done((f32[4,2,1,128]{3,2,1,0:T(1,128)S(1)}, f32[4,2,1,128]{3,2,1,0:T(1,128)S(1)}, u32[]{:S(2)}, u32[]{:S(2)}) %collective-permute-start.9) | collective-permute-done | bytes 4128 | tf_op jit(solution)/shard_map/ppermute | solution.py:26
  149.6 3.9 %collective-permute-start.10 = (f32[4,2,26,1]{3,2,1,0:T(8,128)S(1)}, f32[4,2,26,1]{3,2,1,0:T(8,128)S(1)}, u32[]{:S(2)}, u32[]{:S(2)}) collective-permute-start(f32[4,2,26,1]{3,2,1,0:T(8,128)S(1)} %get-tuple-element.21), channel_id=1, source_target_pairs={{0,1},{1,2},{2,3},{3,4},{4,5},{5,6},{6,7},{7,8},{8,9},{9,10},{10,1... | collective-permute-start | bytes 2504 | tf_op jit(solution)/shard_map/ppermute | solution.py:25
  156.6 14.0 %collective-permute-done.11 = f32[4,2,26,1]{3,2,1,0:T(8,128)S(1)} collective-permute-done((f32[4,2,26,1]{3,2,1,0:T(8,128)S(1)}, f32[4,2,26,1]{3,2,1,0:T(8,128)S(1)}, u32[]{:S(2)}, u32[]{:S(2)}) %collective-permute-start.11) | collective-permute-done | bytes 864 | tf_op jit(solution)/shard_map/ppermute | solution.py:26
  173.0 3.4 %collective-permute-start.13 = (f32[4,2,1,128]{3,2,1,0:T(1,128)S(1)}, f32[4,2,1,128]{3,2,1,0:T(1,128)S(1)}, u32[]{:S(2)}, u32[]{:S(2)}) collective-permute-start(f32[4,2,1,128]{3,2,1,0:T(1,128)S(1)} %get-tuple-element.28), channel_id=1, source_target_pairs={{16,0},{32,16},{48,32},{64,48},{80,64},{96,80},{112,96},{128,112},... | collective-permute-start | bytes 12296 | tf_op jit(solution)/shard_map/ppermute | solution.py:26
  176.3 8.8 %collective-permute-done.13 = f32[4,2,1,128]{3,2,1,0:T(1,128)S(1)} collective-permute-done((f32[4,2,1,128]{3,2,1,0:T(1,128)S(1)}, f32[4,2,1,128]{3,2,1,0:T(1,128)S(1)}, u32[]{:S(2)}, u32[]{:S(2)}) %collective-permute-start.13) | collective-permute-done | bytes 4128 | tf_op jit(solution)/shard_map/ppermute | solution.py:26
  185.3 5.1 %collective-permute-start.14 = (f32[4,2,26,1]{3,2,1,0:T(8,128)S(1)}, f32[4,2,26,1]{3,2,1,0:T(8,128)S(1)}, u32[]{:S(2)}, u32[]{:S(2)}) collective-permute-start(f32[4,2,26,1]{3,2,1,0:T(8,128)S(1)} %get-tuple-element.19), channel_id=1, source_target_pairs={{0,1},{1,2},{2,3},{3,4},{4,5},{5,6},{6,7},{7,8},{8,9},{9,10},{10,1... | collective-permute-start | bytes 2504 | tf_op jit(solution)/shard_map/ppermute | solution.py:25
  192.5 15.0 %collective-permute-done.15 = f32[4,2,26,1]{3,2,1,0:T(8,128)S(1)} collective-permute-done((f32[4,2,26,1]{3,2,1,0:T(8,128)S(1)}, f32[4,2,26,1]{3,2,1,0:T(8,128)S(1)}, u32[]{:S(2)}, u32[]{:S(2)}) %collective-permute-start.15) | collective-permute-done | bytes 864 | tf_op jit(solution)/shard_map/ppermute | solution.py:26
  209.9 3.4 %collective-permute-start.17 = (f32[4,2,1,128]{3,2,1,0:T(1,128)S(1)}, f32[4,2,1,128]{3,2,1,0:T(1,128)S(1)}, u32[]{:S(2)}, u32[]{:S(2)}) collective-permute-start(f32[4,2,1,128]{3,2,1,0:T(1,128)S(1)} %get-tuple-element.26), channel_id=1, source_target_pairs={{16,0},{32,16},{48,32},{64,48},{80,64},{96,80},{112,96},{128,112},... | collective-permute-start | bytes 12296 | tf_op jit(solution)/shard_map/ppermute | solution.py:26
  213.3 8.6 %collective-permute-done.17 = f32[4,2,1,128]{3,2,1,0:T(1,128)S(1)} collective-permute-done((f32[4,2,1,128]{3,2,1,0:T(1,128)S(1)}, f32[4,2,1,128]{3,2,1,0:T(1,128)S(1)}, u32[]{:S(2)}, u32[]{:S(2)}) %collective-permute-start.17) | collective-permute-done | bytes 4128 | tf_op jit(solution)/shard_map/ppermute | solution.py:26
  221.9 3.2 %collective-permute-start.18 = (f32[4,2,26,1]{3,2,1,0:T(8,128)S(1)}, f32[4,2,26,1]{3,2,1,0:T(8,128)S(1)}, u32[]{:S(2)}, u32[]{:S(2)}) collective-permute-start(f32[4,2,26,1]{3,2,1,0:T(8,128)S(1)} %get-tuple-element.17), channel_id=1, source_target_pairs={{0,1},{1,2},{2,3},{3,4},{4,5},{5,6},{6,7},{7,8},{8,9},{9,10},{10,1... | collective-permute-start | bytes 2504 | tf_op jit(solution)/shard_map/ppermute | solution.py:25
  227.1 15.3 %collective-permute-done.19 = f32[4,2,26,1]{3,2,1,0:T(8,128)S(1)} collective-permute-done((f32[4,2,26,1]{3,2,1,0:T(8,128)S(1)}, f32[4,2,26,1]{3,2,1,0:T(8,128)S(1)}, u32[]{:S(2)}, u32[]{:S(2)}) %collective-permute-start.19) | collective-permute-done | bytes 864 | tf_op jit(solution)/shard_map/ppermute | solution.py:26
  244.7 3.4 %collective-permute-start.21 = (f32[4,2,1,128]{3,2,1,0:T(1,128)S(1)}, f32[4,2,1,128]{3,2,1,0:T(1,128)S(1)}, u32[]{:S(2)}, u32[]{:S(2)}) collective-permute-start(f32[4,2,1,128]{3,2,1,0:T(1,128)S(1)} %get-tuple-element.24), channel_id=1, source_target_pairs={{16,0},{32,16},{48,32},{64,48},{80,64},{96,80},{112,96},{128,112},... | collective-permute-start | bytes 12296 | tf_op jit(solution)/shard_map/ppermute | solution.py:26
  248.1 8.9 %collective-permute-done.21 = f32[4,2,1,128]{3,2,1,0:T(1,128)S(1)} collective-permute-done((f32[4,2,1,128]{3,2,1,0:T(1,128)S(1)}, f32[4,2,1,128]{3,2,1,0:T(1,128)S(1)}, u32[]{:S(2)}, u32[]{:S(2)}) %collective-permute-start.21) | collective-permute-done | bytes 4128 | tf_op jit(solution)/shard_map/ppermute | solution.py:26
  257.1 2.8 %collective-permute-start.22 = (f32[4,2,26,1]{3,2,1,0:T(8,128)S(1)}, f32[4,2,26,1]{3,2,1,0:T(8,128)S(1)}, u32[]{:S(2)}, u32[]{:S(2)}) collective-permute-start(f32[4,2,26,1]{3,2,1,0:T(8,128)S(1)} %get-tuple-element.15), channel_id=1, source_target_pairs={{0,1},{1,2},{2,3},{3,4},{4,5},{5,6},{6,7},{7,8},{8,9},{9,10},{10,1... | collective-permute-start | bytes 2504 | tf_op jit(solution)/shard_map/ppermute | solution.py:25
  261.8 15.2 %collective-permute-done.23 = f32[4,2,26,1]{3,2,1,0:T(8,128)S(1)} collective-permute-done((f32[4,2,26,1]{3,2,1,0:T(8,128)S(1)}, f32[4,2,26,1]{3,2,1,0:T(8,128)S(1)}, u32[]{:S(2)}, u32[]{:S(2)}) %collective-permute-start.23) | collective-permute-done | bytes 864 | tf_op jit(solution)/shard_map/ppermute | solution.py:26
  (73 shorter events, 43.9 us)
Async XLA Ops:
  0.0 8.2 %collective-permute-start = (f32[4,2,24,128]{3,2,1,0:T(8,128)}, f32[4,2,24,128]{3,2,1,0:T(8,128)S(1)}, u32[]{:S(2)}, u32[]{:S(2)}) collective-permute-start(f32[4,2,24,128]{3,2,1,0:T(8,128)} %param.7), channel_id=1, source_target_pairs={{0,1},{1,2},{2,3},{3,4},{4,5},{5,6},{6,7},{7,8},{8,9},{9,10},{10,1... | collective-permute-start | bytes 294920 | tf_op jit(solution)/shard_map/ppermute | solution.py:15
  9.2 14.1 %collective-permute-start.1 = (f32[4,2,24,128]{3,2,1,0:T(8,128)S(1)}, f32[4,2,24,128]{3,2,1,0:T(8,128)S(1)}, u32[]{:S(2)}, u32[]{:S(2)}) collective-permute-start(f32[4,2,24,128]{3,2,1,0:T(8,128)S(1)} %broadcast_select_fusion), channel_id=1, source_target_pairs={{0,2},{1,3},{2,4},{3,5},{4,6},{5,7},{6,8},{7,9},{8,10},{9,11},{10,... | collective-permute-start | bytes 294920 | tf_op jit(solution)/shard_map/ppermute | solution.py:15
  23.3 5.4 %collective-permute-start.2 = (f32[4,2,24,128]{3,2,1,0:T(8,128)S(1)}, f32[4,2,24,128]{3,2,1,0:T(8,128)S(1)}, u32[]{:S(2)}, u32[]{:S(2)}) collective-permute-start(f32[4,2,24,128]{3,2,1,0:T(8,128)S(1)} %broadcast_select_fusion.1), channel_id=1, source_target_pairs={{0,4},{1,5},{2,6},{3,7},{4,8},{5,9},{6,10},{7,11},{8,12},{9,13},{1... | collective-permute-start | bytes 294920 | tf_op jit(solution)/shard_map/ppermute | solution.py:15
  28.8 6.9 %collective-permute-start.3 = (f32[4,2,24,128]{3,2,1,0:T(8,128)S(1)}, f32[4,2,24,128]{3,2,1,0:T(8,128)S(1)}, u32[]{:S(2)}, u32[]{:S(2)}) collective-permute-start(f32[4,2,24,128]{3,2,1,0:T(8,128)S(1)} %broadcast_select_fusion.2), channel_id=1, source_target_pairs={{0,8},{1,9},{2,10},{3,11},{4,12},{5,13},{6,14},{7,15},{8,0},{9,1},... | collective-permute-start | bytes 294920 | tf_op jit(solution)/shard_map/ppermute | solution.py:15
  35.8 41.9 %collective-permute-start.4 = (f32[4,2,24,128]{3,2,1,0:T(8,128)S(1)}, f32[4,2,24,128]{3,2,1,0:T(8,128)S(1)}, u32[]{:S(2)}, u32[]{:S(2)}) collective-permute-start(f32[4,2,24,128]{3,2,1,0:T(8,128)S(1)} %broadcast_select_fusion.3), channel_id=1, source_target_pairs={{0,1},{1,2},{2,3},{3,4},{4,5},{5,6},{6,7},{7,8},{8,9},{9,10},{10,1... | collective-permute-start | bytes 294920 | tf_op jit(solution)/shard_map/ppermute | solution.py:15
  58.5 19.1 %collective-permute-start.5 = (f32[4,2,24,7]{3,2,1,0:T(8,128)S(1)}, f32[4,2,24,7]{3,2,1,0:T(8,128)S(1)}, u32[]{:S(2)}, u32[]{:S(2)}) collective-permute-start(f32[4,2,24,7]{3,2,1,0:T(8,128)S(1)} %bitcast.11), channel_id=1, source_target_pairs={{0,15},{1,0},{2,1},{3,2},{4,3},{5,4},{6,5},{7,6},{8,7},{9,8},{10,9... | collective-permute-start | bytes 16136 | tf_op jit(solution)/shard_map/ppermute | solution.py:15
  99.0 2.9 %copy-start.2 = (f32[4,2,24,128]{0,2,1,3:T(8,128)S(1)}, f32[4,2,24,128]{0,2,1,3:T(8,128)}, u32[]{:S(2)}) copy-start(f32[4,2,24,128]{0,2,1,3:T(8,128)} %get-tuple-element.13) | copy-start | bytes 294916
  103.0 5.6 %copy-start.1 = (f32[4,2,24,128]{0,2,1,3:T(8,128)S(1)}, f32[4,2,24,128]{0,2,1,3:T(8,128)}, u32[]{:S(2)}) copy-start(f32[4,2,24,128]{0,2,1,3:T(8,128)} %get-tuple-element.10) | copy-start | bytes 294916
  110.4 6.2 %copy-start = (f32[4,2,24,128]{0,2,1,3:T(8,128)S(1)}, f32[4,2,24,128]{0,2,1,3:T(8,128)}, u32[]{:S(2)}) copy-start(f32[4,2,24,128]{0,2,1,3:T(8,128)} %get-tuple-element.14) | copy-start | bytes 294916
  116.6 24.1 %copy-start.3 = (f32[2,24,128]{2,1,0:T(8,128)S(1)}, f32[2,24,128]{2,1,0:T(8,128)}, u32[]{:S(2)}) copy-start(f32[2,24,128]{2,1,0:T(8,128)} %param.13) | copy-start | bytes 73732
  119.8 6.6 %collective-permute-start.6 = (f32[4,2,3,128]{3,2,1,0:T(4,128)S(1)}, f32[4,2,3,128]{3,2,1,0:T(4,128)S(1)}, u32[]{:S(2)}, u32[]{:S(2)}) collective-permute-start(f32[4,2,3,128]{3,2,1,0:T(4,128)S(1)} %get-tuple-element.32), channel_id=1, source_target_pairs={{0,16},{16,32},{32,48},{48,64},{64,80},{80,96},{96,112},{112,128},... | collective-permute-start | bytes 36872 | tf_op jit(solution)/shard_map/ppermute | solution.py:25
  122.6 12.0 %collective-permute-start.7 = (f32[4,2,3,128]{3,2,1,0:T(4,128)S(1)}, f32[4,2,3,128]{3,2,1,0:T(4,128)S(1)}, u32[]{:S(2)}, u32[]{:S(2)}) collective-permute-start(f32[4,2,3,128]{3,2,1,0:T(4,128)S(1)} %get-tuple-element.31), channel_id=1, source_target_pairs={{16,0},{32,16},{48,32},{64,48},{80,64},{96,80},{112,96},{128,112},... | collective-permute-start | bytes 36872 | tf_op jit(solution)/shard_map/ppermute | solution.py:26
  135.5 5.3 %collective-permute-start.8 = (f32[4,2,1,128]{3,2,1,0:T(1,128)S(1)}, f32[4,2,1,128]{3,2,1,0:T(1,128)S(1)}, u32[]{:S(2)}, u32[]{:S(2)}) collective-permute-start(f32[4,2,1,128]{3,2,1,0:T(1,128)S(1)} %get-tuple-element.29), channel_id=1, source_target_pairs={{0,16},{16,32},{32,48},{48,64},{64,80},{80,96},{96,112},{112,128},... | collective-permute-start | bytes 12296 | tf_op jit(solution)/shard_map/ppermute | solution.py:25
  137.4 12.1 %collective-permute-start.9 = (f32[4,2,1,128]{3,2,1,0:T(1,128)S(1)}, f32[4,2,1,128]{3,2,1,0:T(1,128)S(1)}, u32[]{:S(2)}, u32[]{:S(2)}) collective-permute-start(f32[4,2,1,128]{3,2,1,0:T(1,128)S(1)} %get-tuple-element.30), channel_id=1, source_target_pairs={{16,0},{32,16},{48,32},{64,48},{80,64},{96,80},{112,96},{128,112},... | collective-permute-start | bytes 12296 | tf_op jit(solution)/shard_map/ppermute | solution.py:26
  149.6 7.0 %collective-permute-start.10 = (f32[4,2,26,1]{3,2,1,0:T(8,128)S(1)}, f32[4,2,26,1]{3,2,1,0:T(8,128)S(1)}, u32[]{:S(2)}, u32[]{:S(2)}) collective-permute-start(f32[4,2,26,1]{3,2,1,0:T(8,128)S(1)} %get-tuple-element.21), channel_id=1, source_target_pairs={{0,1},{1,2},{2,3},{3,4},{4,5},{5,6},{6,7},{7,8},{8,9},{9,10},{10,1... | collective-permute-start | bytes 2504 | tf_op jit(solution)/shard_map/ppermute | solution.py:25
  153.5 17.2 %collective-permute-start.11 = (f32[4,2,26,1]{3,2,1,0:T(8,128)S(1)}, f32[4,2,26,1]{3,2,1,0:T(8,128)S(1)}, u32[]{:S(2)}, u32[]{:S(2)}) collective-permute-start(f32[4,2,26,1]{3,2,1,0:T(8,128)S(1)} %get-tuple-element.22), channel_id=1, source_target_pairs={{1,0},{2,1},{3,2},{4,3},{5,4},{6,5},{7,6},{8,7},{9,8},{10,9},{11,1... | collective-permute-start | bytes 2504 | tf_op jit(solution)/shard_map/ppermute | solution.py:26
  171.0 5.3 %collective-permute-start.12 = (f32[4,2,1,128]{3,2,1,0:T(1,128)S(1)}, f32[4,2,1,128]{3,2,1,0:T(1,128)S(1)}, u32[]{:S(2)}, u32[]{:S(2)}) collective-permute-start(f32[4,2,1,128]{3,2,1,0:T(1,128)S(1)} %get-tuple-element.27), channel_id=1, source_target_pairs={{0,16},{16,32},{32,48},{48,64},{64,80},{80,96},{96,112},{112,128},... | collective-permute-start | bytes 12296 | tf_op jit(solution)/shard_map/ppermute | solution.py:25
  173.0 12.2 %collective-permute-start.13 = (f32[4,2,1,128]{3,2,1,0:T(1,128)S(1)}, f32[4,2,1,128]{3,2,1,0:T(1,128)S(1)}, u32[]{:S(2)}, u32[]{:S(2)}) collective-permute-start(f32[4,2,1,128]{3,2,1,0:T(1,128)S(1)} %get-tuple-element.28), channel_id=1, source_target_pairs={{16,0},{32,16},{48,32},{64,48},{80,64},{96,80},{112,96},{128,112},... | collective-permute-start | bytes 12296 | tf_op jit(solution)/shard_map/ppermute | solution.py:26
  185.3 7.2 %collective-permute-start.14 = (f32[4,2,26,1]{3,2,1,0:T(8,128)S(1)}, f32[4,2,26,1]{3,2,1,0:T(8,128)S(1)}, u32[]{:S(2)}, u32[]{:S(2)}) collective-permute-start(f32[4,2,26,1]{3,2,1,0:T(8,128)S(1)} %get-tuple-element.19), channel_id=1, source_target_pairs={{0,1},{1,2},{2,3},{3,4},{4,5},{5,6},{6,7},{7,8},{8,9},{9,10},{10,1... | collective-permute-start | bytes 2504 | tf_op jit(solution)/shard_map/ppermute | solution.py:25
  190.4 17.2 %collective-permute-start.15 = (f32[4,2,26,1]{3,2,1,0:T(8,128)S(1)}, f32[4,2,26,1]{3,2,1,0:T(8,128)S(1)}, u32[]{:S(2)}, u32[]{:S(2)}) collective-permute-start(f32[4,2,26,1]{3,2,1,0:T(8,128)S(1)} %get-tuple-element.20), channel_id=1, source_target_pairs={{1,0},{2,1},{3,2},{4,3},{5,4},{6,5},{7,6},{8,7},{9,8},{10,9},{11,1... | collective-permute-start | bytes 2504 | tf_op jit(solution)/shard_map/ppermute | solution.py:26
  207.9 5.3 %collective-permute-start.16 = (f32[4,2,1,128]{3,2,1,0:T(1,128)S(1)}, f32[4,2,1,128]{3,2,1,0:T(1,128)S(1)}, u32[]{:S(2)}, u32[]{:S(2)}) collective-permute-start(f32[4,2,1,128]{3,2,1,0:T(1,128)S(1)} %get-tuple-element.25), channel_id=1, source_target_pairs={{0,16},{16,32},{32,48},{48,64},{64,80},{80,96},{96,112},{112,128},... | collective-permute-start | bytes 12296 | tf_op jit(solution)/shard_map/ppermute | solution.py:25
  209.9 12.0 %collective-permute-start.17 = (f32[4,2,1,128]{3,2,1,0:T(1,128)S(1)}, f32[4,2,1,128]{3,2,1,0:T(1,128)S(1)}, u32[]{:S(2)}, u32[]{:S(2)}) collective-permute-start(f32[4,2,1,128]{3,2,1,0:T(1,128)S(1)} %get-tuple-element.26), channel_id=1, source_target_pairs={{16,0},{32,16},{48,32},{64,48},{80,64},{96,80},{112,96},{128,112},... | collective-permute-start | bytes 12296 | tf_op jit(solution)/shard_map/ppermute | solution.py:26
  221.9 5.1 %collective-permute-start.18 = (f32[4,2,26,1]{3,2,1,0:T(8,128)S(1)}, f32[4,2,26,1]{3,2,1,0:T(8,128)S(1)}, u32[]{:S(2)}, u32[]{:S(2)}) collective-permute-start(f32[4,2,26,1]{3,2,1,0:T(8,128)S(1)} %get-tuple-element.17), channel_id=1, source_target_pairs={{0,1},{1,2},{2,3},{3,4},{4,5},{5,6},{6,7},{7,8},{8,9},{9,10},{10,1... | collective-permute-start | bytes 2504 | tf_op jit(solution)/shard_map/ppermute | solution.py:25
  225.2 17.3 %collective-permute-start.19 = (f32[4,2,26,1]{3,2,1,0:T(8,128)S(1)}, f32[4,2,26,1]{3,2,1,0:T(8,128)S(1)}, u32[]{:S(2)}, u32[]{:S(2)}) collective-permute-start(f32[4,2,26,1]{3,2,1,0:T(8,128)S(1)} %get-tuple-element.18), channel_id=1, source_target_pairs={{1,0},{2,1},{3,2},{4,3},{5,4},{6,5},{7,6},{8,7},{9,8},{10,9},{11,1... | collective-permute-start | bytes 2504 | tf_op jit(solution)/shard_map/ppermute | solution.py:26
  242.8 5.3 %collective-permute-start.20 = (f32[4,2,1,128]{3,2,1,0:T(1,128)S(1)}, f32[4,2,1,128]{3,2,1,0:T(1,128)S(1)}, u32[]{:S(2)}, u32[]{:S(2)}) collective-permute-start(f32[4,2,1,128]{3,2,1,0:T(1,128)S(1)} %get-tuple-element.23), channel_id=1, source_target_pairs={{0,16},{16,32},{32,48},{48,64},{64,80},{80,96},{96,112},{112,128},... | collective-permute-start | bytes 12296 | tf_op jit(solution)/shard_map/ppermute | solution.py:25
  244.7 12.3 %collective-permute-start.21 = (f32[4,2,1,128]{3,2,1,0:T(1,128)S(1)}, f32[4,2,1,128]{3,2,1,0:T(1,128)S(1)}, u32[]{:S(2)}, u32[]{:S(2)}) collective-permute-start(f32[4,2,1,128]{3,2,1,0:T(1,128)S(1)} %get-tuple-element.24), channel_id=1, source_target_pairs={{16,0},{32,16},{48,32},{64,48},{80,64},{96,80},{112,96},{128,112},... | collective-permute-start | bytes 12296 | tf_op jit(solution)/shard_map/ppermute | solution.py:26
  257.1 4.7 %collective-permute-start.22 = (f32[4,2,26,1]{3,2,1,0:T(8,128)S(1)}, f32[4,2,26,1]{3,2,1,0:T(8,128)S(1)}, u32[]{:S(2)}, u32[]{:S(2)}) collective-permute-start(f32[4,2,26,1]{3,2,1,0:T(8,128)S(1)} %get-tuple-element.15), channel_id=1, source_target_pairs={{0,1},{1,2},{2,3},{3,4},{4,5},{5,6},{6,7},{7,8},{8,9},{9,10},{10,1... | collective-permute-start | bytes 2504 | tf_op jit(solution)/shard_map/ppermute | solution.py:25
  259.9 17.1 %collective-permute-start.23 = (f32[4,2,26,1]{3,2,1,0:T(8,128)S(1)}, f32[4,2,26,1]{3,2,1,0:T(8,128)S(1)}, u32[]{:S(2)}, u32[]{:S(2)}) collective-permute-start(f32[4,2,26,1]{3,2,1,0:T(8,128)S(1)} %get-tuple-element.16), channel_id=1, source_target_pairs={{1,0},{2,1},{3,2},{4,3},{5,4},{6,5},{7,6},{8,7},{9,8},{10,9},{11,1... | collective-permute-start | bytes 2504 | tf_op jit(solution)/shard_map/ppermute | solution.py:26
where the time goes:
time: 279 us; the launch traced here: 278 us
  waiting for transfers between devices  129 us (46%)
  starting transfers between devices  95.9 us (34%)
  local copies, waits for them, and re-layouts  41.3 us (15%)
  other arithmetic  11.1 us (4%)
    ppermute x9, waiting for transfers between devices, with_halo(): after = lax.ppermute(leading, axis, down)  103 us
    ppermute x6, starting transfers between devices, from_behind(): return lax.ppermute(value, axis, pairs)  46.2 us
    ppermute x9, starting transfers between devices, with_halo(): before = lax.ppermute(last, axis, up)  25.5 us
    ppermute x6, waiting for transfers between devices, from_behind(): return lax.ppermute(value, axis, pairs)  25.2 us
    ppermute x9, starting transfers between devices, with_halo(): after = lax.ppermute(leading, axis, down)  24.1 us
    unnamed x16, local copies, waits for them, and re-layouts  19.4 us
    slice x1, local copies, waits for them, and re-layouts, pick_cells(): part = part + weights[k] * window[..., begin:begin + width]  8.47 us
    gather x1, local copies, waits for them, and re-layouts, take_one(): return lax.dynamic_slice_in_dim(piece, begin, length, 1)  7.45 us
  transfers between devices with their start and end apart: 24, of which 16 were waited for; matrix products, arithmetic and copies ran while one was open for 2% of the time, Pallas kernels for 0%

commit v1 on v0

v1 whole, which is shorter than its diff:
```python
import jax
import jax.numpy as jnp
from jax import lax
from jax.experimental import pallas as pl
from jax.experimental.pallas import tpu as pltpu
from jax.sharding import PartitionSpec as P

SWEEPS = 4
F32 = jnp.float32
I32 = jnp.int32
SECTORS = 16
Z_PAIRS = [[4 * y + c, 4 * y + 2 + c] for y in range(4) for c in range(2)]
Y_RINGS = [[4 * y + k for y in range(4)] for k in range(4)]
CORE_SWAP = [(i, i ^ 1) for i in range(SECTORS)]


def lanes(shape):
    return lax.broadcasted_iota(I32, shape, len(shape) - 1)


def cubic_weights(frac):
    return (
        -frac * (frac - 1.0) * (frac - 2.0) / 6.0,
        (frac + 1.0) * (frac - 1.0) * (frac - 2.0) / 2.0,
        -(frac + 1.0) * frac * (frac - 2.0) / 2.0,
        (frac + 1.0) * frac * (frac - 1.0) / 6.0,
    )


def offset_weights(frac, cells, lowest, highest):
    w = cubic_weights(frac)
    result = []
    for offset in range(-1 - highest, 3 - lowest):
        total = jnp.zeros_like(frac)
        for k in range(4):
            c = k - 1 - offset
            if lowest <= c <= highest:
                total = jnp.where(cells == float(c), w[k], total)
        result.append(total)
    return result


def pack_kernel(state, zc, zf, mc, mf, cp, out):
    rows = state.shape[2]
    for f in range(4):
        for l in range(2):
            out[2 * f + l] = state[f, l]
    lane = lanes((rows, 128))
    plane = jnp.zeros((rows, 128), F32)
    for i, ref in enumerate((zc, zf, mc, mf, cp)):
        for l in range(2):
            a = 2 * i + l
            moved = pltpu.roll(ref[l].astype(F32), 8 * a + 4, 1)
            plane = jnp.where(lane // 8 == a, moved, plane)
    out[8] = plane


def zonal_kernel(g0, g1, shift, zc, zf, mc, mf, cp, zonal, coef, ea, eb):
    rows = zc.shape[1]
    me, band = lax.axis_index("lon"), lax.axis_index("lat")
    core = me & 1
    lane = lanes((rows, 128))
    left, right = (me + SECTORS - 1) & 15, (me + 1) & 15
    before = g1[left // 4, (left // 2) & 1, 8]
    behind = g1[right // 4, (right // 2) & 1, 8]

    def extended(ref, i, l):
        a = 2 * i + l
        own = pltpu.roll(ref[l].astype(F32), 4, 1)
        first = jnp.where(lane < 4, pltpu.roll(before, (128 - 8 * a) % 128, 1), own)
        second = jnp.where(lane < 4, own, pltpu.roll(behind, (128 - 8 * a) % 128, 1))
        return jnp.concatenate([first, second], axis=1)

    eye = lax.broadcasted_iota(I32, (rows, rows), 0) == lax.broadcasted_iota(I32, (rows, rows), 1)
    for l in range(2):
        line = jnp.broadcast_to(shift[l : l + 1, :].astype(F32), (rows, rows))
        moved = jnp.sum(jnp.where(eye, line, 0.0), axis=1, keepdims=True).astype(I32)
        begin = jnp.broadcast_to((-moved - 7) & 2047, (rows, 128))
        place = (begin & 127) + lane
        index, inside = place & 127, place < 128
        sector = (me + (begin >> 7)) & 15
        weights = offset_weights(extended(zf, 1, l), extended(zc, 0, l), -2, 2)
        for f in range(4):
            fl = 2 * f + l
            block = [jnp.zeros((rows, 128), F32) for _ in range(3)]
            for y in range(4):
                for z in range(2):
                    for g, ref in enumerate((g0, g1)):
                        s = 4 * y + 2 * z + (core ^ g)
                        value = ref[y, z, fl]
                        for k in range(3):
                            block[k] = jnp.where(sector == ((s - k) & 15), value, block[k])
            r = [jnp.take_along_axis(v, index, axis=1) for v in block]
            window = jnp.concatenate(
                [jnp.where(inside, r[0], r[1]), jnp.where(inside, r[1], r[2])], axis=1
            )
            total = weights[0] * window
            for d in range(1, 8):
                total = total + weights[d] * pltpu.roll(window, 256 - d, 1)
            zonal[fl] = total
    for i, ref in enumerate((mc, mf, cp)):
        for l in range(2):
            coef[2 * i + l] = extended(ref, i + 2, l)
    even = (band & 1) == 0
    for out, base in ((ea, jnp.where(even, rows - 8, 0)), (eb, jnp.where(even, 0, rows - 8))):
        take = pl.ds(pl.multiple_of(base, 8), 8)
        lane8 = lanes((8, 128))
        plane = jnp.zeros((8, 128), F32)
        for fl in range(8):
            out[fl] = zonal[fl, take, 0:128]
            plane = jnp.where(lane8 // 8 == fl, pltpu.roll(zonal[fl, take, 128:256], 8 * fl, 1), plane)
        for a in range(6):
            out[9 + a] = coef[a, take, 0:128]
            plane = jnp.where(
                lane8 // 8 == 8 + a, pltpu.roll(coef[a, take, 128:256], 64 + 8 * a, 1), plane
            )
        out[8] = plane


def sweep_kernel(zonal, coef, ga, gb, out):
    rows = zonal.shape[1]
    total = rows + 16
    band, bands = lax.axis_index("lat"), lax.axis_size("lat")
    even = (band & 1) == 0

    def pick(plane):
        above = jnp.where(even, gb[0, plane], ga[0, plane])
        below = jnp.where(even, ga[1, plane], gb[1, plane])
        return above, below

    tails = pick(8)

    def joined(first, slot, own):
        ends = [
            jnp.concatenate([v, pltpu.roll(t, (128 - 8 * slot) % 128, 1)], axis=1)
            for v, t in zip(pick(first), tails)
        ]
        return jnp.concatenate([ends[0], own, ends[1]], axis=0)

    row = lax.broadcasted_iota(I32, (total, 256), 0)
    outside = ((row < 8) & (band == 0)) | ((row >= rows + 8) & (band == bands - 1))
    for l in range(2):
        cells = joined(9 + l, 8 + l, coef[l])
        frac = joined(11 + l, 10 + l, coef[2 + l])
        weights = offset_weights(frac, cells, -1, 1)
        coupling = joined(13 + l, 12 + l, coef[4 + l])
        inverse = jnp.where(outside, 0.0, 1.0 / (1.0 + 4.0 * coupling))
        factor = coupling * inverse
        for f in range(4):
            fl = 2 * f + l
            value = jnp.where(outside, 0.0, joined(fl, fl, zonal[fl]))
            source = jnp.zeros((total, 256), F32)
            for i, offset in enumerate(range(-2, 4)):
                moved = pltpu.roll(value, (-offset) % total, 0) if offset else value
                source = source + weights[i] * moved
            phi = jnp.where(outside, 0.0, source)
            source = source * inverse
            for _ in range(SWEEPS):
                beside = pltpu.roll(phi, 1, 0) + pltpu.roll(phi, total - 1, 0)
                beside = beside + pltpu.roll(phi, 1, 1) + pltpu.roll(phi, 255, 1)
                phi = source + factor * beside
            out[f, l] = pltpu.roll(phi[8 : 8 + rows], 252, 1)[:, 0:128]


def call(kernel, shapes):
    return pl.pallas_call(
        kernel,
        out_shape=[jax.ShapeDtypeStruct(s, F32) for s in shapes],
        compiler_params=pltpu.CompilerParams(vmem_limit_bytes=48 << 20),
    )


def body(state, zonal_shift, zonal_cells, zonal_fraction, merid_cells, merid_fraction, coupling):
    rows = state.shape[2]
    bands = lax.axis_size("lat")
    coefs = (zonal_cells, zonal_fraction, merid_cells, merid_fraction, coupling)

    def pairs(first):
        return [
            [(b % bands) * SECTORS + s for b in (i, i + 1)]
            for i in range(first, first + bands, 2)
            for s in range(SECTORS)
        ]

    (packed,) = call(pack_kernel, [(9, rows, 128)])(state, *coefs)
    both = lax.all_gather(packed, "lon", axis_index_groups=Z_PAIRS)
    own = lax.all_gather(both, "lon", axis_index_groups=Y_RINGS)
    other = lax.ppermute(own, "lon", CORE_SWAP)
    zonal, coef, ea, eb = call(
        zonal_kernel, [(8, rows, 256), (6, rows, 256), (15, 8, 128), (15, 8, 128)]
    )(own, other, zonal_shift, *coefs)
    ga = lax.all_gather(ea, ("lat", "lon"), axis_index_groups=pairs(0))
    gb = lax.all_gather(eb, ("lat", "lon"), axis_index_groups=pairs(1))
    (advanced,) = call(sweep_kernel, [state.shape])(zonal, coef, ga, gb)
    return advanced


def solution(mesh):
    in_specs = (
        P(None, None, "lat", "lon"),
        P(None, "lat"),
        P(None, "lat", "lon"),
        P(None, "lat", "lon"),
        P(None, "lat", "lon"),
        P(None, "lat", "lon"),
        P(None, "lat", "lon"),
    )
    out_specs = P(None, None, "lat", "lon")
    return jax.shard_map(body, mesh=mesh, in_specs=in_specs, out_specs=out_specs, check_vma=False)
```

time: 279 us -> 70 us (0.25)
  the two profiles are of different devices: /device:TPU:505 before, /device:TPU:8 now
where the time goes in v1:
time: 70 us; the launch traced here: 69.4 us
  blocking collectives  56.3 us (80%)
  local copies, waits for them, and re-layouts  4.6 us (7%)
  Pallas kernels  3.99 us (6%)
  waiting for transfers between devices  2.39 us (3%)
  starting transfers between devices  2.04 us (3%)
    all_gather x1, blocking collectives, body(): both = lax.all_gather(packed, 'lon', axis_index_groups=Z_PAIRS)  17.8 us
    all_gather x1, blocking collectives, body(): own = lax.all_gather(both, 'lon', axis_index_groups=Y_RINGS)  14.8 us
    all_gather x1, blocking collectives, body(): gb = lax.all_gather(eb, ('lat', 'lon'), axis_index_groups=pairs(1))  13.6 us
    all_gather x1, blocking collectives, body(): ga = lax.all_gather(ea, ('lat', 'lon'), axis_index_groups=pairs(0))  10.1 us
    unnamed x24, local copies, waits for them, and re-layouts  4.6 us
    pallas_call x1, Pallas kernels, body(): advanced, = call(sweep_kernel, [state.shape])(zonal, coef, ga, gb)  2.53 us
    ppermute x1, waiting for transfers between devices, body(): other = lax.ppermute(own, 'lon', CORE_SWAP)  2.39 us
    ppermute x1, starting transfers between devices, body(): other = lax.ppermute(own, 'lon', CORE_SWAP)  2.04 us
  transfers between devices with their start and end apart: 1, of which 1 were waited for; matrix products, arithmetic and copies ran while one was open for 0% of the time, Pallas kernels for 0%

profile of v1, /device:TPU:8, one launch (start us, length us, event | category | flops | bytes accessed | tf_op | source)
XLA Modules:
  0.0 69.4 jit_solution(1389442170484226241)
XLA Ops:
  0.0 0.0 copy-start
  0.0 0.7 %copy-done = s32[2,24,128]{2,1,0:T(8,128)S(1)} copy-done((s32[2,24,128]{2,1,0:T(8,128)S(1)}, s32[2,24,128]{2,1,0:T(8,128)}, u32[]{:S(2)}) %copy-start) | copy-done | bytes 24600
  0.7 0.0 copy-start.2
  0.7 0.7 %copy-done.2 = f32[2,24,128]{2,1,0:T(8,128)S(1)} copy-done((f32[2,24,128]{2,1,0:T(8,128)S(1)}, f32[2,24,128]{2,1,0:T(8,128)}, u32[]{:S(2)}) %copy-start.2) | copy-done | bytes 24600
  1.5 0.0 copy-start.4
  1.5 0.7 %copy-done.4 = s32[2,24,128]{2,1,0:T(8,128)S(1)} copy-done((s32[2,24,128]{2,1,0:T(8,128)S(1)}, s32[2,24,128]{2,1,0:T(8,128)}, u32[]{:S(2)}) %copy-start.4) | copy-done | bytes 24600
  2.2 0.0 copy-start.6
  2.2 0.7 %copy-done.6 = f32[2,24,128]{2,1,0:T(8,128)S(1)} copy-done((f32[2,24,128]{2,1,0:T(8,128)S(1)}, f32[2,24,128]{2,1,0:T(8,128)}, u32[]{:S(2)}) %copy-start.6) | copy-done | bytes 24600
  3.0 0.0 copy-start.8
  3.0 0.7 %copy-done.8 = f32[2,24,128]{2,1,0:T(8,128)S(1)} copy-done((f32[2,24,128]{2,1,0:T(8,128)S(1)}, f32[2,24,128]{2,1,0:T(8,128)}, u32[]{:S(2)}) %copy-start.8) | copy-done | bytes 24600
  3.7 0.0 copy-start.10
  3.7 0.9 %copy-done.10 = f32[4,2,24,128]{3,2,1,0:T(8,128)S(1)} copy-done((f32[4,2,24,128]{3,2,1,0:T(8,128)S(1)}, f32[4,2,24,128]{3,2,1,0:T(8,128)}, u32[]{:S(2)}) %copy-start.10) | copy-done | bytes 98328
  4.6 0.1 shard_map.73
  4.7 17.8 %all-gather = f32[18,24,128]{2,1,0:T(8,128)S(1)} all-gather(f32[9,24,128]{2,1,0:T(8,128)S(1)} %shard_map.73), channel_id=2, replica_groups={{0,2},{1,3},{4,6},{5,7},{8,10},{9,11},{12,14},{13,15},{16,18},{17,19},{..., dimensions={0}, use_global_device_ids=true | all-gather | bytes 331776 | tf_op jit(solution)/shard_map/all_gather | solution.py:186
  22.5 0.0 copy-start.1
  22.5 0.0 copy-start.3
  22.5 0.0 copy-start.5
  22.5 0.0 copy-start.7
  22.5 0.0 copy-start.9
  22.5 14.8 %all-gather.1 = f32[8,9,24,128]{3,2,1,0:T(8,128)S(1)} all-gather(f32[2,9,24,128]{3,2,1,0:T(8,128)S(1)} %bitcast.8), channel_id=3, replica_groups={{0,4,8,12},{1,5,9,13},{2,6,10,14},{3,7,11,15},{16,20,24,28},{17,21,25,2..., dimensions={0}, use_global_device_ids=true | all-gather | bytes 1105920 | tf_op jit(solution)/shard_map/all_gather | solution.py:187
  37.3 2.0 %collective-permute-start = (f32[4,2,9,24,128]{4,3,2,1,0:T(8,128)S(1)}, f32[4,2,9,24,128]{4,3,2,1,0:T(8,128)S(1)}, u32[]{:S(2)}, u32[]{:S(2)}) collective-permute-start(f32[4,2,9,24,128]{4,3,2,1,0:T(8,128)S(1)} %bitcast.4), channel_id=1, source_target_pairs={{0,1},{1,0},{2,3},{3,2},{4,5},{5,4},{6,7},{7,6},{8,9},{9,8},{10,11... | collective-permute-start | bytes 2654216 | tf_op jit(solution)/shard_map/ppermute | solution.py:188
  39.4 2.4 %collective-permute-done.g1 = f32[4,2,9,24,128]{4,3,2,1,0:T(8,128)S(1)} collective-permute-done((f32[4,2,9,24,128]{4,3,2,1,0:T(8,128)S(1)}, f32[4,2,9,24,128]{4,3,2,1,0:T(8,128)S(1)}, u32[]{:S(2)}, u32[]{:S(2)}) %collective-permute-start) | collective-permute-done | bytes 884768 | tf_op jit(solution)/shard_map/ppermute | solution.py:188
  41.8 0.0 copy-done.1
  41.8 0.0 copy-done.3
  41.8 0.0 copy-done.5
  41.8 0.0 copy-done.7
  41.8 0.0 copy-done.9
  41.8 0.0 copy-done.11
  41.8 1.4 %shard_map.74 = (f32[8,24,256]{2,1,0:T(8,128)S(1)}, f32[6,24,256]{2,1,0:T(8,128)S(1)}, f32[15,8,128]{2,1,0:T(8,128)S(1)}, f32[15,8,128]{2,1,0:T(8,128)S(1)}) custom-call(f32[4,2,9,24,128]{4,3,2,1,0:T(8,128)S(1)} %bitcast.5, f32[4,2,9,24,128]{4,3,2,1,0:T(8,128)S(1)} %collective-permute-done.g1, s32[2,24]{1,0:T(2,128)S(1)} %copy-done.11, ...), custom_call_target="tpu_custom_call" | custom-call | tf_op jit(solution)/shard_map/pallas_call | solution.py:189
  43.2 10.1 %all-gather.2 = f32[30,8,128]{2,1,0:T(8,128)S(1)} all-gather(f32[15,8,128]{2,1,0:T(8,128)S(1)} %get-tuple-element.11), channel_id=4, replica_groups={{0,16},{1,17},{2,18},{3,19},{4,20},{5,21},{6,22},{7,23},{8,24},{9,25},{..., dimensions={0}, use_global_device_ids=true | all-gather | bytes 184320 | tf_op jit(solution)/shard_map/all_gather | solution.py:192
  53.3 13.6 %all-gather.3 = f32[30,8,128]{2,1,0:T(8,128)S(1)} all-gather(f32[15,8,128]{2,1,0:T(8,128)S(1)} %get-tuple-element.12), channel_id=5, replica_groups={{16,32},{17,33},{18,34},{19,35},{20,36},{21,37},{22,38},{23,39},{24,40}..., dimensions={0}, use_global_device_ids=true | all-gather | bytes 184320 | tf_op jit(solution)/shard_map/all_gather | solution.py:193
  66.9 2.5 %shard_map.75 = f32[4,2,24,128]{3,2,1,0:T(8,128)} custom-call(f32[8,24,256]{2,1,0:T(8,128)S(1)} %get-tuple-element.9.zonal, f32[6,24,256]{2,1,0:T(8,128)S(1)} %get-tuple-element.10.coef, f32[2,15,8,128]{3,2,1,0:T(8,128)S(1)} %bitcast.6, f32[2,15,8,128]{3,2,1,0:T(8,128)S(1)} %bitcast.7), custom_call_target="tpu_custom_call" | custom-call | tf_op jit(solution)/shard_map/pallas_call | solution.py:194
  (1 shorter events, 0.0 us)
Async XLA Ops:
  0.0 0.7 %copy-start = (s32[2,24,128]{2,1,0:T(8,128)S(1)}, s32[2,24,128]{2,1,0:T(8,128)}, u32[]{:S(2)}) copy-start(s32[2,24,128]{2,1,0:T(8,128)} %zc.3) | copy-start | bytes 73732
  0.7 0.7 %copy-start.2 = (f32[2,24,128]{2,1,0:T(8,128)S(1)}, f32[2,24,128]{2,1,0:T(8,128)}, u32[]{:S(2)}) copy-start(f32[2,24,128]{2,1,0:T(8,128)} %zf.3) | copy-start | bytes 73732
  1.5 0.7 %copy-start.4 = (s32[2,24,128]{2,1,0:T(8,128)S(1)}, s32[2,24,128]{2,1,0:T(8,128)}, u32[]{:S(2)}) copy-start(s32[2,24,128]{2,1,0:T(8,128)} %mc.3) | copy-start | bytes 73732
  2.2 0.7 %copy-start.6 = (f32[2,24,128]{2,1,0:T(8,128)S(1)}, f32[2,24,128]{2,1,0:T(8,128)}, u32[]{:S(2)}) copy-start(f32[2,24,128]{2,1,0:T(8,128)} %mf.3) | copy-start | bytes 73732
  3.0 0.7 %copy-start.8 = (f32[2,24,128]{2,1,0:T(8,128)S(1)}, f32[2,24,128]{2,1,0:T(8,128)}, u32[]{:S(2)}) copy-start(f32[2,24,128]{2,1,0:T(8,128)} %cp.3) | copy-start | bytes 73732
  3.7 0.9 %copy-start.10 = (f32[4,2,24,128]{3,2,1,0:T(8,128)S(1)}, f32[4,2,24,128]{3,2,1,0:T(8,128)}, u32[]{:S(2)}) copy-start(f32[4,2,24,128]{3,2,1,0:T(8,128)} %state.1) | copy-start | bytes 294916
  22.5 19.2 %copy-start.1 = (s32[2,24,128]{2,1,0:T(8,128)S(1)}, s32[2,24,128]{2,1,0:T(8,128)}, u32[]{:S(2)}) copy-start(s32[2,24,128]{2,1,0:T(8,128)} %zc.3) | copy-start | bytes 73732
  22.5 19.2 %copy-start.3 = (f32[2,24,128]{2,1,0:T(8,128)S(1)}, f32[2,24,128]{2,1,0:T(8,128)}, u32[]{:S(2)}) copy-start(f32[2,24,128]{2,1,0:T(8,128)} %zf.3) | copy-start | bytes 73732
  22.5 19.2 %copy-start.5 = (s32[2,24,128]{2,1,0:T(8,128)S(1)}, s32[2,24,128]{2,1,0:T(8,128)}, u32[]{:S(2)}) copy-start(s32[2,24,128]{2,1,0:T(8,128)} %mc.3) | copy-start | bytes 73732
  22.5 19.2 %copy-start.7 = (f32[2,24,128]{2,1,0:T(8,128)S(1)}, f32[2,24,128]{2,1,0:T(8,128)}, u32[]{:S(2)}) copy-start(f32[2,24,128]{2,1,0:T(8,128)} %mf.3) | copy-start | bytes 73732
  22.5 19.3 %copy-start.9 = (f32[2,24,128]{2,1,0:T(8,128)S(1)}, f32[2,24,128]{2,1,0:T(8,128)}, u32[]{:S(2)}) copy-start(f32[2,24,128]{2,1,0:T(8,128)} %cp.3) | copy-start | bytes 73732
  37.3 4.5 %copy-start.11 = (s32[2,24]{1,0:T(2,128)S(1)}, s32[2,24]{1,0:T(2,128)}, u32[]{:S(2)}) copy-start(s32[2,24]{1,0:T(2,128)} %shift.1) | copy-start | bytes 580
  37.3 4.4 %collective-permute-start = (f32[4,2,9,24,128]{4,3,2,1,0:T(8,128)S(1)}, f32[4,2,9,24,128]{4,3,2,1,0:T(8,128)S(1)}, u32[]{:S(2)}, u32[]{:S(2)}) collective-permute-start(f32[4,2,9,24,128]{4,3,2,1,0:T(8,128)S(1)} %bitcast.4), channel_id=1, source_target_pairs={{0,1},{1,0},{2,3},{3,2},{4,5},{5,4},{6,7},{7,6},{8,9},{9,8},{10,11... | collective-permute-start | bytes 2654216 | tf_op jit(solution)/shard_map/ppermute | solution.py:188

commit v2 on v1

v2 whole, which is shorter than its diff:
```python
import jax
import jax.numpy as jnp
from jax import lax
from jax.experimental import pallas as pl
from jax.experimental.pallas import tpu as pltpu
from jax.sharding import PartitionSpec as P

SWEEPS = 4
F32 = jnp.float32
I32 = jnp.int32
SECTORS = 16
RUN = 8
Z_PAIRS = [[4 * y + c, 4 * y + 2 + c] for y in range(4) for c in range(2)]
Y_RINGS = [[4 * y + k for y in range(4)] for k in range(4)]
CORES = [[2 * i, 2 * i + 1] for i in range(SECTORS // 2)]


def iota(shape, dim):
    return lax.broadcasted_iota(I32, shape, dim)


def cubic_weights(frac):
    return (
        -frac * (frac - 1.0) * (frac - 2.0) / 6.0,
        (frac + 1.0) * (frac - 1.0) * (frac - 2.0) / 2.0,
        -(frac + 1.0) * frac * (frac - 2.0) / 2.0,
        (frac + 1.0) * frac * (frac - 1.0) / 6.0,
    )


def offset_weights(frac, cells, lowest, highest):
    w = cubic_weights(frac)
    result = []
    for offset in range(-1 - highest, 3 - lowest):
        total = jnp.zeros_like(frac)
        for k in range(4):
            c = k - 1 - offset
            if lowest <= c <= highest:
                total = jnp.where(cells == float(c), w[k], total)
        result.append(total)
    return result


def pack_rows(first, second, top):
    a = jnp.where(top, first, pltpu.roll(first, 4, 0))
    b = jnp.where(top, pltpu.roll(second, 4, 0), second)
    return jnp.where(iota((8, 128), 0) < 4, a, b)


def unpack_rows(packed):
    low = iota((8, 128), 0) < 4
    turned = pltpu.roll(packed, 4, 0)
    return jnp.where(low, packed, turned), jnp.where(low, turned, packed)


def place():
    me, band = lax.axis_index("lon"), lax.axis_index("lat")
    return me, band, (band & (RUN - 1)) == 0, (band & (RUN - 1)) == RUN - 1


def pack_kernel(*refs):
    sources, out, held, sems = refs[:6], refs[6], refs[7:13], refs[13]
    copies = [pltpu.make_async_copy(s, h, sems.at[i]) for i, (s, h) in enumerate(zip(sources, held))]
    for copy in copies:
        copy.start()
    for copy in copies:
        copy.wait()
    state, coefs = held[0], held[1:]
    rows = state.shape[2]
    for f in range(4):
        for l in range(2):
            at = (2 * f + l) * rows
            out[at : at + rows] = state[f, l]
    group = iota((rows, 128), 1) // 8
    plane = jnp.zeros((rows, 128), F32)
    for i, ref in enumerate(coefs):
        for l in range(2):
            a = 2 * i + l
            plane = jnp.where(group == a, pltpu.roll(ref[l].astype(F32), 8 * a + 4, 1), plane)
    out[8 * rows : 9 * rows] = plane
    _, _, opens, _ = place()

    def edge(ref, l):
        return jnp.where(opens, ref[l, 0:8], ref[l, rows - 8 : rows]).astype(F32)

    at = 9 * rows
    for ref in coefs[:2]:
        for l in range(2):
            out[at : at + 8] = edge(ref, l)
            at += 8
    for ref in coefs[2:]:
        out[at : at + 8] = pack_rows(edge(ref, 0), edge(ref, 1), opens)
        at += 8


def window_kernel(circle, shift, keep, send):
    rows = circle.shape[3]
    all_rows = rows + 8
    me, _, opens, _ = place()
    core = me & 1
    lane = iota((all_rows, 128), 1)
    flip = jnp.where(iota((all_rows, 128), 0) < rows, 0, 2)
    eye = iota((rows, rows), 0) == iota((rows, rows), 1)
    base = pl.multiple_of(jnp.where(opens, 0, rows - 8), 8)

    def block_of(y, z, plane):
        return jnp.concatenate([circle[y, z, plane], circle[y, z, plane, pl.ds(base, 8)]], axis=0)

    outs = (keep, send)
    slot = lane // 16
    tails = [jnp.zeros((all_rows, 128), F32) for _ in outs]
    for l in range(2):
        line = jnp.broadcast_to(shift[l : l + 1, :].astype(F32), (rows, rows))
        moved = jnp.sum(jnp.where(eye, line, 0.0), axis=1, keepdims=True).astype(I32)
        begin = jnp.broadcast_to((-moved - 7) & 2047, (rows, 128))
        begin = jnp.concatenate(
            [begin, jnp.where(opens, begin[0:8], begin[rows - 8 : rows])], axis=0
        )
        spot = (begin & 127) + lane
        index, inside = spot & 127, spot < 128
        hops = begin >> 7
        sectors = [((me ^ t ^ flip) + hops) & 15 for t in range(2)]
        for f in range(4):
            fl = 2 * f + l
            block = [[jnp.zeros((all_rows, 128), F32) for _ in range(3)] for _ in range(2)]
            for y in range(4):
                for z in range(2):
                    s = 4 * y + 2 * z + core
                    value = block_of(y, z, fl)
                    for t in range(2):
                        for k in range(3):
                            hit = sectors[t] == ((s - k) & 15)
                            block[t][k] = jnp.where(hit, value, block[t][k])
            for t, out in enumerate(outs):
                r = [jnp.take_along_axis(v, index, axis=1) for v in block[t]]
                out[fl] = jnp.where(inside, r[0], r[1])
                tail = pltpu.roll(jnp.where(inside, r[1], r[2]), 16 * fl, 1)
                tails[t] = jnp.where(slot == fl, tail, tails[t])
    for t, out in enumerate(outs):
        out[8] = tails[t]
    sides = []
    for step in (-1, 1):
        near = (((me ^ 1) + step) & 15) // 2
        far = (((me ^ 3) + step) & 15) // 2
        sides.append(
            jnp.concatenate(
                [circle[near // 2, near & 1, 8], circle[far // 2, far & 1, 8, pl.ds(base, 8)]],
                axis=0,
            )
        )
    send[9] = jnp.where((lane & 7) < 4, sides[0], sides[1])


def zonal_kernel(keep, swapped, around, zc, zf, mc, mf, cp, zonal, coef, ea, eb, edge_zonal, edge_coef):
    rows = zc.shape[1]
    all_rows = rows + 8
    me, band, opens, closes = place()
    mate = 1 - (me & 1)
    across = 1 - ((me >> 1) & 1)
    lane = iota((all_rows, 128), 1)
    beside = swapped[mate, 9]

    def extended(ref, extra, i, l):
        a = 2 * i + l
        own = jnp.concatenate([ref[l].astype(F32), extra], axis=0)
        own = pltpu.roll(own, 4, 1)
        side = pltpu.roll(beside, (128 - 8 * a) % 128, 1) if a else beside
        return jnp.concatenate(
            [jnp.where(lane < 4, side, own), jnp.where(lane < 4, own, side)], axis=1
        )

    def extra(n):
        at = 9 * rows + 8 * n
        return around[across, at : at + 8]

    for l in range(2):
        weights = offset_weights(
            extended(zf, extra(2 + l), 1, l), extended(zc, extra(l), 0, l), -2, 2
        )
        tails = keep[8] + swapped[mate, 8]
        for f in range(4):
            fl = 2 * f + l
            tail = pltpu.roll(tails, 128 - 16 * fl, 1) if fl else tails
            window = jnp.concatenate([keep[fl] + swapped[mate, fl], tail], axis=1)
            total = weights[0] * window
            for d in range(1, 8):
                total = total + weights[d] * pltpu.roll(window, 256 - d, 1)
            zonal[fl] = total[:rows]
            edge_zonal[fl] = total[rows:]
    for i, ref in enumerate((mc, mf, cp)):
        extras = unpack_rows(extra(4 + i))
        for l in range(2):
            wide = extended(ref, extras[l], i + 2, l)
            coef[2 * i + l] = wide[:rows]
            edge_coef[2 * i + l] = wide[rows:]

    even = (band & 1) == 0
    group = iota((8, 128), 1) // 8
    for out, top in ((ea, jnp.logical_not(even)), (eb, even)):
        take = pl.ds(pl.multiple_of(jnp.where(top, 0, rows - 8), 8), 8)
        at_end = opens | closes if out is eb else None

        def tile(ref, edge_ref, n):
            v = ref[n, take]
            return v if at_end is None else jnp.where(at_end, edge_ref[n], v)

        plane = jnp.zeros((8, 128), F32)
        for fl in range(8):
            v = tile(zonal, edge_zonal, fl)
            out[fl] = v[:, 0:128]
            tail = pltpu.roll(v[:, 128:256], 8 * fl, 1) if fl else v[:, 128:256]
            plane = jnp.where(group == fl, tail, plane)
        for i in range(3):
            pair = [tile(coef, edge_coef, 2 * i + l) for l in range(2)]
            out[9 + i] = pack_rows(pair[0][:, 0:128], pair[1][:, 0:128], top)
            for l in range(2):
                a = 8 + 2 * i + l
                plane = jnp.where(group == a, pltpu.roll(pair[l][:, 128:256], 8 * a, 1), plane)
        out[8] = plane


def sweep_kernel(zonal, coef, ga, gb, out):
    rows = zonal.shape[1]
    total = rows + 16
    band, bands = lax.axis_index("lat"), lax.axis_size("lat")
    even = (band & 1) == 0

    def pick(plane):
        above = jnp.where(even, gb[0, plane], ga[0, plane])
        below = jnp.where(even, ga[1, plane], gb[1, plane])
        return above, below

    tails = pick(8)

    def joined(firsts, slot, own):
        ends = [
            jnp.concatenate([v, pltpu.roll(t, 128 - 8 * slot, 1) if slot else t], axis=1)
            for v, t in zip(firsts, tails)
        ]
        return jnp.concatenate([ends[0], own, ends[1]], axis=0)

    row = iota((total, 256), 0)
    outside = ((row < 8) & (band == 0)) | ((row >= rows + 8) & (band == bands - 1))
    packs = [[unpack_rows(v) for v in pick(9 + i)] for i in range(3)]
    for l in range(2):
        cells, frac, coupling = [
            joined([v[l] for v in packs[i]], 8 + 2 * i + l, coef[2 * i + l]) for i in range(3)
        ]
        weights = offset_weights(frac, cells, -1, 1)
        inverse = jnp.where(outside, 0.0, 1.0 / (1.0 + 4.0 * coupling))
        factor = coupling * inverse
        for f in range(4):
            fl = 2 * f + l
            value = jnp.where(outside, 0.0, joined(pick(fl), fl, zonal[fl]))
            source = jnp.zeros((total, 256), F32)
            for i, offset in enumerate(range(-2, 4)):
                moved = pltpu.roll(value, (-offset) % total, 0) if offset else value
                source = source + weights[i] * moved
            phi = jnp.where(outside, 0.0, source)
            source = source * inverse
            for _ in range(SWEEPS):
                beside = pltpu.roll(phi, 1, 0) + pltpu.roll(phi, total - 1, 0)
                beside = beside + pltpu.roll(phi, 1, 1) + pltpu.roll(phi, 255, 1)
                phi = source + factor * beside
            out[f, l] = pltpu.roll(phi[8 : 8 + rows], 252, 1)[:, 0:128]


def call(kernel, shapes, scratch=(), in_specs=None):
    more = {} if in_specs is None else {"in_specs": in_specs}
    return pl.pallas_call(
        kernel,
        out_shape=[jax.ShapeDtypeStruct(s, F32) for s in shapes],
        scratch_shapes=list(scratch),
        compiler_params=pltpu.CompilerParams(vmem_limit_bytes=32 << 20),
        **more,
    )


def body(state, zonal_shift, zonal_cells, zonal_fraction, merid_cells, merid_fraction, coupling):
    rows = state.shape[2]
    bands = lax.axis_size("lat")
    coefs = (zonal_cells, zonal_fraction, merid_cells, merid_fraction, coupling)

    def pairs(first):
        return [
            [i * SECTORS + s, (i + 1) % bands * SECTORS + (s ^ 2 if i % RUN == RUN - 1 else s)]
            for i in range(first, first + bands, 2)
            for s in range(SECTORS)
        ]

    (packed,) = call(
        pack_kernel,
        [(9 * rows + 56, 128)],
        [pltpu.VMEM(v.shape, v.dtype) for v in (state, *coefs)] + [pltpu.SemaphoreType.DMA((6,))],
        [pl.BlockSpec(memory_space=pltpu.HBM)] * 6,
    )(state, *coefs)
    around = lax.all_gather(packed, "lon", axis_index_groups=Z_PAIRS)
    circle = lax.all_gather(around[:, : 9 * rows], "lon", axis_index_groups=Y_RINGS)
    keep, send = call(window_kernel, [(9, rows + 8, 128), (10, rows + 8, 128)])(
        circle.reshape(4, 2, 9, rows, 128), zonal_shift
    )
    swapped = lax.all_gather(send, "lon", axis_index_groups=CORES)
    zonal, coef, ea, eb = call(
        zonal_kernel,
        [(8, rows, 256), (6, rows, 256), (12, 8, 128), (12, 8, 128)],
        [pltpu.VMEM((8, 8, 256), F32), pltpu.VMEM((6, 8, 256), F32)],
    )(keep, swapped, around, *coefs)
    ga = lax.all_gather(ea, ("lat", "lon"), axis_index_groups=pairs(0))
    gb = lax.all_gather(eb, ("lat", "lon"), axis_index_groups=pairs(1))
    (advanced,) = call(sweep_kernel, [state.shape])(zonal, coef, ga, gb)
    return advanced


def solution(mesh):
    in_specs = (
        P(None, None, "lat", "lon"),
        P(None, "lat"),
        P(None, "lat", "lon"),
        P(None, "lat", "lon"),
        P(None, "lat", "lon"),
        P(None, "lat", "lon"),
        P(None, "lat", "lon"),
    )
    out_specs = P(None, None, "lat", "lon")
    return jax.shard_map(body, mesh=mesh, in_specs=in_specs, out_specs=out_specs, check_vma=False)
```

time: 70 us -> 70.2 us (level)
  blocking collectives: 56.3 us -> 58.8 us
  waiting for transfers between devices: 2.39 us -> 0 us
  starting transfers between devices: 2.04 us -> 0 us
  Pallas kernels: 3.99 us -> 5.44 us
    all_gather x2 -> x3, blocking collectives: 32.6 us -> 35.3 us  [the longest x1 18.4 us: body(): around = lax.all_gather(packed, 'lon', axis_index_groups=Z_PAIRS)]
    all_gather x1, blocking collectives: 13.6 us -> 11 us  [body(): gb = lax.all_gather(eb, ('lat', 'lon'), axis_index_groups=pairs(1))]
    ppermute x1 -> x0, waiting for transfers between devices: 2.39 us -> none  [body(): other = lax.ppermute(own, 'lon', CORE_SWAP)]
    all_gather x1, blocking collectives: 10.1 us -> 12.5 us  [body(): ga = lax.all_gather(ea, ('lat', 'lon'), axis_index_groups=pairs(0))]
    ppermute x1 -> x0, starting transfers between devices: 2.04 us -> none  [body(): other = lax.ppermute(own, 'lon', CORE_SWAP)]
    pallas_call x2 -> x3, Pallas kernels: 1.46 us -> 2.91 us  [the longest x1 1.29 us: body(): call(window_kernel, [(9, rows + 8, 128), (10, rows + 8, 128)])]
  transfers between devices with their start and end apart: 1 -> 0, of which waited for: 1 -> 0; matrix products, arithmetic and copies ran while one was open for 0% -> 0% of each run, Pallas kernels for 0% -> 0%
where the time goes in v2:
time: 70.2 us; the launch traced here: 69.6 us
  blocking collectives  58.8 us (84%)
  Pallas kernels  5.44 us (8%)
  local copies, waits for them, and re-layouts  5.3 us (8%)
    all_gather x1, blocking collectives, body(): around = lax.all_gather(packed, 'lon', axis_index_groups=Z_PAIRS)  18.4 us
    all_gather x1, blocking collectives, body(): lax.all_gather(around[:, :9 * rows], 'lon', axis_index_groups=Y_RINGS)  14.6 us
    all_gather x1, blocking collectives, body(): ga = lax.all_gather(ea, ('lat', 'lon'), axis_index_groups=pairs(0))  12.5 us
    all_gather x1, blocking collectives, body(): gb = lax.all_gather(eb, ('lat', 'lon'), axis_index_groups=pairs(1))  11 us
    unnamed x24, local copies, waits for them, and re-layouts  5.29 us
    pallas_call x1, Pallas kernels, body(): advanced, = call(sweep_kernel, [state.shape])(zonal, coef, ga, gb)  2.54 us
    all_gather x1, blocking collectives, body(): swapped = lax.all_gather(send, 'lon', axis_index_groups=CORES)  2.17 us

profile of v2, /device:TPU:8, one launch (start us, length us, event | category | flops | bytes accessed | tf_op | source)
XLA Modules:
  0.0 69.6 jit_solution(18399730931931171016)
XLA Ops:
  0.0 0.0 copy-start
  0.0 0.7 %copy-done = s32[2,24,128]{2,1,0:T(8,128)S(1)} copy-done((s32[2,24,128]{2,1,0:T(8,128)S(1)}, s32[2,24,128]{2,1,0:T(8,128)}, u32[]{:S(2)}) %copy-start) | copy-done | bytes 24600
  0.7 0.0 copy-start.2
  0.7 0.7 %copy-done.2 = f32[2,24,128]{2,1,0:T(8,128)S(1)} copy-done((f32[2,24,128]{2,1,0:T(8,128)S(1)}, f32[2,24,128]{2,1,0:T(8,128)}, u32[]{:S(2)}) %copy-start.2) | copy-done | bytes 24600
  1.5 0.0 copy-start.4
  1.5 0.7 %copy-done.4 = s32[2,24,128]{2,1,0:T(8,128)S(1)} copy-done((s32[2,24,128]{2,1,0:T(8,128)S(1)}, s32[2,24,128]{2,1,0:T(8,128)}, u32[]{:S(2)}) %copy-start.4) | copy-done | bytes 24600
  2.2 0.0 copy-start.6
  2.2 0.7 %copy-done.6 = f32[2,24,128]{2,1,0:T(8,128)S(1)} copy-done((f32[2,24,128]{2,1,0:T(8,128)S(1)}, f32[2,24,128]{2,1,0:T(8,128)}, u32[]{:S(2)}) %copy-start.6) | copy-done | bytes 24600
  3.0 0.0 copy-start.8
  3.0 0.7 %copy-done.8 = f32[2,24,128]{2,1,0:T(8,128)S(1)} copy-done((f32[2,24,128]{2,1,0:T(8,128)S(1)}, f32[2,24,128]{2,1,0:T(8,128)}, u32[]{:S(2)}) %copy-start.8) | copy-done | bytes 24600
  3.7 0.0 copy-start.10
  3.7 0.9 %copy-done.10 = f32[4,2,24,128]{3,2,1,0:T(8,128)S(1)} copy-done((f32[4,2,24,128]{3,2,1,0:T(8,128)S(1)}, f32[4,2,24,128]{3,2,1,0:T(8,128)}, u32[]{:S(2)}) %copy-start.10) | copy-done | bytes 98328
  4.6 0.4 shard_map.73
  5.0 18.4 %all-gather = f32[544,128]{1,0:T(8,128)S(1)} all-gather(f32[272,128]{1,0:T(8,128)S(1)} %shard_map.73), channel_id=2, replica_groups={{0,2},{1,3},{4,6},{5,7},{8,10},{9,11},{12,14},{13,15},{16,18},{17,19},{..., dimensions={0}, use_global_device_ids=true | all-gather | bytes 417792 | tf_op jit(solution)/shard_map/all_gather | solution.py:297
  23.5 14.6 %all-gather.1 = f32[8,216,128]{2,1,0:T(8,128)S(1)} all-gather(f32[2,216,128]{2,1,0:T(8,128)S(1)} %slice.4), channel_id=3, replica_groups={{0,4,8,12},{1,5,9,13},{2,6,10,14},{3,7,11,15},{16,20,24,28},{17,21,25,2..., dimensions={0}, use_global_device_ids=true | all-gather | bytes 1105920 | tf_op jit(solution)/shard_map/all_gather | solution.py:298
  38.1 0.7 copy-done.11
  38.8 1.3 %shard_map.74 = (f32[9,32,128]{2,1,0:T(8,128)S(1)}, f32[10,32,128]{2,1,0:T(8,128)S(1)}) custom-call(f32[4,2,9,24,128]{4,3,2,1,0:T(8,128)S(1)} %bitcast.5, s32[2,24]{1,0:T(2,128)S(1)} %copy-done.11), custom_call_target="tpu_custom_call" | custom-call | tf_op jit(solution)/shard_map/pallas_call | solution.py:299
  40.1 0.0 copy-start.1
  40.1 0.0 copy-start.3
  40.1 0.0 copy-start.5
  40.1 0.0 copy-start.7
  40.1 0.0 copy-start.9
  40.1 2.2 %all-gather.2 = f32[20,32,128]{2,1,0:T(8,128)S(1)} all-gather(f32[10,32,128]{2,1,0:T(8,128)S(1)} %get-tuple-element.12), channel_id=4, replica_groups={{0,1},{2,3},{4,5},{6,7},{8,9},{10,11},{12,13},{14,15},{16,17},{18,19},{..., dimensions={0}, use_global_device_ids=true | all-gather | bytes 491520 | tf_op jit(solution)/shard_map/all_gather | solution.py:302
  42.3 0.0 copy-done.1
  42.3 0.0 copy-done.3
  42.3 0.0 copy-done.5
  42.3 0.0 copy-done.7
  42.3 0.0 copy-done.9
  42.3 1.2 %shard_map.75 = (f32[8,24,256]{2,1,0:T(8,128)S(1)}, f32[6,24,256]{2,1,0:T(8,128)S(1)}, f32[12,8,128]{2,1,0:T(8,128)S(1)}, f32[12,8,128]{2,1,0:T(8,128)S(1)}) custom-call(f32[9,32,128]{2,1,0:T(8,128)S(1)} %get-tuple-element.11.keep, f32[2,10,32,128]{3,2,1,0:T(8,128)S(1)} %bitcast.8, f32[2,272,128]{2,1,0:T(8,128)S(1)} %bitcast.7, s32[2,24,128]{2,1,0:T(8,128)S(1)} %copy-done.1, ...), custom_call_target="tpu_custom_call" | custom-call | tf_op jit(solution)/shard_map/pallas_call | solution.py:303
  43.6 12.5 %all-gather.3 = f32[24,8,128]{2,1,0:T(8,128)S(1)} all-gather(f32[12,8,128]{2,1,0:T(8,128)S(1)} %get-tuple-element.15), channel_id=5, replica_groups={{0,16},{1,17},{2,18},{3,19},{4,20},{5,21},{6,22},{7,23},{8,24},{9,25},{..., dimensions={0}, use_global_device_ids=true | all-gather | bytes 147456 | tf_op jit(solution)/shard_map/all_gather | solution.py:308
  56.1 11.0 %all-gather.4 = f32[24,8,128]{2,1,0:T(8,128)S(1)} all-gather(f32[12,8,128]{2,1,0:T(8,128)S(1)} %get-tuple-element.16), channel_id=6, replica_groups={{16,32},{17,33},{18,34},{19,35},{20,36},{21,37},{22,38},{23,39},{24,40}..., dimensions={0}, use_global_device_ids=true | all-gather | bytes 147456 | tf_op jit(solution)/shard_map/all_gather | solution.py:309
  67.1 2.5 %shard_map.76 = f32[4,2,24,128]{3,2,1,0:T(8,128)} custom-call(f32[8,24,256]{2,1,0:T(8,128)S(1)} %get-tuple-element.13.zonal, f32[6,24,256]{2,1,0:T(8,128)S(1)} %get-tuple-element.14.coef, f32[2,12,8,128]{3,2,1,0:T(8,128)S(1)} %bitcast.9, f32[2,12,8,128]{3,2,1,0:T(8,128)S(1)} %bitcast.10), custom_call_target="tpu_custom_call" | custom-call | tf_op jit(solution)/shard_map/pallas_call | solution.py:310
  (2 shorter events, 0.0 us)
Async XLA Ops:
  0.0 0.7 %copy-start = (s32[2,24,128]{2,1,0:T(8,128)S(1)}, s32[2,24,128]{2,1,0:T(8,128)}, u32[]{:S(2)}) copy-start(s32[2,24,128]{2,1,0:T(8,128)} %zc.1) | copy-start | bytes 73732
  0.7 0.7 %copy-start.2 = (f32[2,24,128]{2,1,0:T(8,128)S(1)}, f32[2,24,128]{2,1,0:T(8,128)}, u32[]{:S(2)}) copy-start(f32[2,24,128]{2,1,0:T(8,128)} %zf.1) | copy-start | bytes 73732
  1.5 0.7 %copy-start.4 = (s32[2,24,128]{2,1,0:T(8,128)S(1)}, s32[2,24,128]{2,1,0:T(8,128)}, u32[]{:S(2)}) copy-start(s32[2,24,128]{2,1,0:T(8,128)} %mc.1) | copy-start | bytes 73732
  2.2 0.7 %copy-start.6 = (f32[2,24,128]{2,1,0:T(8,128)S(1)}, f32[2,24,128]{2,1,0:T(8,128)}, u32[]{:S(2)}) copy-start(f32[2,24,128]{2,1,0:T(8,128)} %mf.1) | copy-start | bytes 73732
  3.0 0.7 %copy-start.8 = (f32[2,24,128]{2,1,0:T(8,128)S(1)}, f32[2,24,128]{2,1,0:T(8,128)}, u32[]{:S(2)}) copy-start(f32[2,24,128]{2,1,0:T(8,128)} %cp.1) | copy-start | bytes 73732
  3.7 0.9 %copy-start.10 = (f32[4,2,24,128]{3,2,1,0:T(8,128)S(1)}, f32[4,2,24,128]{3,2,1,0:T(8,128)}, u32[]{:S(2)}) copy-start(f32[4,2,24,128]{3,2,1,0:T(8,128)} %refs_0_.1) | copy-start | bytes 294916
  38.1 0.7 copy-start.11
  40.1 2.2 %copy-start.1 = (s32[2,24,128]{2,1,0:T(8,128)S(1)}, s32[2,24,128]{2,1,0:T(8,128)}, u32[]{:S(2)}) copy-start(s32[2,24,128]{2,1,0:T(8,128)} %zc.1) | copy-start | bytes 73732
  40.1 2.2 %copy-start.3 = (f32[2,24,128]{2,1,0:T(8,128)S(1)}, f32[2,24,128]{2,1,0:T(8,128)}, u32[]{:S(2)}) copy-start(f32[2,24,128]{2,1,0:T(8,128)} %zf.1) | copy-start | bytes 73732
  40.1 2.2 %copy-start.5 = (s32[2,24,128]{2,1,0:T(8,128)S(1)}, s32[2,24,128]{2,1,0:T(8,128)}, u32[]{:S(2)}) copy-start(s32[2,24,128]{2,1,0:T(8,128)} %mc.1) | copy-start | bytes 73732
  40.1 2.2 %copy-start.7 = (f32[2,24,128]{2,1,0:T(8,128)S(1)}, f32[2,24,128]{2,1,0:T(8,128)}, u32[]{:S(2)}) copy-start(f32[2,24,128]{2,1,0:T(8,128)} %mf.1) | copy-start | bytes 73732
  40.1 2.2 %copy-start.9 = (f32[2,24,128]{2,1,0:T(8,128)S(1)}, f32[2,24,128]{2,1,0:T(8,128)}, u32[]{:S(2)}) copy-start(f32[2,24,128]{2,1,0:T(8,128)} %cp.1) | copy-start | bytes 73732

commit v3 on v2

v3 whole, which is shorter than its diff:
```python
import jax
import jax.numpy as jnp
from jax import lax
from jax.experimental import pallas as pl
from jax.experimental.pallas import tpu as pltpu
from jax.sharding import PartitionSpec as P

SWEEPS = 4
F32 = jnp.float32
I32 = jnp.int32
SECTORS = 16
Z_PAIRS = [[4 * y + c, 4 * y + 2 + c] for y in range(4) for c in range(2)]
Y_RINGS = [[4 * y + k for y in range(4)] for k in range(4)]
CORES = [[2 * i, 2 * i + 1] for i in range(SECTORS // 2)]


def iota(shape, dim):
    return lax.broadcasted_iota(I32, shape, dim)


def cubic_weights(frac):
    return (
        -frac * (frac - 1.0) * (frac - 2.0) / 6.0,
        (frac + 1.0) * (frac - 1.0) * (frac - 2.0) / 2.0,
        -(frac + 1.0) * frac * (frac - 2.0) / 2.0,
        (frac + 1.0) * frac * (frac - 1.0) / 6.0,
    )


def offset_weights(frac, cells, lowest, highest):
    w = cubic_weights(frac)
    result = []
    for offset in range(-1 - highest, 3 - lowest):
        total = jnp.zeros_like(frac)
        for k in range(4):
            c = k - 1 - offset
            if lowest <= c <= highest:
                total = jnp.where(cells == float(c), w[k], total)
        result.append(total)
    return result


def pack_rows(first, second, top):
    a = jnp.where(top, first, pltpu.roll(first, 4, 0))
    b = jnp.where(top, pltpu.roll(second, 4, 0), second)
    return jnp.where(iota((8, 128), 0) < 4, a, b)


def unpack_rows(packed):
    low = iota((8, 128), 0) < 4
    turned = pltpu.roll(packed, 4, 0)
    return jnp.where(low, packed, turned), jnp.where(low, turned, packed)


def pack_kernel(*refs):
    sources, out, begin, held, sems = refs[:7], refs[7], refs[8], refs[9:16], refs[16]
    copies = [pltpu.make_async_copy(s, h, sems.at[i]) for i, (s, h) in enumerate(zip(sources, held))]
    for copy in copies:
        copy.start()
    for copy in copies:
        copy.wait()
    state, shift, coefs = held[0], held[1], held[2:]
    rows = state.shape[2]
    group = iota((rows, 128), 1) // 8
    plane = jnp.zeros((rows, 128), F32)
    for i, ref in enumerate(coefs):
        for l in range(2):
            a = 2 * i + l
            plane = jnp.where(group == a, pltpu.roll(ref[l].astype(F32), 8 * a + 4, 1), plane)
    for peer in range(4):
        for f in range(4):
            for l in range(2):
                out[peer, 2 * f + l] = state[f, l]
        out[peer, 8] = plane
    eye = iota((rows, rows), 0) == iota((rows, rows), 1)
    for l in range(2):
        line = jnp.broadcast_to(shift[l : l + 1, :].astype(F32), (rows, rows))
        moved = jnp.sum(jnp.where(eye, line, 0.0), axis=1, keepdims=True).astype(I32)
        begin[l] = jnp.broadcast_to((-moved - 7) & 2047, (rows, 128))


def window_kernel(circle, begin, keep, send):
    rows = circle.shape[3]
    me = lax.axis_index("lon")
    core, side = me & 1, me & 2
    lane = iota((rows, 128), 1)
    outs = (keep, send)
    slot = lane // 16
    tails = [jnp.zeros((rows, 128), F32) for _ in outs]
    for l in range(2):
        spot = (begin[l] & 127) + lane
        index, inside = spot & 127, spot < 128
        hops = begin[l] >> 7
        sectors = [((me ^ (2 * t)) + hops) & 15 for t in range(2)]
        for f in range(4):
            fl = 2 * f + l
            block = [[jnp.zeros((rows, 128), F32) for _ in range(3)] for _ in range(2)]
            for y in range(4):
                for c in range(2):
                    s = 4 * y + side + c
                    value = circle[c, y, fl]
                    for t in range(2):
                        for k in range(3):
                            hit = sectors[t] == ((s - k) & 15)
                            block[t][k] = jnp.where(hit, value, block[t][k])
            for t, out in enumerate(outs):
                r = [jnp.take_along_axis(v, index, axis=1) for v in block[t]]
                out[fl] = jnp.where(inside, r[0], r[1])
                tail = jnp.where(inside, r[1], r[2])
                tail = pltpu.roll(tail, 16 * fl, 1) if fl else tail
                tails[t] = jnp.where(slot == fl, tail, tails[t])
    early = (lane & 7) < 4
    inner = circle[1 - core, (me // 4), 8]
    outer = ((me ^ 2) + jnp.where(core == 0, 15, 1)) & 15
    outer = circle[1 - core, outer // 4, 8]
    first = core == 0
    keep[9] = jnp.where(early != first, inner, 0.0)
    send[9] = jnp.where(early == first, outer, 0.0)
    for t, out in enumerate(outs):
        out[8] = tails[t]


def zonal_kernel(keep, swapped, zc, zf, mc, mf, cp, zonal, coef, ea, eb):
    rows = zc.shape[1]
    me, band = lax.axis_index("lon"), lax.axis_index("lat")
    across = 1 - ((me >> 1) & 1)
    lane = iota((rows, 128), 1)
    beside = keep[9] + swapped[across, 9]

    def extended(ref, i, l):
        a = 2 * i + l
        own = pltpu.roll(ref[l].astype(F32), 4, 1)
        side = pltpu.roll(beside, 128 - 8 * a, 1) if a else beside
        return jnp.concatenate(
            [jnp.where(lane < 4, side, own), jnp.where(lane < 4, own, side)], axis=1
        )

    tails = keep[8] + swapped[across, 8]
    for l in range(2):
        weights = offset_weights(extended(zf, 1, l), extended(zc, 0, l), -2, 2)
        for f in range(4):
            fl = 2 * f + l
            tail = pltpu.roll(tails, 128 - 16 * fl, 1) if fl else tails
            window = jnp.concatenate([keep[fl] + swapped[across, fl], tail], axis=1)
            total = weights[0] * window
            for d in range(1, 8):
                total = total + weights[d] * pltpu.roll(window, 256 - d, 1)
            zonal[fl] = total
    for i, ref in enumerate((mc, mf, cp)):
        for l in range(2):
            coef[2 * i + l] = extended(ref, i + 2, l)

    even = (band & 1) == 0
    group = iota((8, 128), 1) // 8
    for out, top in ((ea, jnp.logical_not(even)), (eb, even)):
        take = pl.ds(pl.multiple_of(jnp.where(top, 0, rows - 8), 8), 8)
        plane = jnp.zeros((8, 128), F32)
        for fl in range(8):
            v = zonal[fl, take]
            out[fl] = v[:, 0:128]
            tail = pltpu.roll(v[:, 128:256], 8 * fl, 1) if fl else v[:, 128:256]
            plane = jnp.where(group == fl, tail, plane)
        for i in range(3):
            pair = [coef[2 * i + l, take] for l in range(2)]
            out[9 + i] = pack_rows(pair[0][:, 0:128], pair[1][:, 0:128], top)
            for l in range(2):
                a = 8 + 2 * i + l
                plane = jnp.where(group == a, pltpu.roll(pair[l][:, 128:256], 8 * a, 1), plane)
        out[8] = plane


def sweep_kernel(zonal, coef, ga, gb, out):
    rows = zonal.shape[1]
    total = rows + 16
    band, bands = lax.axis_index("lat"), lax.axis_size("lat")
    even = (band & 1) == 0

    def pick(plane):
        above = jnp.where(even, gb[plane], ga[0, plane])
        below = jnp.where(even, ga[1, plane], gb[plane])
        return above, below

    tails = pick(8)

    def joined(firsts, slot, own):
        ends = [
            jnp.concatenate([v, pltpu.roll(t, 128 - 8 * slot, 1) if slot else t], axis=1)
            for v, t in zip(firsts, tails)
        ]
        return jnp.concatenate([ends[0], own, ends[1]], axis=0)

    row = iota((total, 256), 0)
    outside = ((row < 8) & (band == 0)) | ((row >= rows + 8) & (band == bands - 1))
    packs = [[unpack_rows(v) for v in pick(9 + i)] for i in range(3)]
    for l in range(2):
        cells, frac, coupling = [
            joined([v[l] for v in packs[i]], 8 + 2 * i + l, coef[2 * i + l]) for i in range(3)
        ]
        weights = offset_weights(frac, cells, -1, 1)
        inverse = jnp.where(outside, 0.0, 1.0 / (1.0 + 4.0 * coupling))
        factor = coupling * inverse
        for f in range(4):
            fl = 2 * f + l
            value = jnp.where(outside, 0.0, joined(pick(fl), fl, zonal[fl]))
            source = jnp.zeros((total, 256), F32)
            for i, offset in enumerate(range(-2, 4)):
                moved = pltpu.roll(value, (-offset) % total, 0) if offset else value
                source = source + weights[i] * moved
            phi = jnp.where(outside, 0.0, source)
            source = source * inverse
            for _ in range(SWEEPS):
                beside = pltpu.roll(phi, 1, 0) + pltpu.roll(phi, total - 1, 0)
                beside = beside + pltpu.roll(phi, 1, 1) + pltpu.roll(phi, 255, 1)
                phi = source + factor * beside
            out[f, l] = pltpu.roll(phi[8 : 8 + rows], 252, 1)[:, 0:128]


def call(kernel, shapes, limit=32, **more):
    return pl.pallas_call(
        kernel,
        out_shape=[jax.ShapeDtypeStruct(s, d) for s, d in shapes],
        compiler_params=pltpu.CompilerParams(vmem_limit_bytes=limit << 20),
        **more,
    )


def body(state, zonal_shift, zonal_cells, zonal_fraction, merid_cells, merid_fraction, coupling):
    rows = state.shape[2]
    bands = lax.axis_size("lat")
    coefs = (zonal_cells, zonal_fraction, merid_cells, merid_fraction, coupling)
    loads = (state, zonal_shift, *coefs)
    lat_pairs = [
        [i * SECTORS + s, (i + 1) * SECTORS + s] for i in range(0, bands, 2) for s in range(SECTORS)
    ]
    lat_swaps = [p for i in range(1, bands - 1, 2) for p in ((i, i + 1), (i + 1, i))]

    packed, begin = call(
        pack_kernel,
        [((4, 9, rows, 128), F32), ((2, rows, 128), I32)],
        60,
        scratch_shapes=[pltpu.VMEM(v.shape, v.dtype) for v in loads] + [pltpu.SemaphoreType.DMA((7,))],
        in_specs=[pl.BlockSpec(memory_space=pltpu.HBM)] * 7,
    )(*loads)
    ring = lax.all_to_all(packed, "lon", 0, 0, axis_index_groups=Y_RINGS)
    circle = lax.all_gather(ring, "lon", axis_index_groups=CORES)
    keep, send = call(window_kernel, [((10, rows, 128), F32)] * 2)(circle, begin)
    swapped = lax.all_gather(send, "lon", axis_index_groups=Z_PAIRS)
    zonal, coef, ea, eb = call(
        zonal_kernel,
        [((8, rows, 256), F32), ((6, rows, 256), F32), ((12, 8, 128), F32), ((12, 8, 128), F32)],
    )(keep, swapped, *coefs)
    gb = lax.ppermute(eb, "lat", lat_swaps)
    ga = lax.all_gather(ea, ("lat", "lon"), axis_index_groups=lat_pairs)
    (advanced,) = call(sweep_kernel, [(state.shape, F32)])(zonal, coef, ga, gb)
    return advanced


def solution(mesh):
    in_specs = (
        P(None, None, "lat", "lon"),
        P(None, "lat"),
        P(None, "lat", "lon"),
        P(None, "lat", "lon"),
        P(None, "lat", "lon"),
        P(None, "lat", "lon"),
        P(None, "lat", "lon"),
    )
    out_specs = P(None, None, "lat", "lon")
    return jax.shard_map(body, mesh=mesh, in_specs=in_specs, out_specs=out_specs, check_vma=False)
```

time: 70.2 us -> 55.6 us (0.79)
  the two profiles are of different devices: /device:TPU:8 before, /device:TPU:6 now
where the time goes in v3:
time: 55.6 us; the launch traced here: 55.3 us
  blocking collectives  38.9 us (70%)
  starting transfers between devices  9.85 us (18%)
  Pallas kernels  6.39 us (11%)
    all_gather x1, blocking collectives, body(): swapped = lax.all_gather(send, 'lon', axis_index_groups=Z_PAIRS)  18.5 us
    all_to_all x1, blocking collectives, body(): ring = lax.all_to_all(packed, 'lon', 0, 0, axis_index_groups=Y_RINGS)  13.1 us
    ppermute x1, starting transfers between devices, body(): gb = lax.ppermute(eb, 'lat', lat_swaps)  9.85 us
    all_gather x1, blocking collectives, body(): ga = lax.all_gather(ea, ('lat', 'lon'), axis_index_groups=lat_pairs)  4.77 us
    all_gather x1, blocking collectives, body(): circle = lax.all_gather(ring, 'lon', axis_index_groups=CORES)  2.56 us
    pallas_call x1, Pallas kernels, body(): advanced, = call(sweep_kernel, [(state.shape, F32)])(zonal, coef, ga, gb)  2.53 us
    pallas_call x1, Pallas kernels, body(): call(pack_kernel, [((4, 9, rows, 128), F32), ((2, rows, 128), I32)], 60,...  1.84 us
  transfers between devices with their start and end apart: 1, of which 0 were waited for; matrix products, arithmetic and copies ran while one was open for 0% of the time, Pallas kernels for 0%

profile of v3, /device:TPU:6, one launch (start us, length us, event | category | flops | bytes accessed | tf_op | source)
XLA Modules:
  0.0 55.3 jit_solution(1692753543746634190)
XLA Ops:
  0.0 1.8 %shard_map.73 = (f32[4,9,24,128]{3,2,1,0:T(8,128)}, s32[2,24,128]{2,1,0:T(8,128)}) custom-call(f32[4,2,24,128]{3,2,1,0:T(8,128)} %refs_0_.1, s32[2,24]{1,0:T(2,128)} %refs_1_.1, s32[2,24,128]{2,1,0:T(8,128)} %zc.1, f32[2,24,128]{2,1,0:T(8,128)} %zf.1, s32[2,24,128]{2,1,0:T(8,128)} %mc.1, f32[2,24,128]{2,1,0:T(8,128)} %mf.1, f32[2,24,128]{2,1,0:T(8,128)} %cp.1), custom_call_target="tpu_custom_call" | custom-call | tf_op jit(solution)/shard_map/pallas_call | solution.py:237
  1.9 13.1 %all_to_all.5 = f32[4,9,24,128]{3,2,1,0:T(8,128)S(1)} all-to-all(f32[4,9,24,128]{3,2,1,0:T(8,128)} %get-tuple-element.13), channel_id=1, replica_groups={{0,4,8,12},{1,5,9,13},{2,6,10,14},{3,7,11,15},{16,20,24,28},{17,21,25,2..., dimensions={0} | all-to-all | bytes 884736 | tf_op jit(solution)/shard_map/all_to_all | solution.py:244
  14.9 0.0 copy-start.5
  14.9 2.6 %all-gather = f32[8,9,24,128]{3,2,1,0:T(8,128)S(1)} all-gather(f32[4,9,24,128]{3,2,1,0:T(8,128)S(1)} %all_to_all.5), channel_id=2, replica_groups={{0,1},{2,3},{4,5},{6,7},{8,9},{10,11},{12,13},{14,15},{16,17},{18,19},{..., dimensions={0}, use_global_device_ids=true | all-gather | bytes 1327104 | tf_op jit(solution)/shard_map/all_gather | solution.py:245
  17.5 0.0 copy-done.5
  17.5 0.9 %shard_map.74 = (f32[10,24,128]{2,1,0:T(8,128)S(1)}, f32[10,24,128]{2,1,0:T(8,128)S(1)}) custom-call(f32[2,4,9,24,128]{4,3,2,1,0:T(8,128)S(1)} %bitcast.3, s32[2,24,128]{2,1,0:T(8,128)S(1)} %copy-done.5), custom_call_target="tpu_custom_call" | custom-call | tf_op jit(solution)/shard_map/pallas_call | solution.py:246
  18.4 0.0 copy-start
  18.5 0.0 copy-start.1
  18.5 0.0 copy-start.2
  18.5 0.0 copy-start.3
  18.5 0.0 copy-start.4
  18.5 18.5 %all-gather.1 = f32[20,24,128]{2,1,0:T(8,128)S(1)} all-gather(f32[10,24,128]{2,1,0:T(8,128)S(1)} %get-tuple-element.16), channel_id=3, replica_groups={{0,2},{1,3},{4,6},{5,7},{8,10},{9,11},{12,14},{13,15},{16,18},{17,19},{..., dimensions={0}, use_global_device_ids=true | all-gather | bytes 368640 | tf_op jit(solution)/shard_map/all_gather | solution.py:247
  37.0 0.0 copy-done
  37.0 0.0 copy-done.1
  37.0 0.0 copy-done.2
  37.0 0.0 copy-done.3
  37.0 0.0 copy-done.4
  37.1 1.1 %shard_map.75 = (f32[8,24,256]{2,1,0:T(8,128)S(1)}, f32[6,24,256]{2,1,0:T(8,128)S(1)}, f32[12,8,128]{2,1,0:T(8,128)S(1)}, f32[12,8,128]{2,1,0:T(8,128)S(1)}) custom-call(f32[10,24,128]{2,1,0:T(8,128)S(1)} %get-tuple-element.15.keep, f32[2,10,24,128]{3,2,1,0:T(8,128)S(1)} %bitcast.4, s32[2,24,128]{2,1,0:T(8,128)S(1)} %copy-done, f32[2,24,128]{2,1,0:T(8,128)S(1)} %copy-done.1, ...), custom_call_target="tpu_custom_call" | custom-call | tf_op jit(solution)/shard_map/pallas_call | solution.py:248
  38.1 9.8 %collective-permute-start = (f32[12,8,128]{2,1,0:T(8,128)S(1)}, f32[12,8,128]{2,1,0:T(8,128)S(1)}, u32[]{:S(2)}, u32[]{:S(2)}) collective-permute-start(f32[12,8,128]{2,1,0:T(8,128)S(1)} %get-tuple-element.20), channel_id=1, source_target_pairs={{16,32},{32,16},{48,64},{64,48},{80,96},{96,80},{112,128},{128,112... | collective-permute-start | bytes 147464 | tf_op jit(solution)/shard_map/ppermute | solution.py:252
  48.0 4.8 %all-gather.2 = f32[24,8,128]{2,1,0:T(8,128)S(1)} all-gather(f32[12,8,128]{2,1,0:T(8,128)S(1)} %get-tuple-element.19), channel_id=4, replica_groups={{0,16},{1,17},{2,18},{3,19},{4,20},{5,21},{6,22},{7,23},{8,24},{9,25},{..., dimensions={0}, use_global_device_ids=true | all-gather | bytes 147456 | tf_op jit(solution)/shard_map/all_gather | solution.py:253
  52.7 0.0 collective-permute-done.gb
  52.8 2.5 %shard_map.76 = f32[4,2,24,128]{3,2,1,0:T(8,128)} custom-call(f32[8,24,256]{2,1,0:T(8,128)S(1)} %get-tuple-element.17.zonal, f32[6,24,256]{2,1,0:T(8,128)S(1)} %get-tuple-element.18.coef, f32[2,12,8,128]{3,2,1,0:T(8,128)S(1)} %bitcast.5, f32[12,8,128]{2,1,0:T(8,128)S(1)} %collective-permute-done.gb), custom_call_target="tpu_custom_call" | custom-call | tf_op jit(solution)/shard_map/pallas_call | solution.py:254
Async XLA Ops:
  14.9 2.6 %copy-start.5 = (s32[2,24,128]{2,1,0:T(8,128)S(1)}, s32[2,24,128]{2,1,0:T(8,128)}, u32[]{:S(2)}) copy-start(s32[2,24,128]{2,1,0:T(8,128)} %get-tuple-element.14.begin) | copy-start | bytes 73732
  18.4 18.6 %copy-start = (s32[2,24,128]{2,1,0:T(8,128)S(1)}, s32[2,24,128]{2,1,0:T(8,128)}, u32[]{:S(2)}) copy-start(s32[2,24,128]{2,1,0:T(8,128)} %zc.1) | copy-start | bytes 73732
  18.5 18.6 %copy-start.1 = (f32[2,24,128]{2,1,0:T(8,128)S(1)}, f32[2,24,128]{2,1,0:T(8,128)}, u32[]{:S(2)}) copy-start(f32[2,24,128]{2,1,0:T(8,128)} %zf.1) | copy-start | bytes 73732
  18.5 18.6 %copy-start.2 = (s32[2,24,128]{2,1,0:T(8,128)S(1)}, s32[2,24,128]{2,1,0:T(8,128)}, u32[]{:S(2)}) copy-start(s32[2,24,128]{2,1,0:T(8,128)} %mc.1) | copy-start | bytes 73732
  18.5 18.6 %copy-start.3 = (f32[2,24,128]{2,1,0:T(8,128)S(1)}, f32[2,24,128]{2,1,0:T(8,128)}, u32[]{:S(2)}) copy-start(f32[2,24,128]{2,1,0:T(8,128)} %mf.1) | copy-start | bytes 73732
  18.5 18.6 %copy-start.4 = (f32[2,24,128]{2,1,0:T(8,128)S(1)}, f32[2,24,128]{2,1,0:T(8,128)}, u32[]{:S(2)}) copy-start(f32[2,24,128]{2,1,0:T(8,128)} %cp.1) | copy-start | bytes 73732
  38.1 14.6 %collective-permute-start = (f32[12,8,128]{2,1,0:T(8,128)S(1)}, f32[12,8,128]{2,1,0:T(8,128)S(1)}, u32[]{:S(2)}, u32[]{:S(2)}) collective-permute-start(f32[12,8,128]{2,1,0:T(8,128)S(1)} %get-tuple-element.20), channel_id=1, source_target_pairs={{16,32},{32,16},{48,64},{64,48},{80,96},{96,80},{112,128},{128,112... | collective-permute-start | bytes 147464 | tf_op jit(solution)/shard_map/ppermute | solution.py:252

commit v4 on v3

v4 whole, which is shorter than its diff:
```python
import jax
import jax.numpy as jnp
from jax import lax
from jax.experimental import pallas as pl
from jax.experimental.pallas import tpu as pltpu
from jax.sharding import PartitionSpec as P

SWEEPS = 4
F32 = jnp.float32
I32 = jnp.int32
SECTORS = 16
Z_PAIRS = [[4 * y + c, 4 * y + 2 + c] for y in range(4) for c in range(2)]
Y_RINGS = [[4 * y + k for y in range(4)] for k in range(4)]
CORES = [[2 * i, 2 * i + 1] for i in range(SECTORS // 2)]


def iota(shape, dim):
    return lax.broadcasted_iota(I32, shape, dim)


def cubic_weights(frac):
    return (
        -frac * (frac - 1.0) * (frac - 2.0) / 6.0,
        (frac + 1.0) * (frac - 1.0) * (frac - 2.0) / 2.0,
        -(frac + 1.0) * frac * (frac - 2.0) / 2.0,
        (frac + 1.0) * frac * (frac - 1.0) / 6.0,
    )


def offset_weights(frac, cells, lowest, highest):
    w = cubic_weights(frac)
    result = []
    for offset in range(-1 - highest, 3 - lowest):
        total = jnp.zeros_like(frac)
        for k in range(4):
            c = k - 1 - offset
            if lowest <= c <= highest:
                total = jnp.where(cells == float(c), w[k], total)
        result.append(total)
    return result


def pack_rows(first, second, top):
    a = jnp.where(top, first, pltpu.roll(first, 4, 0))
    b = jnp.where(top, pltpu.roll(second, 4, 0), second)
    return jnp.where(iota((8, 128), 0) < 4, a, b)


def unpack_rows(packed):
    low = iota((8, 128), 0) < 4
    turned = pltpu.roll(packed, 4, 0)
    return jnp.where(low, packed, turned), jnp.where(low, turned, packed)


def fold(x):
    lane = iota((8, 128), 1)
    low, early = lane < 80, (lane & 7) < 4
    first = jnp.where(early, x[0:8], pltpu.roll(x[8:16], 4, 1))
    second = jnp.where(early, pltpu.roll(x[16:24], 80, 1), pltpu.roll(x[16:24], 36, 1))
    return jnp.where(low, first, second)


def unfold(x):
    lane = iota((8, 128), 1)
    third = jnp.where(lane < 48, pltpu.roll(x, 48, 1), pltpu.roll(x, 92, 1))
    return jnp.concatenate([x, pltpu.roll(x, 124, 1), third], axis=0)


def pack_kernel(state, *refs):
    sources, out, begin, held, plane, sems = refs[:6], refs[6], refs[7], refs[8:14], refs[14], refs[15]
    loads = [pltpu.make_async_copy(s, h, sems.at[i]) for i, (s, h) in enumerate(zip(sources, held))]
    blocks = [
        pltpu.make_async_copy(state, out.at[peer, pl.ds(0, 8)], sems.at[6 + peer]) for peer in range(4)
    ]
    for copy in loads + blocks:
        copy.start()
    for copy in loads:
        copy.wait()
    shift, coefs = held[0], held[1:]
    rows = state.shape[1]
    group = iota((rows, 128), 1) // 8
    edges = jnp.zeros((rows, 128), F32)
    for i, ref in enumerate(coefs):
        for l in range(2):
            a = 2 * i + l
            edges = jnp.where(group == a, pltpu.roll(ref[l].astype(F32), 8 * a + 4, 1), edges)
    plane[...] = edges
    planes = [pltpu.make_async_copy(plane, out.at[peer, 8], sems.at[10 + peer]) for peer in range(4)]
    for copy in planes:
        copy.start()
    eye = iota((rows, rows), 0) == iota((rows, rows), 1)
    for l in range(2):
        line = jnp.broadcast_to(shift[l : l + 1, :].astype(F32), (rows, rows))
        moved = jnp.sum(jnp.where(eye, line, 0.0), axis=1, keepdims=True).astype(I32)
        begin[l] = jnp.broadcast_to((-moved - 7) & 2047, (rows, 128))
    for copy in blocks + planes:
        copy.wait()


def window_kernel(circle, begin, keep, send):
    rows = circle.shape[3]
    me = lax.axis_index("lon")
    core, side = me & 1, me & 2
    lane = iota((rows, 128), 1)
    outs = (keep, send)
    slot = lane // 16
    tails = [jnp.zeros((rows, 128), F32) for _ in outs]
    for l in range(2):
        spot = (begin[l] & 127) + lane
        index, inside = spot & 127, spot < 128
        hops = begin[l] >> 7
        sectors = [((me ^ (2 * t)) + hops) & 15 for t in range(2)]
        for f in range(4):
            fl = 2 * f + l
            block = [[jnp.zeros((rows, 128), F32) for _ in range(3)] for _ in range(2)]
            for y in range(4):
                for c in range(2):
                    s = 4 * y + side + c
                    value = circle[c, y, fl]
                    for t in range(2):
                        for k in range(3):
                            hit = sectors[t] == ((s - k) & 15)
                            block[t][k] = jnp.where(hit, value, block[t][k])
            for t, out in enumerate(outs):
                r = [jnp.take_along_axis(v, index, axis=1) for v in block[t]]
                out[rows * fl : rows * fl + rows] = jnp.where(inside, r[0], r[1])
                tail = jnp.where(inside, r[1], r[2])
                tail = pltpu.roll(tail, 16 * fl, 1) if fl else tail
                tails[t] = jnp.where(slot == fl, tail, tails[t])
    for t, out in enumerate(outs):
        out[8 * rows : 9 * rows] = tails[t]
    keep[9 * rows : 10 * rows] = circle[1 - core, me // 4, 8]
    outer = ((me ^ 2) + jnp.where(core == 0, 15, 1)) & 15
    outer = circle[1 - core, outer // 4, 8]
    outer = jnp.where(core == 0, outer, pltpu.roll(outer, 124, 1))
    send[9 * rows : 9 * rows + 8] = fold(outer)


def zonal_kernel(keep, swapped, zc, zf, mc, mf, cp, out, ea, eb):
    rows = zc.shape[1]
    me, band = lax.axis_index("lon"), lax.axis_index("lat")
    core = me & 1
    across = 1 - ((me >> 1) & 1)
    lane = iota((rows, 128), 1)
    outer = unfold(swapped[across, 9 * rows : 9 * rows + 8])
    outer = jnp.where(core == 0, outer, pltpu.roll(outer, 4, 1))
    early = jnp.where((lane & 7) < 4, 0, 1)
    beside = jnp.where(early == core, outer, keep[9 * rows : 10 * rows])

    def both(plane):
        at = plane * rows
        return keep[at : at + rows] + swapped[across, at : at + rows]

    def extended(ref, i, l):
        a = 2 * i + l
        own = pltpu.roll(ref[l].astype(F32), 4, 1)
        side = pltpu.roll(beside, 128 - 8 * a, 1) if a else beside
        return jnp.where(lane < 4, side, own), jnp.where(lane < 4, own, side)

    ends = both(8)
    slot = lane // 8
    tails = jnp.zeros((rows, 128), F32)
    for l in range(2):
        cells, frac = [jnp.concatenate(extended(r, i, l), axis=1) for i, r in enumerate((zc, zf))]
        weights = offset_weights(frac, cells, -2, 2)
        for f in range(4):
            fl = 2 * f + l
            end = pltpu.roll(ends, 128 - 16 * fl, 1) if fl else ends
            window = jnp.concatenate([both(fl), end], axis=1)
            total = weights[0] * window
            for d in range(1, 8):
                total = total + weights[d] * pltpu.roll(window, 256 - d, 1)
            out[fl] = total[:, 0:128]
            tail = pltpu.roll(total[:, 128:256], 8 * fl, 1) if fl else total[:, 128:256]
            tails = jnp.where(slot == fl, tail, tails)
    for i, ref in enumerate((mc, mf, cp)):
        for l in range(2):
            a = 8 + 2 * i + l
            out[a + 1], tail = extended(ref, i + 2, l)
            tails = jnp.where(slot == a, pltpu.roll(tail, 8 * a, 1), tails)
    out[8] = tails

    even = (band & 1) == 0
    for e, top in ((ea, jnp.logical_not(even)), (eb, even)):
        take = pl.ds(pl.multiple_of(jnp.where(top, 0, rows - 8), 8), 8)
        for plane in range(9):
            e[plane] = out[plane, take]
        for i in range(3):
            e[9 + i] = pack_rows(out[9 + 2 * i, take], out[10 + 2 * i, take], top)


def sweep_kernel(main, ga, gb, result, done, sems):
    rows = main.shape[1]
    total = rows + 8
    band, bands = lax.axis_index("lat"), lax.axis_size("lat")
    even = (band & 1) == 0
    lane, row = iota((total, 128), 1), iota((total, 128), 0)
    outside = ((row < 4) & (band == 0)) | ((row >= rows + 4) & (band == bands - 1))
    tall = iota((rows + 16, 128), 0)
    beyond = ((tall < 8) & (band == 0)) | ((tall >= rows + 8) & (band == bands - 1))

    def pick(plane):
        above = jnp.where(even, gb[plane], ga[0, plane])
        below = jnp.where(even, ga[1, plane], gb[plane])
        return above, below

    def joined(ends, own):
        return jnp.concatenate([ends[0], own, ends[1]], axis=0)

    def rotated(x, lanes):
        return pltpu.roll(x, lanes % 128, 1) if lanes % 128 else x

    def prepare(cells, frac, coupling):
        weights = offset_weights(frac, cells, -1, 1)
        inverse = jnp.where(outside, 0.0, 1.0 / (1.0 + 4.0 * coupling))
        return weights, inverse, coupling * inverse

    def source_of(value, weights):
        value = jnp.where(beyond, 0.0, value)
        source = jnp.zeros((total, 128), F32)
        for i in range(6):
            moved = pltpu.roll(value, rows + 16 - (2 + i), 0)[:total]
            source = source + weights[i] * moved
        return jnp.where(outside, 0.0, source)

    packs = [[unpack_rows(v) for v in pick(9 + i)] for i in range(3)]
    tails = joined(pick(8), main[8])
    edge = pltpu.roll(tails, rows + 12, 0)[:total]
    group = []
    for i in range(3):
        v = rotated(edge, 64 - 16 * i)
        v = jnp.where(lane < 16, v, pltpu.roll(v, 16, 1))
        group.append(jnp.where(lane < 32, v, pltpu.roll(v, 32, 1)))
    weights, inverse, tail_factor = prepare(*group)
    tail = source_of(tails, weights)
    tail_source = tail * inverse
    phi, source, factor = [None] * 8, [None] * 8, [None] * 8
    for l in range(2):
        coefs = []
        for i in range(3):
            own = joined([v[l] for v in packs[i]], main[9 + 2 * i + l])
            coefs.append(pltpu.roll(own, rows + 12, 0)[:total])
        weights, inverse, level_factor = prepare(*coefs)
        for f in range(4):
            fl = 2 * f + l
            value = source_of(joined(pick(fl), main[fl]), weights)
            phi[fl] = rotated(value, 8 * fl)
            source[fl] = rotated(value * inverse, 8 * fl)
            factor[fl] = rotated(level_factor, 8 * fl)
    for sweep in range(SWEEPS):
        old_tail = tail
        tail_left, tail_right = pltpu.roll(tail, 1, 1), pltpu.roll(tail, 127, 1)
        for fl in range(8):
            old = phi[fl]
            left = pltpu.roll(old, 1, 1)
            tail_left = jnp.where(lane == 8 * fl, left, tail_left)
            right = jnp.where(lane == (8 * fl - 1) % 128, tail_right, pltpu.roll(old, 127, 1))
            beside = pltpu.roll(old, 1, 0) + pltpu.roll(old, total - 1, 0) + left + right
            phi[fl] = source[fl] + factor[fl] * beside
        beside = pltpu.roll(old_tail, 1, 0) + pltpu.roll(old_tail, total - 1, 0)
        tail = tail_source + tail_factor * (beside + tail_left + tail_right)
    copies = []
    for fl in range(8):
        whole = jnp.where((lane >= 8 * fl) & (lane < 8 * fl + 4), tail, phi[fl])
        whole = rotated(whole, -4 - 8 * fl)
        done[fl] = pltpu.roll(whole, total - 4, 0)[:rows]
        copies.append(pltpu.make_async_copy(done.at[fl], result.at[fl], sems.at[fl]))
        copies[-1].start()
    for copy in copies:
        copy.wait()


def call(kernel, shapes, limit=32, **more):
    return pl.pallas_call(
        kernel,
        out_shape=[jax.ShapeDtypeStruct(s, d) for s, d in shapes],
        compiler_params=pltpu.CompilerParams(vmem_limit_bytes=limit << 20),
        **more,
    )


def body(state, zonal_shift, zonal_cells, zonal_fraction, merid_cells, merid_fraction, coupling):
    rows = state.shape[2]
    bands = lax.axis_size("lat")
    coefs = (zonal_cells, zonal_fraction, merid_cells, merid_fraction, coupling)
    loads = (state, zonal_shift, *coefs)
    lat_pairs = [
        [i * SECTORS + s, (i + 1) * SECTORS + s] for i in range(0, bands, 2) for s in range(SECTORS)
    ]
    lat_swaps = [p for i in range(1, bands - 1, 2) for p in ((i, i + 1), (i + 1, i))]

    hbm = pl.BlockSpec(memory_space=pltpu.HBM)
    vmem = pl.BlockSpec(memory_space=pltpu.VMEM)
    packed, begin = call(
        pack_kernel,
        [((4, 9, rows, 128), F32), ((2, rows, 128), I32)],
        60,
        scratch_shapes=[pltpu.VMEM(v.shape, v.dtype) for v in loads[1:]]
        + [pltpu.VMEM((rows, 128), F32), pltpu.SemaphoreType.DMA((14,))],
        in_specs=[hbm] * 7,
        out_specs=[hbm, vmem],
    )(state.reshape(8, rows, 128), *loads[1:])
    ring = lax.all_to_all(packed, "lon", 0, 0, axis_index_groups=Y_RINGS)
    circle = lax.all_gather(ring, "lon", axis_index_groups=CORES)
    keep, send = call(
        window_kernel, [((10 * rows, 128), F32), ((9 * rows + 8, 128), F32)]
    )(circle, begin)
    swapped = lax.all_gather(send, "lon", axis_index_groups=Z_PAIRS)
    main, ea, eb = call(
        zonal_kernel, [((15, rows, 128), F32), ((12, 8, 128), F32), ((12, 8, 128), F32)]
    )(keep, swapped, *coefs)
    gb = lax.ppermute(eb, "lat", lat_swaps)
    ga = lax.all_gather(ea, ("lat", "lon"), axis_index_groups=lat_pairs)
    (advanced,) = call(
        sweep_kernel,
        [((8, rows, 128), F32)],
        scratch_shapes=[pltpu.VMEM((8, rows, 128), F32), pltpu.SemaphoreType.DMA((8,))],
        out_specs=[hbm],
    )(main, ga, gb)
    return advanced.reshape(state.shape)


def solution(mesh):
    in_specs = (
        P(None, None, "lat", "lon"),
        P(None, "lat"),
        P(None, "lat", "lon"),
        P(None, "lat", "lon"),
        P(None, "lat", "lon"),
        P(None, "lat", "lon"),
        P(None, "lat", "lon"),
    )
    out_specs = P(None, None, "lat", "lon")
    return jax.shard_map(body, mesh=mesh, in_specs=in_specs, out_specs=out_specs, check_vma=False)
```

time: 55.6 us -> 66.6 us (1.20)
  Pallas kernels: 6.39 us -> 17.5 us
    pallas_call x1, Pallas kernels: 1.84 us -> 13.8 us  [body(): call(pack_kernel, [((4, 9, rows, 128), F32), ((2, rows, 128), I32)], 60,...]
    pallas_call x3, Pallas kernels: 4.55 us -> 3.79 us  [the longest x1 1.5 us: body(): call(sweep_kernel, [((8, rows, 128), F32)], scratch_shapes=[pltpu.VMEM((8...]
where the time goes in v4:
time: 66.6 us; the launch traced here: 66.2 us
  blocking collectives  38.7 us (58%)
  Pallas kernels  17.5 us (26%)
  starting transfers between devices  9.83 us (15%)
    all_gather x1, blocking collectives, body(): swapped = lax.all_gather(send, 'lon', axis_index_groups=Z_PAIRS)  18.3 us
    pallas_call x1, Pallas kernels, body(): call(pack_kernel, [((4, 9, rows, 128), F32), ((2, rows, 128), I32)], 60,...  13.8 us
    all_to_all x1, blocking collectives, body(): ring = lax.all_to_all(packed, 'lon', 0, 0, axis_index_groups=Y_RINGS)  13.1 us
    ppermute x1, starting transfers between devices, body(): gb = lax.ppermute(eb, 'lat', lat_swaps)  9.83 us
    all_gather x1, blocking collectives, body(): ga = lax.all_gather(ea, ('lat', 'lon'), axis_index_groups=lat_pairs)  4.77 us
    all_gather x1, blocking collectives, body(): circle = lax.all_gather(ring, 'lon', axis_index_groups=CORES)  2.56 us
    pallas_call x1, Pallas kernels, body(): call(sweep_kernel, [((8, rows, 128), F32)], scratch_shapes=[pltpu.VMEM((8...  1.5 us
  transfers between devices with their start and end apart: 1, of which 0 were waited for; matrix products, arithmetic and copies ran while one was open for 0% of the time, Pallas kernels for 0%

profile of v4, /device:TPU:6, one launch (start us, length us, event | category | flops | bytes accessed | tf_op | source)
XLA Modules:
  0.0 66.2 jit_solution(1085182341020242035)
XLA Ops:
  0.0 13.8 %shard_map.73 = (f32[4,9,24,128]{3,2,1,0:T(8,128)}, s32[2,24,128]{2,1,0:T(8,128)}) custom-call(f32[8,24,128]{2,1,0:T(8,128)} %bitcast.8, s32[2,24]{1,0:T(2,128)} %refs_0_.1, s32[2,24,128]{2,1,0:T(8,128)} %zc.1, f32[2,24,128]{2,1,0:T(8,128)} %zf.1, s32[2,24,128]{2,1,0:T(8,128)} %mc.1, f32[2,24,128]{2,1,0:T(8,128)} %mf.1, f32[2,24,128]{2,1,0:T(8,128)} %cp.1), custom_call_target="tpu_custom_call" | custom-call | tf_op jit(solution)/shard_map/pallas_call | solution.py:294
  13.8 13.1 %all_to_all.5 = f32[4,9,24,128]{3,2,1,0:T(8,128)S(1)} all-to-all(f32[4,9,24,128]{3,2,1,0:T(8,128)} %get-tuple-element.12), channel_id=1, replica_groups={{0,4,8,12},{1,5,9,13},{2,6,10,14},{3,7,11,15},{16,20,24,28},{17,21,25,2..., dimensions={0} | all-to-all | bytes 884736 | tf_op jit(solution)/shard_map/all_to_all | solution.py:303
  26.8 0.0 copy-start.5
  26.8 2.6 %all-gather = f32[8,9,24,128]{3,2,1,0:T(8,128)S(1)} all-gather(f32[4,9,24,128]{3,2,1,0:T(8,128)S(1)} %all_to_all.5), channel_id=2, replica_groups={{0,1},{2,3},{4,5},{6,7},{8,9},{10,11},{12,13},{14,15},{16,17},{18,19},{..., dimensions={0}, use_global_device_ids=true | all-gather | bytes 1327104 | tf_op jit(solution)/shard_map/all_gather | solution.py:304
  29.4 0.0 copy-done.5
  29.4 1.0 %shard_map.74 = (f32[240,128]{1,0:T(8,128)S(1)}, f32[224,128]{1,0:T(8,128)S(1)}) custom-call(f32[2,4,9,24,128]{4,3,2,1,0:T(8,128)S(1)} %bitcast.5, s32[2,24,128]{2,1,0:T(8,128)S(1)} %copy-done.5), custom_call_target="tpu_custom_call" | custom-call | tf_op jit(solution)/shard_map/pallas_call | solution.py:305
  30.4 0.0 copy-start
  30.4 0.0 copy-start.1
  30.4 0.0 copy-start.2
  30.4 0.0 copy-start.3
  30.5 0.0 copy-start.4
  30.5 18.3 %all-gather.1 = f32[448,128]{1,0:T(8,128)S(1)} all-gather(f32[224,128]{1,0:T(8,128)S(1)} %get-tuple-element.15), channel_id=3, replica_groups={{0,2},{1,3},{4,6},{5,7},{8,10},{9,11},{12,14},{13,15},{16,18},{17,19},{..., dimensions={0}, use_global_device_ids=true | all-gather | bytes 344064 | tf_op jit(solution)/shard_map/all_gather | solution.py:308
  48.8 0.0 copy-done
  48.8 0.0 copy-done.1
  48.8 0.0 copy-done.2
  48.8 0.0 copy-done.3
  48.8 0.0 copy-done.4
  48.8 1.3 %shard_map.75 = (f32[15,24,128]{2,1,0:T(8,128)S(1)}, f32[12,8,128]{2,1,0:T(8,128)S(1)}, f32[12,8,128]{2,1,0:T(8,128)S(1)}) custom-call(f32[240,128]{1,0:T(8,128)S(1)} %get-tuple-element.14.keep, f32[2,224,128]{2,1,0:T(8,128)S(1)} %bitcast.6, s32[2,24,128]{2,1,0:T(8,128)S(1)} %copy-done, f32[2,24,128]{2,1,0:T(8,128)S(1)} %copy-done.1, ...), custom_call_target="tpu_custom_call" | custom-call | tf_op jit(solution)/shard_map/pallas_call | solution.py:309
  50.1 9.8 %collective-permute-start = (f32[12,8,128]{2,1,0:T(8,128)S(1)}, f32[12,8,128]{2,1,0:T(8,128)S(1)}, u32[]{:S(2)}, u32[]{:S(2)}) collective-permute-start(f32[12,8,128]{2,1,0:T(8,128)S(1)} %get-tuple-element.18), channel_id=1, source_target_pairs={{16,32},{32,16},{48,64},{64,48},{80,96},{96,80},{112,128},{128,112... | collective-permute-start | bytes 147464 | tf_op jit(solution)/shard_map/ppermute | solution.py:312
  60.0 4.8 %all-gather.2 = f32[24,8,128]{2,1,0:T(8,128)S(1)} all-gather(f32[12,8,128]{2,1,0:T(8,128)S(1)} %get-tuple-element.17), channel_id=4, replica_groups={{0,16},{1,17},{2,18},{3,19},{4,20},{5,21},{6,22},{7,23},{8,24},{9,25},{..., dimensions={0}, use_global_device_ids=true | all-gather | bytes 147456 | tf_op jit(solution)/shard_map/all_gather | solution.py:313
  64.7 0.0 collective-permute-done.gb
  64.7 1.5 %shard_map.76 = f32[8,24,128]{2,1,0:T(8,128)} custom-call(f32[15,24,128]{2,1,0:T(8,128)S(1)} %get-tuple-element.16.main, f32[2,12,8,128]{3,2,1,0:T(8,128)S(1)} %bitcast.7, f32[12,8,128]{2,1,0:T(8,128)S(1)} %collective-permute-done.gb), custom_call_target="tpu_custom_call" | custom-call | tf_op jit(solution)/shard_map/pallas_call | solution.py:314
Async XLA Ops:
  26.8 2.6 %copy-start.5 = (s32[2,24,128]{2,1,0:T(8,128)S(1)}, s32[2,24,128]{2,1,0:T(8,128)}, u32[]{:S(2)}) copy-start(s32[2,24,128]{2,1,0:T(8,128)} %get-tuple-element.13.begin) | copy-start | bytes 73732
  30.4 18.4 %copy-start = (s32[2,24,128]{2,1,0:T(8,128)S(1)}, s32[2,24,128]{2,1,0:T(8,128)}, u32[]{:S(2)}) copy-start(s32[2,24,128]{2,1,0:T(8,128)} %zc.1) | copy-start | bytes 73732
  30.4 18.4 %copy-start.1 = (f32[2,24,128]{2,1,0:T(8,128)S(1)}, f32[2,24,128]{2,1,0:T(8,128)}, u32[]{:S(2)}) copy-start(f32[2,24,128]{2,1,0:T(8,128)} %zf.1) | copy-start | bytes 73732
  30.4 18.4 %copy-start.2 = (s32[2,24,128]{2,1,0:T(8,128)S(1)}, s32[2,24,128]{2,1,0:T(8,128)}, u32[]{:S(2)}) copy-start(s32[2,24,128]{2,1,0:T(8,128)} %mc.1) | copy-start | bytes 73732
  30.4 18.4 %copy-start.3 = (f32[2,24,128]{2,1,0:T(8,128)S(1)}, f32[2,24,128]{2,1,0:T(8,128)}, u32[]{:S(2)}) copy-start(f32[2,24,128]{2,1,0:T(8,128)} %mf.1) | copy-start | bytes 73732
  30.5 18.4 %copy-start.4 = (f32[2,24,128]{2,1,0:T(8,128)S(1)}, f32[2,24,128]{2,1,0:T(8,128)}, u32[]{:S(2)}) copy-start(f32[2,24,128]{2,1,0:T(8,128)} %cp.1) | copy-start | bytes 73732
  50.1 14.6 %collective-permute-start = (f32[12,8,128]{2,1,0:T(8,128)S(1)}, f32[12,8,128]{2,1,0:T(8,128)S(1)}, u32[]{:S(2)}, u32[]{:S(2)}) collective-permute-start(f32[12,8,128]{2,1,0:T(8,128)S(1)} %get-tuple-element.18), channel_id=1, source_target_pairs={{16,32},{32,16},{48,64},{64,48},{80,96},{96,80},{112,128},{128,112... | collective-permute-start | bytes 147464 | tf_op jit(solution)/shard_map/ppermute | solution.py:312

commit v5 on v4

--- a/solution.py
+++ b/solution.py
@@ -66,17 +66,14 @@
     return jnp.concatenate([x, pltpu.roll(x, 124, 1), third], axis=0)
 
 
-def pack_kernel(state, *refs):
-    sources, out, begin, held, plane, sems = refs[:6], refs[6], refs[7], refs[8:14], refs[14], refs[15]
+def pack_kernel(*refs):
+    sources, out, begin, held, sems = refs[:7], refs[7], refs[8], refs[9:16], refs[16]
     loads = [pltpu.make_async_copy(s, h, sems.at[i]) for i, (s, h) in enumerate(zip(sources, held))]
-    blocks = [
-        pltpu.make_async_copy(state, out.at[peer, pl.ds(0, 8)], sems.at[6 + peer]) for peer in range(4)
-    ]
-    for copy in loads + blocks:
+    for copy in loads:
         copy.start()
-    for copy in loads:
+    for copy in loads[1:]:
         copy.wait()
-    shift, coefs = held[0], held[1:]
+    state, shift, coefs = held[0], held[1], held[2:]
     rows = state.shape[1]
     group = iota((rows, 128), 1) // 8
     edges = jnp.zeros((rows, 128), F32)
@@ -84,17 +81,17 @@
         for l in range(2):
             a = 2 * i + l
             edges = jnp.where(group == a, pltpu.roll(ref[l].astype(F32), 8 * a + 4, 1), edges)
-    plane[...] = edges
-    planes = [pltpu.make_async_copy(plane, out.at[peer, 8], sems.at[10 + peer]) for peer in range(4)]
-    for copy in planes:
-        copy.start()
     eye = iota((rows, rows), 0) == iota((rows, rows), 1)
     for l in range(2):
         line = jnp.broadcast_to(shift[l : l + 1, :].astype(F32), (rows, rows))
         moved = jnp.sum(jnp.where(eye, line, 0.0), axis=1, keepdims=True).astype(I32)
         begin[l] = jnp.broadcast_to((-moved - 7) & 2047, (rows, 128))
-    for copy in blocks + planes:
-        copy.wait()
+    loads[0].wait()
+    for fl in range(8):
+        for peer in range(4):
+            out[peer, fl] = state[fl]
+    for peer in range(4):
+        out[peer, 8] = edges
 
 
 def window_kernel(circle, begin, keep, send):
@@ -283,23 +280,21 @@
     rows = state.shape[2]
     bands = lax.axis_size("lat")
     coefs = (zonal_cells, zonal_fraction, merid_cells, merid_fraction, coupling)
-    loads = (state, zonal_shift, *coefs)
+    loads = (state.reshape(8, rows, 128), zonal_shift, *coefs)
     lat_pairs = [
         [i * SECTORS + s, (i + 1) * SECTORS + s] for i in range(0, bands, 2) for s in range(SECTORS)
     ]
     lat_swaps = [p for i in range(1, bands - 1, 2) for p in ((i, i + 1), (i + 1, i))]
 
     hbm = pl.BlockSpec(memory_space=pltpu.HBM)
-    vmem = pl.BlockSpec(memory_space=pltpu.VMEM)
     packed, begin = call(
         pack_kernel,
         [((4, 9, rows, 128), F32), ((2, rows, 128), I32)],
         60,
-        scratch_shapes=[pltpu.VMEM(v.shape, v.dtype) for v in loads[1:]]
-        + [pltpu.VMEM((rows, 128), F32), pltpu.SemaphoreType.DMA((14,))],
+        scratch_shapes=[pltpu.VMEM(v.shape, v.dtype) for v in loads]
+        + [pltpu.SemaphoreType.DMA((7,))],
         in_specs=[hbm] * 7,
-        out_specs=[hbm, vmem],
-    )(state.reshape(8, rows, 128), *loads[1:])
+    )(*loads)
     ring = lax.all_to_all(packed, "lon", 0, 0, axis_index_groups=Y_RINGS)
     circle = lax.all_gather(ring, "lon", axis_index_groups=CORES)
     keep, send = call(

time: 66.6 us -> 54.6 us (0.82)
  Pallas kernels: 17.5 us -> 5.63 us
    pallas_call x1, Pallas kernels: 13.8 us -> 1.84 us  [body(): call(pack_kernel, [((4, 9, rows, 128), F32), ((2, rows, 128), I32)], 60,...]
where the time goes in v5:
time: 54.6 us; the launch traced here: 54.3 us
  blocking collectives  38.7 us (71%)
  starting transfers between devices  9.83 us (18%)
  Pallas kernels  5.63 us (10%)
    all_gather x1, blocking collectives, body(): swapped = lax.all_gather(send, 'lon', axis_index_groups=Z_PAIRS)  18.3 us
    all_to_all x1, blocking collectives, body(): ring = lax.all_to_all(packed, 'lon', 0, 0, axis_index_groups=Y_RINGS)  13.1 us
    ppermute x1, starting transfers between devices, body(): gb = lax.ppermute(eb, 'lat', lat_swaps)  9.83 us
    all_gather x1, blocking collectives, body(): ga = lax.all_gather(ea, ('lat', 'lon'), axis_index_groups=lat_pairs)  4.77 us
    all_gather x1, blocking collectives, body(): circle = lax.all_gather(ring, 'lon', axis_index_groups=CORES)  2.56 us
    pallas_call x1, Pallas kernels, body(): call(pack_kernel, [((4, 9, rows, 128), F32), ((2, rows, 128), I32)], 60,...  1.84 us
    pallas_call x1, Pallas kernels, body(): call(sweep_kernel, [((8, rows, 128), F32)], scratch_shapes=[pltpu.VMEM((8...  1.5 us
    pallas_call x1, Pallas kernels, body(): call(zonal_kernel, [((15, rows, 128), F32), ((12, 8, 128), F32), ((12, 8,...  1.28 us
  transfers between devices with their start and end apart: 1, of which 0 were waited for; matrix products, arithmetic and copies ran while one was open for 0% of the time, Pallas kernels for 0%

profile of v5, /device:TPU:6, one launch (start us, length us, event | category | flops | bytes accessed | tf_op | source)
XLA Modules:
  0.0 54.3 jit_solution(6164815194053381476)
XLA Ops:
  0.0 1.8 %shard_map.73 = (f32[4,9,24,128]{3,2,1,0:T(8,128)}, s32[2,24,128]{2,1,0:T(8,128)}) custom-call(f32[8,24,128]{2,1,0:T(8,128)} %bitcast.8, s32[2,24]{1,0:T(2,128)} %refs_1_.1, s32[2,24,128]{2,1,0:T(8,128)} %zc.1, f32[2,24,128]{2,1,0:T(8,128)} %zf.1, s32[2,24,128]{2,1,0:T(8,128)} %mc.1, f32[2,24,128]{2,1,0:T(8,128)} %mf.1, f32[2,24,128]{2,1,0:T(8,128)} %cp.1), custom_call_target="tpu_custom_call" | custom-call | tf_op jit(solution)/shard_map/pallas_call | solution.py:290
  1.8 13.1 %all_to_all.5 = f32[4,9,24,128]{3,2,1,0:T(8,128)S(1)} all-to-all(f32[4,9,24,128]{3,2,1,0:T(8,128)} %get-tuple-element.12), channel_id=1, replica_groups={{0,4,8,12},{1,5,9,13},{2,6,10,14},{3,7,11,15},{16,20,24,28},{17,21,25,2..., dimensions={0} | all-to-all | bytes 884736 | tf_op jit(solution)/shard_map/all_to_all | solution.py:298
  14.9 0.0 copy-start.5
  14.9 2.6 %all-gather = f32[8,9,24,128]{3,2,1,0:T(8,128)S(1)} all-gather(f32[4,9,24,128]{3,2,1,0:T(8,128)S(1)} %all_to_all.5), channel_id=2, replica_groups={{0,1},{2,3},{4,5},{6,7},{8,9},{10,11},{12,13},{14,15},{16,17},{18,19},{..., dimensions={0}, use_global_device_ids=true | all-gather | bytes 1327104 | tf_op jit(solution)/shard_map/all_gather | solution.py:299
  17.5 0.0 copy-done.5
  17.5 1.0 %shard_map.74 = (f32[240,128]{1,0:T(8,128)S(1)}, f32[224,128]{1,0:T(8,128)S(1)}) custom-call(f32[2,4,9,24,128]{4,3,2,1,0:T(8,128)S(1)} %bitcast.5, s32[2,24,128]{2,1,0:T(8,128)S(1)} %copy-done.5), custom_call_target="tpu_custom_call" | custom-call | tf_op jit(solution)/shard_map/pallas_call | solution.py:300
  18.5 0.0 copy-start
  18.5 0.0 copy-start.1
  18.5 0.0 copy-start.2
  18.5 0.0 copy-start.3
  18.5 0.0 copy-start.4
  18.6 18.3 %all-gather.1 = f32[448,128]{1,0:T(8,128)S(1)} all-gather(f32[224,128]{1,0:T(8,128)S(1)} %get-tuple-element.15), channel_id=3, replica_groups={{0,2},{1,3},{4,6},{5,7},{8,10},{9,11},{12,14},{13,15},{16,18},{17,19},{..., dimensions={0}, use_global_device_ids=true | all-gather | bytes 344064 | tf_op jit(solution)/shard_map/all_gather | solution.py:303
  36.9 0.0 copy-done
  36.9 0.0 copy-done.1
  36.9 0.0 copy-done.2
  36.9 0.0 copy-done.3
  36.9 0.0 copy-done.4
  36.9 1.3 %shard_map.75 = (f32[15,24,128]{2,1,0:T(8,128)S(1)}, f32[12,8,128]{2,1,0:T(8,128)S(1)}, f32[12,8,128]{2,1,0:T(8,128)S(1)}) custom-call(f32[240,128]{1,0:T(8,128)S(1)} %get-tuple-element.14.keep, f32[2,224,128]{2,1,0:T(8,128)S(1)} %bitcast.6, s32[2,24,128]{2,1,0:T(8,128)S(1)} %copy-done, f32[2,24,128]{2,1,0:T(8,128)S(1)} %copy-done.1, ...), custom_call_target="tpu_custom_call" | custom-call | tf_op jit(solution)/shard_map/pallas_call | solution.py:304
  38.2 9.8 %collective-permute-start = (f32[12,8,128]{2,1,0:T(8,128)S(1)}, f32[12,8,128]{2,1,0:T(8,128)S(1)}, u32[]{:S(2)}, u32[]{:S(2)}) collective-permute-start(f32[12,8,128]{2,1,0:T(8,128)S(1)} %get-tuple-element.18), channel_id=1, source_target_pairs={{16,32},{32,16},{48,64},{64,48},{80,96},{96,80},{112,128},{128,112... | collective-permute-start | bytes 147464 | tf_op jit(solution)/shard_map/ppermute | solution.py:307
  48.1 4.8 %all-gather.2 = f32[24,8,128]{2,1,0:T(8,128)S(1)} all-gather(f32[12,8,128]{2,1,0:T(8,128)S(1)} %get-tuple-element.17), channel_id=4, replica_groups={{0,16},{1,17},{2,18},{3,19},{4,20},{5,21},{6,22},{7,23},{8,24},{9,25},{..., dimensions={0}, use_global_device_ids=true | all-gather | bytes 147456 | tf_op jit(solution)/shard_map/all_gather | solution.py:308
  52.8 0.0 collective-permute-done.gb
  52.8 1.5 %shard_map.76 = f32[8,24,128]{2,1,0:T(8,128)} custom-call(f32[15,24,128]{2,1,0:T(8,128)S(1)} %get-tuple-element.16.main, f32[2,12,8,128]{3,2,1,0:T(8,128)S(1)} %bitcast.7, f32[12,8,128]{2,1,0:T(8,128)S(1)} %collective-permute-done.gb), custom_call_target="tpu_custom_call" | custom-call | tf_op jit(solution)/shard_map/pallas_call | solution.py:309
Async XLA Ops:
  14.9 2.6 %copy-start.5 = (s32[2,24,128]{2,1,0:T(8,128)S(1)}, s32[2,24,128]{2,1,0:T(8,128)}, u32[]{:S(2)}) copy-start(s32[2,24,128]{2,1,0:T(8,128)} %get-tuple-element.13.begin) | copy-start | bytes 73732
  18.5 18.4 %copy-start = (s32[2,24,128]{2,1,0:T(8,128)S(1)}, s32[2,24,128]{2,1,0:T(8,128)}, u32[]{:S(2)}) copy-start(s32[2,24,128]{2,1,0:T(8,128)} %zc.1) | copy-start | bytes 73732
  18.5 18.4 %copy-start.1 = (f32[2,24,128]{2,1,0:T(8,128)S(1)}, f32[2,24,128]{2,1,0:T(8,128)}, u32[]{:S(2)}) copy-start(f32[2,24,128]{2,1,0:T(8,128)} %zf.1) | copy-start | bytes 73732
  18.5 18.4 %copy-start.2 = (s32[2,24,128]{2,1,0:T(8,128)S(1)}, s32[2,24,128]{2,1,0:T(8,128)}, u32[]{:S(2)}) copy-start(s32[2,24,128]{2,1,0:T(8,128)} %mc.1) | copy-start | bytes 73732
  18.5 18.4 %copy-start.3 = (f32[2,24,128]{2,1,0:T(8,128)S(1)}, f32[2,24,128]{2,1,0:T(8,128)}, u32[]{:S(2)}) copy-start(f32[2,24,128]{2,1,0:T(8,128)} %mf.1) | copy-start | bytes 73732
  18.5 18.4 %copy-start.4 = (f32[2,24,128]{2,1,0:T(8,128)S(1)}, f32[2,24,128]{2,1,0:T(8,128)}, u32[]{:S(2)}) copy-start(f32[2,24,128]{2,1,0:T(8,128)} %cp.1) | copy-start | bytes 73732
  38.2 14.6 %collective-permute-start = (f32[12,8,128]{2,1,0:T(8,128)S(1)}, f32[12,8,128]{2,1,0:T(8,128)S(1)}, u32[]{:S(2)}, u32[]{:S(2)}) collective-permute-start(f32[12,8,128]{2,1,0:T(8,128)S(1)} %get-tuple-element.18), channel_id=1, source_target_pairs={{16,32},{32,16},{48,64},{64,48},{80,96},{96,80},{112,128},{128,112... | collective-permute-start | bytes 147464 | tf_op jit(solution)/shard_map/ppermute | solution.py:307

commit v6 on v5

--- a/solution.py
+++ b/solution.py
@@ -10,8 +10,7 @@
 I32 = jnp.int32
 SECTORS = 16
 Z_PAIRS = [[4 * y + c, 4 * y + 2 + c] for y in range(4) for c in range(2)]
-Y_RINGS = [[4 * y + k for y in range(4)] for k in range(4)]
-CORES = [[2 * i, 2 * i + 1] for i in range(SECTORS // 2)]
+SIDES = [[4 * y + 2 * z + c for y in range(4) for c in range(2)] for z in range(2)]
 
 
 def iota(shape, dim):
@@ -88,14 +87,12 @@
         begin[l] = jnp.broadcast_to((-moved - 7) & 2047, (rows, 128))
     loads[0].wait()
     for fl in range(8):
-        for peer in range(4):
-            out[peer, fl] = state[fl]
-    for peer in range(4):
-        out[peer, 8] = edges
+        out[fl] = state[fl]
+    out[8] = edges
 
 
 def window_kernel(circle, begin, keep, send):
-    rows = circle.shape[3]
+    rows = circle.shape[2]
     me = lax.axis_index("lon")
     core, side = me & 1, me & 2
     lane = iota((rows, 128), 1)
@@ -113,7 +110,7 @@
             for y in range(4):
                 for c in range(2):
                     s = 4 * y + side + c
-                    value = circle[c, y, fl]
+                    value = circle[2 * y + c, fl]
                     for t in range(2):
                         for k in range(3):
                             hit = sectors[t] == ((s - k) & 15)
@@ -126,9 +123,9 @@
                 tails[t] = jnp.where(slot == fl, tail, tails[t])
     for t, out in enumerate(outs):
         out[8 * rows : 9 * rows] = tails[t]
-    keep[9 * rows : 10 * rows] = circle[1 - core, me // 4, 8]
+    keep[9 * rows : 10 * rows] = circle[me // 4 * 2 + 1 - core, 8]
     outer = ((me ^ 2) + jnp.where(core == 0, 15, 1)) & 15
-    outer = circle[1 - core, outer // 4, 8]
+    outer = circle[outer // 4 * 2 + 1 - core, 8]
     outer = jnp.where(core == 0, outer, pltpu.roll(outer, 124, 1))
     send[9 * rows : 9 * rows + 8] = fold(outer)
 
@@ -289,14 +286,13 @@
     hbm = pl.BlockSpec(memory_space=pltpu.HBM)
     packed, begin = call(
         pack_kernel,
-        [((4, 9, rows, 128), F32), ((2, rows, 128), I32)],
+        [((9, rows, 128), F32), ((2, rows, 128), I32)],
         60,
         scratch_shapes=[pltpu.VMEM(v.shape, v.dtype) for v in loads]
         + [pltpu.SemaphoreType.DMA((7,))],
         in_specs=[hbm] * 7,
     )(*loads)
-    ring = lax.all_to_all(packed, "lon", 0, 0, axis_index_groups=Y_RINGS)
-    circle = lax.all_gather(ring, "lon", axis_index_groups=CORES)
+    circle = lax.all_gather(packed, "lon", axis_index_groups=SIDES)
     keep, send = call(
         window_kernel, [((10 * rows, 128), F32), ((9 * rows + 8, 128), F32)]
     )(circle, begin)

time: 54.6 us -> 53.2 us (0.974)
  blocking collectives: 38.7 us -> 37.5 us
    all_to_all x1 -> x0, blocking collectives: 13.1 us -> none  [body(): ring = lax.all_to_all(packed, 'lon', 0, 0, axis_index_groups=Y_RINGS)]
    all_gather x1, blocking collectives: 2.56 us -> 14.2 us  [body(): circle = lax.all_gather(packed, 'lon', axis_index_groups=SIDES)]
where the time goes in v6:
time: 53.2 us; the launch traced here: 53 us
  blocking collectives  37.5 us (70%)
  starting transfers between devices  9.83 us (18%)
  Pallas kernels  5.49 us (10%)
    all_gather x1, blocking collectives, body(): swapped = lax.all_gather(send, 'lon', axis_index_groups=Z_PAIRS)  18.6 us
    all_gather x1, blocking collectives, body(): circle = lax.all_gather(packed, 'lon', axis_index_groups=SIDES)  14.2 us
    ppermute x1, starting transfers between devices, body(): gb = lax.ppermute(eb, 'lat', lat_swaps)  9.83 us
    all_gather x1, blocking collectives, body(): ga = lax.all_gather(ea, ('lat', 'lon'), axis_index_groups=lat_pairs)  4.77 us
    pallas_call x1, Pallas kernels, body(): call(pack_kernel, [((9, rows, 128), F32), ((2, rows, 128), I32)], 60, scr...  1.71 us
    pallas_call x1, Pallas kernels, body(): call(sweep_kernel, [((8, rows, 128), F32)], scratch_shapes=[pltpu.VMEM((8...  1.5 us
    pallas_call x1, Pallas kernels, body(): call(zonal_kernel, [((15, rows, 128), F32), ((12, 8, 128), F32), ((12, 8,...  1.28 us
  transfers between devices with their start and end apart: 1, of which 0 were waited for; matrix products, arithmetic and copies ran while one was open for 0% of the time, Pallas kernels for 0%

profile of v6, /device:TPU:6, one launch (start us, length us, event | category | flops | bytes accessed | tf_op | source)
XLA Modules:
  0.0 53.0 jit_solution(16067383938642061358)
XLA Ops:
  0.0 1.7 %shard_map.73 = (f32[9,24,128]{2,1,0:T(8,128)}, s32[2,24,128]{2,1,0:T(8,128)}) custom-call(f32[8,24,128]{2,1,0:T(8,128)} %bitcast.8, s32[2,24]{1,0:T(2,128)} %refs_1_.1, s32[2,24,128]{2,1,0:T(8,128)} %zc.1, f32[2,24,128]{2,1,0:T(8,128)} %zf.1, s32[2,24,128]{2,1,0:T(8,128)} %mc.1, f32[2,24,128]{2,1,0:T(8,128)} %mf.1, f32[2,24,128]{2,1,0:T(8,128)} %cp.1), custom_call_target="tpu_custom_call" | custom-call | tf_op jit(solution)/shard_map/pallas_call | solution.py:287
  1.7 0.0 copy-start.5
  1.7 14.2 %all-gather = f32[72,24,128]{2,1,0:T(8,128)S(1)} all-gather(f32[9,24,128]{2,1,0:T(8,128)} %get-tuple-element.12), channel_id=2, replica_groups={{0,1,4,5,8,9,12,13},{2,3,6,7,10,11,14,15},{16,17,20,21,24,25,28,29},{18..., dimensions={0}, use_global_device_ids=true | all-gather | bytes 995328 | tf_op jit(solution)/shard_map/all_gather | solution.py:295
  15.9 0.0 copy-done.5
  16.0 1.0 %shard_map.74 = (f32[240,128]{1,0:T(8,128)S(1)}, f32[224,128]{1,0:T(8,128)S(1)}) custom-call(f32[8,9,24,128]{3,2,1,0:T(8,128)S(1)} %bitcast.5, s32[2,24,128]{2,1,0:T(8,128)S(1)} %copy-done.5), custom_call_target="tpu_custom_call" | custom-call | tf_op jit(solution)/shard_map/pallas_call | solution.py:296
  17.0 0.0 copy-start
  17.0 0.0 copy-start.1
  17.0 0.0 copy-start.2
  17.0 0.0 copy-start.3
  17.0 0.0 copy-start.4
  17.0 18.6 %all-gather.1 = f32[448,128]{1,0:T(8,128)S(1)} all-gather(f32[224,128]{1,0:T(8,128)S(1)} %get-tuple-element.15), channel_id=3, replica_groups={{0,2},{1,3},{4,6},{5,7},{8,10},{9,11},{12,14},{13,15},{16,18},{17,19},{..., dimensions={0}, use_global_device_ids=true | all-gather | bytes 344064 | tf_op jit(solution)/shard_map/all_gather | solution.py:299
  35.6 0.0 copy-done
  35.6 0.0 copy-done.1
  35.6 0.0 copy-done.2
  35.6 0.0 copy-done.3
  35.6 0.0 copy-done.4
  35.6 1.3 %shard_map.75 = (f32[15,24,128]{2,1,0:T(8,128)S(1)}, f32[12,8,128]{2,1,0:T(8,128)S(1)}, f32[12,8,128]{2,1,0:T(8,128)S(1)}) custom-call(f32[240,128]{1,0:T(8,128)S(1)} %get-tuple-element.14.keep, f32[2,224,128]{2,1,0:T(8,128)S(1)} %bitcast.6, s32[2,24,128]{2,1,0:T(8,128)S(1)} %copy-done, f32[2,24,128]{2,1,0:T(8,128)S(1)} %copy-done.1, ...), custom_call_target="tpu_custom_call" | custom-call | tf_op jit(solution)/shard_map/pallas_call | solution.py:300
  36.9 9.8 %collective-permute-start = (f32[12,8,128]{2,1,0:T(8,128)S(1)}, f32[12,8,128]{2,1,0:T(8,128)S(1)}, u32[]{:S(2)}, u32[]{:S(2)}) collective-permute-start(f32[12,8,128]{2,1,0:T(8,128)S(1)} %get-tuple-element.18), channel_id=1, source_target_pairs={{16,32},{32,16},{48,64},{64,48},{80,96},{96,80},{112,128},{128,112... | collective-permute-start | bytes 147464 | tf_op jit(solution)/shard_map/ppermute | solution.py:303
  46.7 4.8 %all-gather.2 = f32[24,8,128]{2,1,0:T(8,128)S(1)} all-gather(f32[12,8,128]{2,1,0:T(8,128)S(1)} %get-tuple-element.17), channel_id=4, replica_groups={{0,16},{1,17},{2,18},{3,19},{4,20},{5,21},{6,22},{7,23},{8,24},{9,25},{..., dimensions={0}, use_global_device_ids=true | all-gather | bytes 147456 | tf_op jit(solution)/shard_map/all_gather | solution.py:304
  51.5 0.0 collective-permute-done.gb
  51.5 1.5 %shard_map.76 = f32[8,24,128]{2,1,0:T(8,128)} custom-call(f32[15,24,128]{2,1,0:T(8,128)S(1)} %get-tuple-element.16.main, f32[2,12,8,128]{3,2,1,0:T(8,128)S(1)} %bitcast.7, f32[12,8,128]{2,1,0:T(8,128)S(1)} %collective-permute-done.gb), custom_call_target="tpu_custom_call" | custom-call | tf_op jit(solution)/shard_map/pallas_call | solution.py:305
Async XLA Ops:
  1.7 14.2 %copy-start.5 = (s32[2,24,128]{2,1,0:T(8,128)S(1)}, s32[2,24,128]{2,1,0:T(8,128)}, u32[]{:S(2)}) copy-start(s32[2,24,128]{2,1,0:T(8,128)} %get-tuple-element.13.begin) | copy-start | bytes 73732
  17.0 18.6 %copy-start = (s32[2,24,128]{2,1,0:T(8,128)S(1)}, s32[2,24,128]{2,1,0:T(8,128)}, u32[]{:S(2)}) copy-start(s32[2,24,128]{2,1,0:T(8,128)} %zc.1) | copy-start | bytes 73732
  17.0 18.6 %copy-start.1 = (f32[2,24,128]{2,1,0:T(8,128)S(1)}, f32[2,24,128]{2,1,0:T(8,128)}, u32[]{:S(2)}) copy-start(f32[2,24,128]{2,1,0:T(8,128)} %zf.1) | copy-start | bytes 73732
  17.0 18.6 %copy-start.2 = (s32[2,24,128]{2,1,0:T(8,128)S(1)}, s32[2,24,128]{2,1,0:T(8,128)}, u32[]{:S(2)}) copy-start(s32[2,24,128]{2,1,0:T(8,128)} %mc.1) | copy-start | bytes 73732
  17.0 18.6 %copy-start.3 = (f32[2,24,128]{2,1,0:T(8,128)S(1)}, f32[2,24,128]{2,1,0:T(8,128)}, u32[]{:S(2)}) copy-start(f32[2,24,128]{2,1,0:T(8,128)} %mf.1) | copy-start | bytes 73732
  17.0 18.6 %copy-start.4 = (f32[2,24,128]{2,1,0:T(8,128)S(1)}, f32[2,24,128]{2,1,0:T(8,128)}, u32[]{:S(2)}) copy-start(f32[2,24,128]{2,1,0:T(8,128)} %cp.1) | copy-start | bytes 73732
  36.9 14.6 %collective-permute-start = (f32[12,8,128]{2,1,0:T(8,128)S(1)}, f32[12,8,128]{2,1,0:T(8,128)S(1)}, u32[]{:S(2)}, u32[]{:S(2)}) collective-permute-start(f32[12,8,128]{2,1,0:T(8,128)S(1)} %get-tuple-element.18), channel_id=1, source_target_pairs={{16,32},{32,16},{48,64},{64,48},{80,96},{96,80},{112,128},{128,112... | collective-permute-start | bytes 147464 | tf_op jit(solution)/shard_map/ppermute | solution.py:303

commit v7 on v6

--- a/solution.py
+++ b/solution.py
@@ -1,3 +1,5 @@
+from functools import partial
+
 import jax
 import jax.numpy as jnp
 from jax import lax
@@ -91,43 +93,42 @@
     out[8] = edges
 
 
-def window_kernel(circle, begin, keep, send):
+def windows(circle, begin, l, at, target, fields):
+    me = lax.axis_index("lon")
+    first = begin[l, at : at + 8]
+    spot = (first & 127) + iota((8, 128), 1)
+    index, inside = spot & 127, spot < 128
+    sector = ((me ^ target) + (first >> 7) - (me & 2)) & 15
+    for fl in fields:
+        block = [jnp.zeros((8, 128), F32) for _ in range(3)]
+        for y in range(4):
+            for c in range(2):
+                value = circle[2 * y + c, fl, at : at + 8]
+                for k in range(3):
+                    block[k] = jnp.where(sector == ((4 * y + c - k) & 15), value, block[k])
+        r = [jnp.take_along_axis(v, index, axis=1) for v in block]
+        yield fl, jnp.where(inside, r[0], r[1]), jnp.where(inside, r[1], r[2])
+
+
+def window_kernel(target, circle, begin, out):
     rows = circle.shape[2]
     me = lax.axis_index("lon")
-    core, side = me & 1, me & 2
-    lane = iota((rows, 128), 1)
-    outs = (keep, send)
-    slot = lane // 16
-    tails = [jnp.zeros((rows, 128), F32) for _ in outs]
-    for l in range(2):
-        spot = (begin[l] & 127) + lane
-        index, inside = spot & 127, spot < 128
-        hops = begin[l] >> 7
-        sectors = [((me ^ (2 * t)) + hops) & 15 for t in range(2)]
-        for f in range(4):
-            fl = 2 * f + l
-            block = [[jnp.zeros((rows, 128), F32) for _ in range(3)] for _ in range(2)]
-            for y in range(4):
-                for c in range(2):
-                    s = 4 * y + side + c
-                    value = circle[2 * y + c, fl]
-                    for t in range(2):
-                        for k in range(3):
-                            hit = sectors[t] == ((s - k) & 15)
-                            block[t][k] = jnp.where(hit, value, block[t][k])
-            for t, out in enumerate(outs):
-                r = [jnp.take_along_axis(v, index, axis=1) for v in block[t]]
-                out[rows * fl : rows * fl + rows] = jnp.where(inside, r[0], r[1])
-                tail = jnp.where(inside, r[1], r[2])
-                tail = pltpu.roll(tail, 16 * fl, 1) if fl else tail
-                tails[t] = jnp.where(slot == fl, tail, tails[t])
-    for t, out in enumerate(outs):
-        out[8 * rows : 9 * rows] = tails[t]
-    keep[9 * rows : 10 * rows] = circle[me // 4 * 2 + 1 - core, 8]
-    outer = ((me ^ 2) + jnp.where(core == 0, 15, 1)) & 15
-    outer = circle[outer // 4 * 2 + 1 - core, 8]
-    outer = jnp.where(core == 0, outer, pltpu.roll(outer, 124, 1))
-    send[9 * rows : 9 * rows + 8] = fold(outer)
+    core = me & 1
+    slot = iota((8, 128), 1) // 16
+    for at in range(0, rows, 8):
+        tails = jnp.zeros((8, 128), F32)
+        for l in range(2):
+            for fl, head, tail in windows(circle, begin, l, at, target, range(l, 8, 2)):
+                out[rows * fl + at : rows * fl + at + 8] = head
+                tails = jnp.where(slot == fl, pltpu.roll(tail, 16 * fl, 1) if fl else tail, tails)
+        out[8 * rows + at : 8 * rows + at + 8] = tails
+    if target == 0:
+        out[9 * rows : 10 * rows] = circle[me // 4 * 2 + 1 - core, 8]
+    else:
+        outer = ((me ^ 2) + jnp.where(core == 0, 15, 1)) & 15
+        outer = circle[outer // 4 * 2 + 1 - core, 8]
+        outer = jnp.where(core == 0, outer, pltpu.roll(outer, 124, 1))
+        out[9 * rows : 9 * rows + 8] = fold(outer)
 
 
 def zonal_kernel(keep, swapped, zc, zf, mc, mf, cp, out, ea, eb):
@@ -155,17 +156,20 @@
     slot = lane // 8
     tails = jnp.zeros((rows, 128), F32)
     for l in range(2):
-        cells, frac = [jnp.concatenate(extended(r, i, l), axis=1) for i, r in enumerate((zc, zf))]
-        weights = offset_weights(frac, cells, -2, 2)
+        cells, frac = extended(zc, 0, l), extended(zf, 1, l)
+        near, far = [offset_weights(frac[n], cells[n], -2, 2) for n in range(2)]
         for f in range(4):
             fl = 2 * f + l
             end = pltpu.roll(ends, 128 - 16 * fl, 1) if fl else ends
-            window = jnp.concatenate([both(fl), end], axis=1)
-            total = weights[0] * window
+            head = both(fl)
+            total, tail = near[0] * head, far[0] * end
             for d in range(1, 8):
-                total = total + weights[d] * pltpu.roll(window, 256 - d, 1)
-            out[fl] = total[:, 0:128]
-            tail = pltpu.roll(total[:, 128:256], 8 * fl, 1) if fl else total[:, 128:256]
+                moved = pltpu.roll(end, 128 - d, 1)
+                shifted = jnp.where(lane < 128 - d, pltpu.roll(head, 128 - d, 1), moved)
+                total = total + near[d] * shifted
+                tail = tail + far[d] * moved
+            out[fl] = total
+            tail = pltpu.roll(tail, 8 * fl, 1) if fl else tail
             tails = jnp.where(slot == fl, tail, tails)
     for i, ref in enumerate((mc, mf, cp)):
         for l in range(2):
@@ -293,9 +297,8 @@
         in_specs=[hbm] * 7,
     )(*loads)
     circle = lax.all_gather(packed, "lon", axis_index_groups=SIDES)
-    keep, send = call(
-        window_kernel, [((10 * rows, 128), F32), ((9 * rows + 8, 128), F32)]
-    )(circle, begin)
+    (send,) = call(partial(window_kernel, 2), [((9 * rows + 8, 128), F32)])(circle, begin)
+    (keep,) = call(partial(window_kernel, 0), [((10 * rows, 128), F32)])(circle, begin)
     swapped = lax.all_gather(send, "lon", axis_index_groups=Z_PAIRS)
     main, ea, eb = call(
         zonal_kernel, [((15, rows, 128), F32), ((12, 8, 128), F32), ((12, 8, 128), F32)]

time: 53.2 us -> 52.8 us (level)
  no operation moved by 1% of the time
where the time goes in v7:
time: 52.8 us; the launch traced here: 52.5 us
  blocking collectives  37.5 us (71%)
  starting transfers between devices  9.83 us (19%)
  Pallas kernels  5 us (9%)
    all_gather x1, blocking collectives, body(): swapped = lax.all_gather(send, 'lon', axis_index_groups=Z_PAIRS)  18.6 us
    all_gather x1, blocking collectives, body(): circle = lax.all_gather(packed, 'lon', axis_index_groups=SIDES)  14.2 us
    ppermute x1, starting transfers between devices, body(): gb = lax.ppermute(eb, 'lat', lat_swaps)  9.83 us
    all_gather x1, blocking collectives, body(): ga = lax.all_gather(ea, ('lat', 'lon'), axis_index_groups=lat_pairs)  4.77 us
    pallas_call x1, Pallas kernels, body(): call(pack_kernel, [((9, rows, 128), F32), ((2, rows, 128), I32)], 60, scr...  1.71 us
    pallas_call x1, Pallas kernels, body(): call(sweep_kernel, [((8, rows, 128), F32)], scratch_shapes=[pltpu.VMEM((8...  1.5 us
    pallas_call x1, Pallas kernels, body(): call(zonal_kernel, [((15, rows, 128), F32), ((12, 8, 128), F32), ((12, 8,...  1.23 us
  transfers between devices with their start and end apart: 1, of which 0 were waited for; matrix products, arithmetic and copies ran while one was open for 0% of the time, Pallas kernels for 0%

profile of v7, /device:TPU:6, one launch (start us, length us, event | category | flops | bytes accessed | tf_op | source)
XLA Modules:
  0.0 52.5 jit_solution(7475558944975454119)
XLA Ops:
  0.0 1.7 %shard_map.73 = (f32[9,24,128]{2,1,0:T(8,128)}, s32[2,24,128]{2,1,0:T(8,128)}) custom-call(f32[8,24,128]{2,1,0:T(8,128)} %bitcast.9, s32[2,24]{1,0:T(2,128)} %refs_1_.1, s32[2,24,128]{2,1,0:T(8,128)} %zc.1, f32[2,24,128]{2,1,0:T(8,128)} %zf.1, s32[2,24,128]{2,1,0:T(8,128)} %mc.1, f32[2,24,128]{2,1,0:T(8,128)} %mf.1, f32[2,24,128]{2,1,0:T(8,128)} %cp.1), custom_call_target="tpu_custom_call" | custom-call | tf_op jit(solution)/shard_map/pallas_call | solution.py:291
  1.7 0.0 copy-start.5
  1.7 14.2 %all-gather = f32[72,24,128]{2,1,0:T(8,128)S(1)} all-gather(f32[9,24,128]{2,1,0:T(8,128)} %get-tuple-element.10), channel_id=2, replica_groups={{0,1,4,5,8,9,12,13},{2,3,6,7,10,11,14,15},{16,17,20,21,24,25,28,29},{18..., dimensions={0}, use_global_device_ids=true | all-gather | bytes 995328 | tf_op jit(solution)/shard_map/all_gather | solution.py:299
  16.0 0.0 copy-done.5
  16.0 0.3 shard_map.75
  16.2 0.3 shard_map.74.keep
  16.5 0.0 copy-start
  16.5 0.0 copy-start.1
  16.5 0.0 copy-start.2
  16.5 0.0 copy-start.3
  16.6 0.0 copy-start.4
  16.6 18.6 %all-gather.1 = f32[448,128]{1,0:T(8,128)S(1)} all-gather(f32[224,128]{1,0:T(8,128)S(1)} %shard_map.75), channel_id=3, replica_groups={{0,2},{1,3},{4,6},{5,7},{8,10},{9,11},{12,14},{13,15},{16,18},{17,19},{..., dimensions={0}, use_global_device_ids=true | all-gather | bytes 344064 | tf_op jit(solution)/shard_map/all_gather | solution.py:302
  35.1 0.0 copy-done
  35.1 0.0 copy-done.1
  35.1 0.0 copy-done.2
  35.1 0.0 copy-done.3
  35.2 0.0 copy-done.4
  35.2 1.2 %shard_map.76 = (f32[15,24,128]{2,1,0:T(8,128)S(1)}, f32[12,8,128]{2,1,0:T(8,128)S(1)}, f32[12,8,128]{2,1,0:T(8,128)S(1)}) custom-call(f32[240,128]{1,0:T(8,128)S(1)} %shard_map.74.keep, f32[2,224,128]{2,1,0:T(8,128)S(1)} %bitcast.7, s32[2,24,128]{2,1,0:T(8,128)S(1)} %copy-done, f32[2,24,128]{2,1,0:T(8,128)S(1)} %copy-done.1, s32[2,24,128]{2,1,0:T(8,128)S(1)} %copy-done.2, ...), custom_call_target="tpu_custom_call" | custom-call | tf_op jit(solution)/shard_map/pallas_call | solution.py:303
  36.4 9.8 %collective-permute-start = (f32[12,8,128]{2,1,0:T(8,128)S(1)}, f32[12,8,128]{2,1,0:T(8,128)S(1)}, u32[]{:S(2)}, u32[]{:S(2)}) collective-permute-start(f32[12,8,128]{2,1,0:T(8,128)S(1)} %get-tuple-element.14), channel_id=1, source_target_pairs={{16,32},{32,16},{48,64},{64,48},{80,96},{96,80},{112,128},{128,112... | collective-permute-start | bytes 147464 | tf_op jit(solution)/shard_map/ppermute | solution.py:306
  46.2 4.8 %all-gather.2 = f32[24,8,128]{2,1,0:T(8,128)S(1)} all-gather(f32[12,8,128]{2,1,0:T(8,128)S(1)} %get-tuple-element.13), channel_id=4, replica_groups={{0,16},{1,17},{2,18},{3,19},{4,20},{5,21},{6,22},{7,23},{8,24},{9,25},{..., dimensions={0}, use_global_device_ids=true | all-gather | bytes 147456 | tf_op jit(solution)/shard_map/all_gather | solution.py:307
  51.0 0.0 collective-permute-done.gb
  51.0 1.5 %shard_map.77 = f32[8,24,128]{2,1,0:T(8,128)} custom-call(f32[15,24,128]{2,1,0:T(8,128)S(1)} %get-tuple-element.12.main, f32[2,12,8,128]{3,2,1,0:T(8,128)S(1)} %bitcast.8, f32[12,8,128]{2,1,0:T(8,128)S(1)} %collective-permute-done.gb), custom_call_target="tpu_custom_call" | custom-call | tf_op jit(solution)/shard_map/pallas_call | solution.py:308
Async XLA Ops:
  1.7 14.2 %copy-start.5 = (s32[2,24,128]{2,1,0:T(8,128)S(1)}, s32[2,24,128]{2,1,0:T(8,128)}, u32[]{:S(2)}) copy-start(s32[2,24,128]{2,1,0:T(8,128)} %get-tuple-element.11.begin) | copy-start | bytes 73732
  16.5 18.6 %copy-start = (s32[2,24,128]{2,1,0:T(8,128)S(1)}, s32[2,24,128]{2,1,0:T(8,128)}, u32[]{:S(2)}) copy-start(s32[2,24,128]{2,1,0:T(8,128)} %zc.1) | copy-start | bytes 73732
  16.5 18.6 %copy-start.1 = (f32[2,24,128]{2,1,0:T(8,128)S(1)}, f32[2,24,128]{2,1,0:T(8,128)}, u32[]{:S(2)}) copy-start(f32[2,24,128]{2,1,0:T(8,128)} %zf.1) | copy-start | bytes 73732
  16.5 18.6 %copy-start.2 = (s32[2,24,128]{2,1,0:T(8,128)S(1)}, s32[2,24,128]{2,1,0:T(8,128)}, u32[]{:S(2)}) copy-start(s32[2,24,128]{2,1,0:T(8,128)} %mc.1) | copy-start | bytes 73732
  16.5 18.6 %copy-start.3 = (f32[2,24,128]{2,1,0:T(8,128)S(1)}, f32[2,24,128]{2,1,0:T(8,128)}, u32[]{:S(2)}) copy-start(f32[2,24,128]{2,1,0:T(8,128)} %mf.1) | copy-start | bytes 73732
  16.6 18.6 %copy-start.4 = (f32[2,24,128]{2,1,0:T(8,128)S(1)}, f32[2,24,128]{2,1,0:T(8,128)}, u32[]{:S(2)}) copy-start(f32[2,24,128]{2,1,0:T(8,128)} %cp.1) | copy-start | bytes 73732
  36.4 14.6 %collective-permute-start = (f32[12,8,128]{2,1,0:T(8,128)S(1)}, f32[12,8,128]{2,1,0:T(8,128)S(1)}, u32[]{:S(2)}, u32[]{:S(2)}) collective-permute-start(f32[12,8,128]{2,1,0:T(8,128)S(1)} %get-tuple-element.14), channel_id=1, source_target_pairs={{16,32},{32,16},{48,64},{64,48},{80,96},{96,80},{112,128},{128,112... | collective-permute-start | bytes 147464 | tf_op jit(solution)/shard_map/ppermute | solution.py:306

commit v8 on v7

--- a/solution.py
+++ b/solution.py
@@ -291,11 +291,11 @@
     packed, begin = call(
         pack_kernel,
         [((9, rows, 128), F32), ((2, rows, 128), I32)],
-        60,
+        32,
         scratch_shapes=[pltpu.VMEM(v.shape, v.dtype) for v in loads]
         + [pltpu.SemaphoreType.DMA((7,))],
         in_specs=[hbm] * 7,
-    )(*loads)
+    )(*[pltpu.with_memory_space_constraint(v, pltpu.HBM) for v in loads])
     circle = lax.all_gather(packed, "lon", axis_index_groups=SIDES)
     (send,) = call(partial(window_kernel, 2), [((9 * rows + 8, 128), F32)])(circle, begin)
     (keep,) = call(partial(window_kernel, 0), [((10 * rows, 128), F32)])(circle, begin)

time: 52.8 us -> 51.8 us (0.981)
  Pallas kernels: 5 us -> 4.34 us
    pallas_call x1, Pallas kernels: 1.71 us -> 1.06 us  [body(): call(pack_kernel, [((9, rows, 128), F32), ((2, rows, 128), I32)], 32, scr...]
where the time goes in v8:
time: 51.8 us; the launch traced here: 51.6 us
  blocking collectives  37.3 us (72%)
  starting transfers between devices  9.83 us (19%)
  Pallas kernels  4.34 us (8%)
    all_gather x1, blocking collectives, body(): swapped = lax.all_gather(send, 'lon', axis_index_groups=Z_PAIRS)  18.6 us
    all_gather x1, blocking collectives, body(): circle = lax.all_gather(packed, 'lon', axis_index_groups=SIDES)  14 us
    ppermute x1, starting transfers between devices, body(): gb = lax.ppermute(eb, 'lat', lat_swaps)  9.83 us
    all_gather x1, blocking collectives, body(): ga = lax.all_gather(ea, ('lat', 'lon'), axis_index_groups=lat_pairs)  4.77 us
    pallas_call x1, Pallas kernels, body(): call(sweep_kernel, [((8, rows, 128), F32)], scratch_shapes=[pltpu.VMEM((8...  1.5 us
    pallas_call x1, Pallas kernels, body(): call(zonal_kernel, [((15, rows, 128), F32), ((12, 8, 128), F32), ((12, 8,...  1.23 us
    pallas_call x1, Pallas kernels, body(): call(pack_kernel, [((9, rows, 128), F32), ((2, rows, 128), I32)], 32, scr...  1.06 us
  transfers between devices with their start and end apart: 1, of which 0 were waited for; matrix products, arithmetic and copies ran while one was open for 0% of the time, Pallas kernels for 0%

profile of v8, /device:TPU:6, one launch (start us, length us, event | category | flops | bytes accessed | tf_op | source)
XLA Modules:
  0.0 51.6 jit_solution(12900518533323851007)
XLA Ops:
  0.0 1.1 %shard_map.73 = (f32[9,24,128]{2,1,0:T(8,128)S(1)}, s32[2,24,128]{2,1,0:T(8,128)S(1)}) custom-call(f32[8,24,128]{2,1,0:T(8,128)} %bitcast.9, s32[2,24]{1,0:T(2,128)} %refs_1_.1, s32[2,24,128]{2,1,0:T(8,128)} %zc.1, f32[2,24,128]{2,1,0:T(8,128)} %zf.1, s32[2,24,128]{2,1,0:T(8,128)} %mc.1, f32[2,24,128]{2,1,0:T(8,128)} %mf.1, f32[2,24,128]{2,1,0:T(8,128)} %cp.1), custom_call_target="tpu_custom_call" | custom-call | tf_op jit(solution)/shard_map/pallas_call | solution.py:291
  1.1 14.0 %all-gather = f32[72,24,128]{2,1,0:T(8,128)S(1)} all-gather(f32[9,24,128]{2,1,0:T(8,128)S(1)} %get-tuple-element.10), channel_id=2, replica_groups={{0,1,4,5,8,9,12,13},{2,3,6,7,10,11,14,15},{16,17,20,21,24,25,28,29},{18..., dimensions={0}, use_global_device_ids=true | all-gather | bytes 995328 | tf_op jit(solution)/shard_map/all_gather | solution.py:299
  15.1 0.3 shard_map.75
  15.4 0.3 shard_map.74.keep
  15.6 0.0 copy-start
  15.6 0.0 copy-start.1
  15.7 0.0 copy-start.2
  15.7 0.0 copy-start.3
  15.7 0.0 copy-start.4
  15.7 18.6 %all-gather.1 = f32[448,128]{1,0:T(8,128)S(1)} all-gather(f32[224,128]{1,0:T(8,128)S(1)} %shard_map.75), channel_id=3, replica_groups={{0,2},{1,3},{4,6},{5,7},{8,10},{9,11},{12,14},{13,15},{16,18},{17,19},{..., dimensions={0}, use_global_device_ids=true | all-gather | bytes 344064 | tf_op jit(solution)/shard_map/all_gather | solution.py:302
  34.2 0.0 copy-done
  34.3 0.0 copy-done.1
  34.3 0.0 copy-done.2
  34.3 0.0 copy-done.3
  34.3 0.0 copy-done.4
  34.3 1.2 %shard_map.76 = (f32[15,24,128]{2,1,0:T(8,128)S(1)}, f32[12,8,128]{2,1,0:T(8,128)S(1)}, f32[12,8,128]{2,1,0:T(8,128)S(1)}) custom-call(f32[240,128]{1,0:T(8,128)S(1)} %shard_map.74.keep, f32[2,224,128]{2,1,0:T(8,128)S(1)} %bitcast.7, s32[2,24,128]{2,1,0:T(8,128)S(1)} %copy-done, f32[2,24,128]{2,1,0:T(8,128)S(1)} %copy-done.1, s32[2,24,128]{2,1,0:T(8,128)S(1)} %copy-done.2, ...), custom_call_target="tpu_custom_call" | custom-call | tf_op jit(solution)/shard_map/pallas_call | solution.py:303
  35.5 9.8 %collective-permute-start = (f32[12,8,128]{2,1,0:T(8,128)S(1)}, f32[12,8,128]{2,1,0:T(8,128)S(1)}, u32[]{:S(2)}, u32[]{:S(2)}) collective-permute-start(f32[12,8,128]{2,1,0:T(8,128)S(1)} %get-tuple-element.14), channel_id=1, source_target_pairs={{16,32},{32,16},{48,64},{64,48},{80,96},{96,80},{112,128},{128,112... | collective-permute-start | bytes 147464 | tf_op jit(solution)/shard_map/ppermute | solution.py:306
  45.4 4.8 %all-gather.2 = f32[24,8,128]{2,1,0:T(8,128)S(1)} all-gather(f32[12,8,128]{2,1,0:T(8,128)S(1)} %get-tuple-element.13), channel_id=4, replica_groups={{0,16},{1,17},{2,18},{3,19},{4,20},{5,21},{6,22},{7,23},{8,24},{9,25},{..., dimensions={0}, use_global_device_ids=true | all-gather | bytes 147456 | tf_op jit(solution)/shard_map/all_gather | solution.py:307
  50.1 0.0 collective-permute-done.gb
  50.1 1.5 %shard_map.77 = f32[8,24,128]{2,1,0:T(8,128)} custom-call(f32[15,24,128]{2,1,0:T(8,128)S(1)} %get-tuple-element.12.main, f32[2,12,8,128]{3,2,1,0:T(8,128)S(1)} %bitcast.8, f32[12,8,128]{2,1,0:T(8,128)S(1)} %collective-permute-done.gb), custom_call_target="tpu_custom_call" | custom-call | tf_op jit(solution)/shard_map/pallas_call | solution.py:308
Async XLA Ops:
  15.6 18.6 %copy-start = (s32[2,24,128]{2,1,0:T(8,128)S(1)}, s32[2,24,128]{2,1,0:T(8,128)}, u32[]{:S(2)}) copy-start(s32[2,24,128]{2,1,0:T(8,128)} %zc.1) | copy-start | bytes 73732
  15.6 18.6 %copy-start.1 = (f32[2,24,128]{2,1,0:T(8,128)S(1)}, f32[2,24,128]{2,1,0:T(8,128)}, u32[]{:S(2)}) copy-start(f32[2,24,128]{2,1,0:T(8,128)} %zf.1) | copy-start | bytes 73732
  15.7 18.6 %copy-start.2 = (s32[2,24,128]{2,1,0:T(8,128)S(1)}, s32[2,24,128]{2,1,0:T(8,128)}, u32[]{:S(2)}) copy-start(s32[2,24,128]{2,1,0:T(8,128)} %mc.1) | copy-start | bytes 73732
  15.7 18.6 %copy-start.3 = (f32[2,24,128]{2,1,0:T(8,128)S(1)}, f32[2,24,128]{2,1,0:T(8,128)}, u32[]{:S(2)}) copy-start(f32[2,24,128]{2,1,0:T(8,128)} %mf.1) | copy-start | bytes 73732
  15.7 18.6 %copy-start.4 = (f32[2,24,128]{2,1,0:T(8,128)S(1)}, f32[2,24,128]{2,1,0:T(8,128)}, u32[]{:S(2)}) copy-start(f32[2,24,128]{2,1,0:T(8,128)} %cp.1) | copy-start | bytes 73732
  35.5 14.6 %collective-permute-start = (f32[12,8,128]{2,1,0:T(8,128)S(1)}, f32[12,8,128]{2,1,0:T(8,128)S(1)}, u32[]{:S(2)}, u32[]{:S(2)}) collective-permute-start(f32[12,8,128]{2,1,0:T(8,128)S(1)} %get-tuple-element.14), channel_id=1, source_target_pairs={{16,32},{32,16},{48,64},{64,48},{80,96},{96,80},{112,128},{128,112... | collective-permute-start | bytes 147464 | tf_op jit(solution)/shard_map/ppermute | solution.py:306

commit v9 on v8

--- a/solution.py
+++ b/solution.py
@@ -158,19 +158,21 @@
     for l in range(2):
         cells, frac = extended(zc, 0, l), extended(zf, 1, l)
         near, far = [offset_weights(frac[n], cells[n], -2, 2) for n in range(2)]
-        for f in range(4):
-            fl = 2 * f + l
-            end = pltpu.roll(ends, 128 - 16 * fl, 1) if fl else ends
-            head = both(fl)
-            total, tail = near[0] * head, far[0] * end
-            for d in range(1, 8):
-                moved = pltpu.roll(end, 128 - d, 1)
-                shifted = jnp.where(lane < 128 - d, pltpu.roll(head, 128 - d, 1), moved)
-                total = total + near[d] * shifted
-                tail = tail + far[d] * moved
-            out[fl] = total
-            tail = pltpu.roll(tail, 8 * fl, 1) if fl else tail
-            tails = jnp.where(slot == fl, tail, tails)
+        fields = range(l, 8, 2)
+        heads = {fl: both(fl) for fl in fields}
+        rests = {fl: pltpu.roll(ends, 128 - 16 * fl, 1) if fl else ends for fl in fields}
+        total = {fl: near[0] * heads[fl] for fl in fields}
+        tail = {fl: far[0] * rests[fl] for fl in fields}
+        for d in range(1, 8):
+            for fl in fields:
+                moved = pltpu.roll(rests[fl], 128 - d, 1)
+                shifted = jnp.where(lane < 128 - d, pltpu.roll(heads[fl], 128 - d, 1), moved)
+                total[fl] = total[fl] + near[d] * shifted
+                tail[fl] = tail[fl] + far[d] * moved
+        for fl in fields:
+            out[fl] = total[fl]
+            end = pltpu.roll(tail[fl], 8 * fl, 1) if fl else tail[fl]
+            tails = jnp.where(slot == fl, end, tails)
     for i, ref in enumerate((mc, mf, cp)):
         for l in range(2):
             a = 8 + 2 * i + l
@@ -213,13 +215,14 @@
         inverse = jnp.where(outside, 0.0, 1.0 / (1.0 + 4.0 * coupling))
         return weights, inverse, coupling * inverse
 
-    def source_of(value, weights):
-        value = jnp.where(beyond, 0.0, value)
-        source = jnp.zeros((total, 128), F32)
+    def source_of(values, weights):
+        values = [jnp.where(beyond, 0.0, v) for v in values]
+        sources = [jnp.zeros((total, 128), F32) for _ in values]
         for i in range(6):
-            moved = pltpu.roll(value, rows + 16 - (2 + i), 0)[:total]
-            source = source + weights[i] * moved
-        return jnp.where(outside, 0.0, source)
+            for n, value in enumerate(values):
+                moved = pltpu.roll(value, rows + 16 - (2 + i), 0)[:total]
+                sources[n] = sources[n] + weights[i] * moved
+        return [jnp.where(outside, 0.0, v) for v in sources]
 
     packs = [[unpack_rows(v) for v in pick(9 + i)] for i in range(3)]
     tails = joined(pick(8), main[8])
@@ -230,7 +233,7 @@
         v = jnp.where(lane < 16, v, pltpu.roll(v, 16, 1))
         group.append(jnp.where(lane < 32, v, pltpu.roll(v, 32, 1)))
     weights, inverse, tail_factor = prepare(*group)
-    tail = source_of(tails, weights)
+    (tail,) = source_of([tails], weights)
     tail_source = tail * inverse
     phi, source, factor = [None] * 8, [None] * 8, [None] * 8
     for l in range(2):
@@ -239,31 +242,31 @@
             own = joined([v[l] for v in packs[i]], main[9 + 2 * i + l])
             coefs.append(pltpu.roll(own, rows + 12, 0)[:total])
         weights, inverse, level_factor = prepare(*coefs)
-        for f in range(4):
-            fl = 2 * f + l
-            value = source_of(joined(pick(fl), main[fl]), weights)
+        fields = range(l, 8, 2)
+        values = source_of([joined(pick(fl), main[fl]) for fl in fields], weights)
+        for fl, value in zip(fields, values):
             phi[fl] = rotated(value, 8 * fl)
             source[fl] = rotated(value * inverse, 8 * fl)
             factor[fl] = rotated(level_factor, 8 * fl)
+    copies = []
     for sweep in range(SWEEPS):
-        old_tail = tail
         tail_left, tail_right = pltpu.roll(tail, 1, 1), pltpu.roll(tail, 127, 1)
+        lefts = [pltpu.roll(v, 1, 1) for v in phi]
+        for fl in range(8):
+            tail_left = jnp.where(lane == 8 * fl, lefts[fl], tail_left)
+        beside = pltpu.roll(tail, 1, 0) + pltpu.roll(tail, total - 1, 0)
+        tail = tail_source + tail_factor * (beside + tail_left + tail_right)
         for fl in range(8):
             old = phi[fl]
-            left = pltpu.roll(old, 1, 1)
-            tail_left = jnp.where(lane == 8 * fl, left, tail_left)
             right = jnp.where(lane == (8 * fl - 1) % 128, tail_right, pltpu.roll(old, 127, 1))
-            beside = pltpu.roll(old, 1, 0) + pltpu.roll(old, total - 1, 0) + left + right
+            beside = pltpu.roll(old, 1, 0) + pltpu.roll(old, total - 1, 0) + lefts[fl] + right
             phi[fl] = source[fl] + factor[fl] * beside
-        beside = pltpu.roll(old_tail, 1, 0) + pltpu.roll(old_tail, total - 1, 0)
-        tail = tail_source + tail_factor * (beside + tail_left + tail_right)
-    copies = []
-    for fl in range(8):
-        whole = jnp.where((lane >= 8 * fl) & (lane < 8 * fl + 4), tail, phi[fl])
-        whole = rotated(whole, -4 - 8 * fl)
-        done[fl] = pltpu.roll(whole, total - 4, 0)[:rows]
-        copies.append(pltpu.make_async_copy(done.at[fl], result.at[fl], sems.at[fl]))
-        copies[-1].start()
+            if sweep == SWEEPS - 1:
+                whole = jnp.where((lane >= 8 * fl) & (lane < 8 * fl + 4), tail, phi[fl])
+                whole = rotated(whole, -4 - 8 * fl)
+                done[fl] = pltpu.roll(whole, total - 4, 0)[:rows]
+                copies.append(pltpu.make_async_copy(done.at[fl], result.at[fl], sems.at[fl]))
+                copies[-1].start()
     for copy in copies:
         copy.wait()
 

time: 51.8 us -> 51.4 us (level)
  no operation moved by 1% of the time
where the time goes in v9:
time: 51.4 us; the launch traced here: 51.1 us
  blocking collectives  37.3 us (73%)
  starting transfers between devices  9.83 us (19%)
  Pallas kernels  3.86 us (8%)
    all_gather x1, blocking collectives, body(): swapped = lax.all_gather(send, 'lon', axis_index_groups=Z_PAIRS)  18.6 us
    all_gather x1, blocking collectives, body(): circle = lax.all_gather(packed, 'lon', axis_index_groups=SIDES)  14 us
    ppermute x1, starting transfers between devices, body(): gb = lax.ppermute(eb, 'lat', lat_swaps)  9.83 us
    all_gather x1, blocking collectives, body(): ga = lax.all_gather(ea, ('lat', 'lon'), axis_index_groups=lat_pairs)  4.77 us
    pallas_call x1, Pallas kernels, body(): call(sweep_kernel, [((8, rows, 128), F32)], scratch_shapes=[pltpu.VMEM((8...  1.51 us
    pallas_call x1, Pallas kernels, body(): call(pack_kernel, [((9, rows, 128), F32), ((2, rows, 128), I32)], 32, scr...  1.06 us
  transfers between devices with their start and end apart: 1, of which 0 were waited for; matrix products, arithmetic and copies ran while one was open for 0% of the time, Pallas kernels for 0%

profile of v9, /device:TPU:6, one launch (start us, length us, event | category | flops | bytes accessed | tf_op | source)
XLA Modules:
  0.0 51.1 jit_solution(7293364676449550843)
XLA Ops:
  0.0 1.1 %shard_map.73 = (f32[9,24,128]{2,1,0:T(8,128)S(1)}, s32[2,24,128]{2,1,0:T(8,128)S(1)}) custom-call(f32[8,24,128]{2,1,0:T(8,128)} %bitcast.9, s32[2,24]{1,0:T(2,128)} %refs_1_.1, s32[2,24,128]{2,1,0:T(8,128)} %zc.1, f32[2,24,128]{2,1,0:T(8,128)} %zf.1, s32[2,24,128]{2,1,0:T(8,128)} %mc.1, f32[2,24,128]{2,1,0:T(8,128)} %mf.1, f32[2,24,128]{2,1,0:T(8,128)} %cp.1), custom_call_target="tpu_custom_call" | custom-call | tf_op jit(solution)/shard_map/pallas_call | solution.py:294
  1.1 14.0 %all-gather = f32[72,24,128]{2,1,0:T(8,128)S(1)} all-gather(f32[9,24,128]{2,1,0:T(8,128)S(1)} %get-tuple-element.10), channel_id=2, replica_groups={{0,1,4,5,8,9,12,13},{2,3,6,7,10,11,14,15},{16,17,20,21,24,25,28,29},{18..., dimensions={0}, use_global_device_ids=true | all-gather | bytes 995328 | tf_op jit(solution)/shard_map/all_gather | solution.py:302
  15.1 0.3 shard_map.75
  15.4 0.3 shard_map.74.keep
  15.6 0.0 copy-start
  15.6 0.0 copy-start.1
  15.7 0.0 copy-start.2
  15.7 0.0 copy-start.3
  15.7 0.0 copy-start.4
  15.7 18.6 %all-gather.1 = f32[448,128]{1,0:T(8,128)S(1)} all-gather(f32[224,128]{1,0:T(8,128)S(1)} %shard_map.75), channel_id=3, replica_groups={{0,2},{1,3},{4,6},{5,7},{8,10},{9,11},{12,14},{13,15},{16,18},{17,19},{..., dimensions={0}, use_global_device_ids=true | all-gather | bytes 344064 | tf_op jit(solution)/shard_map/all_gather | solution.py:305
  34.2 0.0 copy-done
  34.3 0.0 copy-done.1
  34.3 0.0 copy-done.2
  34.3 0.0 copy-done.3
  34.3 0.0 copy-done.4
  34.3 0.7 %shard_map.76 = (f32[15,24,128]{2,1,0:T(8,128)S(1)}, f32[12,8,128]{2,1,0:T(8,128)S(1)}, f32[12,8,128]{2,1,0:T(8,128)S(1)}) custom-call(f32[240,128]{1,0:T(8,128)S(1)} %shard_map.74.keep, f32[2,224,128]{2,1,0:T(8,128)S(1)} %bitcast.7, s32[2,24,128]{2,1,0:T(8,128)S(1)} %copy-done, f32[2,24,128]{2,1,0:T(8,128)S(1)} %copy-done.1, s32[2,24,128]{2,1,0:T(8,128)S(1)} %copy-done.2, ...), custom_call_target="tpu_custom_call" | custom-call | tf_op jit(solution)/shard_map/pallas_call | solution.py:306
  35.0 9.8 %collective-permute-start = (f32[12,8,128]{2,1,0:T(8,128)S(1)}, f32[12,8,128]{2,1,0:T(8,128)S(1)}, u32[]{:S(2)}, u32[]{:S(2)}) collective-permute-start(f32[12,8,128]{2,1,0:T(8,128)S(1)} %get-tuple-element.14), channel_id=1, source_target_pairs={{16,32},{32,16},{48,64},{64,48},{80,96},{96,80},{112,128},{128,112... | collective-permute-start | bytes 147464 | tf_op jit(solution)/shard_map/ppermute | solution.py:309
  44.9 4.8 %all-gather.2 = f32[24,8,128]{2,1,0:T(8,128)S(1)} all-gather(f32[12,8,128]{2,1,0:T(8,128)S(1)} %get-tuple-element.13), channel_id=4, replica_groups={{0,16},{1,17},{2,18},{3,19},{4,20},{5,21},{6,22},{7,23},{8,24},{9,25},{..., dimensions={0}, use_global_device_ids=true | all-gather | bytes 147456 | tf_op jit(solution)/shard_map/all_gather | solution.py:310
  49.6 0.0 collective-permute-done.gb
  49.6 1.5 %shard_map.77 = f32[8,24,128]{2,1,0:T(8,128)} custom-call(f32[15,24,128]{2,1,0:T(8,128)S(1)} %get-tuple-element.12.main, f32[2,12,8,128]{3,2,1,0:T(8,128)S(1)} %bitcast.8, f32[12,8,128]{2,1,0:T(8,128)S(1)} %collective-permute-done.gb), custom_call_target="tpu_custom_call" | custom-call | tf_op jit(solution)/shard_map/pallas_call | solution.py:311
Async XLA Ops:
  15.6 18.6 %copy-start = (s32[2,24,128]{2,1,0:T(8,128)S(1)}, s32[2,24,128]{2,1,0:T(8,128)}, u32[]{:S(2)}) copy-start(s32[2,24,128]{2,1,0:T(8,128)} %zc.1) | copy-start | bytes 73732
  15.6 18.6 %copy-start.1 = (f32[2,24,128]{2,1,0:T(8,128)S(1)}, f32[2,24,128]{2,1,0:T(8,128)}, u32[]{:S(2)}) copy-start(f32[2,24,128]{2,1,0:T(8,128)} %zf.1) | copy-start | bytes 73732
  15.7 18.6 %copy-start.2 = (s32[2,24,128]{2,1,0:T(8,128)S(1)}, s32[2,24,128]{2,1,0:T(8,128)}, u32[]{:S(2)}) copy-start(s32[2,24,128]{2,1,0:T(8,128)} %mc.1) | copy-start | bytes 73732
  15.7 18.6 %copy-start.3 = (f32[2,24,128]{2,1,0:T(8,128)S(1)}, f32[2,24,128]{2,1,0:T(8,128)}, u32[]{:S(2)}) copy-start(f32[2,24,128]{2,1,0:T(8,128)} %mf.1) | copy-start | bytes 73732
  15.7 18.6 %copy-start.4 = (f32[2,24,128]{2,1,0:T(8,128)S(1)}, f32[2,24,128]{2,1,0:T(8,128)}, u32[]{:S(2)}) copy-start(f32[2,24,128]{2,1,0:T(8,128)} %cp.1) | copy-start | bytes 73732
  35.0 14.6 %collective-permute-start = (f32[12,8,128]{2,1,0:T(8,128)S(1)}, f32[12,8,128]{2,1,0:T(8,128)S(1)}, u32[]{:S(2)}, u32[]{:S(2)}) collective-permute-start(f32[12,8,128]{2,1,0:T(8,128)S(1)} %get-tuple-element.14), channel_id=1, source_target_pairs={{16,32},{32,16},{48,64},{64,48},{80,96},{96,80},{112,128},{128,112... | collective-permute-start | bytes 147464 | tf_op jit(solution)/shard_map/ppermute | solution.py:309

commit v10 on v9

--- a/solution.py
+++ b/solution.py
@@ -189,7 +189,7 @@
             e[9 + i] = pack_rows(out[9 + 2 * i, take], out[10 + 2 * i, take], top)
 
 
-def sweep_kernel(main, ga, gb, result, done, sems):
+def source_kernel(main, ga, gb, now, fixed, scale):
     rows = main.shape[1]
     total = rows + 8
     band, bands = lax.axis_index("lat"), lax.axis_size("lat")
@@ -248,7 +248,25 @@
             phi[fl] = rotated(value, 8 * fl)
             source[fl] = rotated(value * inverse, 8 * fl)
             factor[fl] = rotated(level_factor, 8 * fl)
-    copies = []
+    for n, v in enumerate(phi + [tail]):
+        now[n] = v
+    for n, v in enumerate(source + [tail_source]):
+        fixed[n] = v
+    for n, v in enumerate(factor + [tail_factor]):
+        scale[n] = v
+
+
+def sweep_kernel(now, fixed, scale, result):
+    total = now.shape[1]
+    rows = total - 8
+    lane = iota((total, 128), 1)
+    phi, tail = [now[fl] for fl in range(8)], now[8]
+    source, tail_source = [fixed[fl] for fl in range(8)], fixed[8]
+    factor, tail_factor = [scale[fl] for fl in range(8)], scale[8]
+
+    def rotated(x, lanes):
+        return pltpu.roll(x, lanes % 128, 1) if lanes % 128 else x
+
     for sweep in range(SWEEPS):
         tail_left, tail_right = pltpu.roll(tail, 1, 1), pltpu.roll(tail, 127, 1)
         lefts = [pltpu.roll(v, 1, 1) for v in phi]
@@ -264,11 +282,7 @@
             if sweep == SWEEPS - 1:
                 whole = jnp.where((lane >= 8 * fl) & (lane < 8 * fl + 4), tail, phi[fl])
                 whole = rotated(whole, -4 - 8 * fl)
-                done[fl] = pltpu.roll(whole, total - 4, 0)[:rows]
-                copies.append(pltpu.make_async_copy(done.at[fl], result.at[fl], sems.at[fl]))
-                copies[-1].start()
-    for copy in copies:
-        copy.wait()
+                result[fl] = pltpu.roll(whole, total - 4, 0)[:rows]
 
 
 def call(kernel, shapes, limit=32, **more):
@@ -308,12 +322,8 @@
     )(keep, swapped, *coefs)
     gb = lax.ppermute(eb, "lat", lat_swaps)
     ga = lax.all_gather(ea, ("lat", "lon"), axis_index_groups=lat_pairs)
-    (advanced,) = call(
-        sweep_kernel,
-        [((8, rows, 128), F32)],
-        scratch_shapes=[pltpu.VMEM((8, rows, 128), F32), pltpu.SemaphoreType.DMA((8,))],
-        out_specs=[hbm],
-    )(main, ga, gb)
+    prepared = call(source_kernel, [((9, rows + 8, 128), F32)] * 3)(main, ga, gb)
+    (advanced,) = call(sweep_kernel, [((8, rows, 128), F32)])(*prepared)
     return advanced.reshape(state.shape)
 
 

time: 51.4 us -> 51.4 us (level)
    pallas_call x1 -> x2, Pallas kernels: 1.51 us -> 1.52 us  [the longest x1 1.2 us: body(): advanced, = call(sweep_kernel, [((8, rows, 128), F32)])(*prepared)]
where the time goes in v10:
time: 51.4 us; the launch traced here: 51.2 us
  blocking collectives  37.3 us (73%)
  starting transfers between devices  9.83 us (19%)
  Pallas kernels  3.87 us (8%)
    all_gather x1, blocking collectives, body(): swapped = lax.all_gather(send, 'lon', axis_index_groups=Z_PAIRS)  18.6 us
    all_gather x1, blocking collectives, body(): circle = lax.all_gather(packed, 'lon', axis_index_groups=SIDES)  14 us
    ppermute x1, starting transfers between devices, body(): gb = lax.ppermute(eb, 'lat', lat_swaps)  9.83 us
    all_gather x1, blocking collectives, body(): ga = lax.all_gather(ea, ('lat', 'lon'), axis_index_groups=lat_pairs)  4.77 us
    pallas_call x1, Pallas kernels, body(): advanced, = call(sweep_kernel, [((8, rows, 128), F32)])(*prepared)  1.2 us
    pallas_call x1, Pallas kernels, body(): call(pack_kernel, [((9, rows, 128), F32), ((2, rows, 128), I32)], 32, scr...  1.06 us
  transfers between devices with their start and end apart: 1, of which 0 were waited for; matrix products, arithmetic and copies ran while one was open for 0% of the time, Pallas kernels for 0%

profile of v10, /device:TPU:6, one launch (start us, length us, event | category | flops | bytes accessed | tf_op | source)
XLA Modules:
  0.0 51.2 jit_solution(6812587928409779145)
XLA Ops:
  0.0 1.1 %shard_map.73 = (f32[9,24,128]{2,1,0:T(8,128)S(1)}, s32[2,24,128]{2,1,0:T(8,128)S(1)}) custom-call(f32[8,24,128]{2,1,0:T(8,128)} %bitcast.9, s32[2,24]{1,0:T(2,128)} %refs_1_.1, s32[2,24,128]{2,1,0:T(8,128)} %zc.1, f32[2,24,128]{2,1,0:T(8,128)} %zf.1, s32[2,24,128]{2,1,0:T(8,128)} %mc.1, f32[2,24,128]{2,1,0:T(8,128)} %mf.1, f32[2,24,128]{2,1,0:T(8,128)} %cp.1), custom_call_target="tpu_custom_call" | custom-call | tf_op jit(solution)/shard_map/pallas_call | solution.py:308
  1.1 14.0 %all-gather = f32[72,24,128]{2,1,0:T(8,128)S(1)} all-gather(f32[9,24,128]{2,1,0:T(8,128)S(1)} %get-tuple-element.13), channel_id=2, replica_groups={{0,1,4,5,8,9,12,13},{2,3,6,7,10,11,14,15},{16,17,20,21,24,25,28,29},{18..., dimensions={0}, use_global_device_ids=true | all-gather | bytes 995328 | tf_op jit(solution)/shard_map/all_gather | solution.py:316
  15.1 0.3 shard_map.75
  15.4 0.3 shard_map.74.keep
  15.6 0.0 copy-start
  15.6 0.0 copy-start.1
  15.7 0.0 copy-start.2
  15.7 0.0 copy-start.3
  15.7 0.0 copy-start.4
  15.7 18.6 %all-gather.1 = f32[448,128]{1,0:T(8,128)S(1)} all-gather(f32[224,128]{1,0:T(8,128)S(1)} %shard_map.75), channel_id=3, replica_groups={{0,2},{1,3},{4,6},{5,7},{8,10},{9,11},{12,14},{13,15},{16,18},{17,19},{..., dimensions={0}, use_global_device_ids=true | all-gather | bytes 344064 | tf_op jit(solution)/shard_map/all_gather | solution.py:319
  34.2 0.0 copy-done
  34.3 0.0 copy-done.1
  34.3 0.0 copy-done.2
  34.3 0.0 copy-done.3
  34.3 0.0 copy-done.4
  34.3 0.7 %shard_map.76 = (f32[15,24,128]{2,1,0:T(8,128)S(1)}, f32[12,8,128]{2,1,0:T(8,128)S(1)}, f32[12,8,128]{2,1,0:T(8,128)S(1)}) custom-call(f32[240,128]{1,0:T(8,128)S(1)} %shard_map.74.keep, f32[2,224,128]{2,1,0:T(8,128)S(1)} %bitcast.7, s32[2,24,128]{2,1,0:T(8,128)S(1)} %copy-done, f32[2,24,128]{2,1,0:T(8,128)S(1)} %copy-done.1, s32[2,24,128]{2,1,0:T(8,128)S(1)} %copy-done.2, ...), custom_call_target="tpu_custom_call" | custom-call | tf_op jit(solution)/shard_map/pallas_call | solution.py:320
  35.0 9.8 %collective-permute-start = (f32[12,8,128]{2,1,0:T(8,128)S(1)}, f32[12,8,128]{2,1,0:T(8,128)S(1)}, u32[]{:S(2)}, u32[]{:S(2)}) collective-permute-start(f32[12,8,128]{2,1,0:T(8,128)S(1)} %get-tuple-element.17), channel_id=1, source_target_pairs={{16,32},{32,16},{48,64},{64,48},{80,96},{96,80},{112,128},{128,112... | collective-permute-start | bytes 147464 | tf_op jit(solution)/shard_map/ppermute | solution.py:323
  44.9 4.8 %all-gather.2 = f32[24,8,128]{2,1,0:T(8,128)S(1)} all-gather(f32[12,8,128]{2,1,0:T(8,128)S(1)} %get-tuple-element.16), channel_id=4, replica_groups={{0,16},{1,17},{2,18},{3,19},{4,20},{5,21},{6,22},{7,23},{8,24},{9,25},{..., dimensions={0}, use_global_device_ids=true | all-gather | bytes 147456 | tf_op jit(solution)/shard_map/all_gather | solution.py:324
  49.6 0.0 collective-permute-done.gb
  49.6 0.3 shard_map.77
  50.0 1.2 %shard_map.78 = f32[8,24,128]{2,1,0:T(8,128)} custom-call(f32[9,32,128]{2,1,0:T(8,128)S(1)} %get-tuple-element.18.now, f32[9,32,128]{2,1,0:T(8,128)S(1)} %get-tuple-element.19.fixed, f32[9,32,128]{2,1,0:T(8,128)S(1)} %get-tuple-element.20.scale), custom_call_target="tpu_custom_call" | custom-call | tf_op jit(solution)/shard_map/pallas_call | solution.py:326
Async XLA Ops:
  15.6 18.6 %copy-start = (s32[2,24,128]{2,1,0:T(8,128)S(1)}, s32[2,24,128]{2,1,0:T(8,128)}, u32[]{:S(2)}) copy-start(s32[2,24,128]{2,1,0:T(8,128)} %zc.1) | copy-start | bytes 73732
  15.6 18.6 %copy-start.1 = (f32[2,24,128]{2,1,0:T(8,128)S(1)}, f32[2,24,128]{2,1,0:T(8,128)}, u32[]{:S(2)}) copy-start(f32[2,24,128]{2,1,0:T(8,128)} %zf.1) | copy-start | bytes 73732
  15.7 18.6 %copy-start.2 = (s32[2,24,128]{2,1,0:T(8,128)S(1)}, s32[2,24,128]{2,1,0:T(8,128)}, u32[]{:S(2)}) copy-start(s32[2,24,128]{2,1,0:T(8,128)} %mc.1) | copy-start | bytes 73732
  15.7 18.6 %copy-start.3 = (f32[2,24,128]{2,1,0:T(8,128)S(1)}, f32[2,24,128]{2,1,0:T(8,128)}, u32[]{:S(2)}) copy-start(f32[2,24,128]{2,1,0:T(8,128)} %mf.1) | copy-start | bytes 73732
  15.7 18.6 %copy-start.4 = (f32[2,24,128]{2,1,0:T(8,128)S(1)}, f32[2,24,128]{2,1,0:T(8,128)}, u32[]{:S(2)}) copy-start(f32[2,24,128]{2,1,0:T(8,128)} %cp.1) | copy-start | bytes 73732
  35.0 14.6 %collective-permute-start = (f32[12,8,128]{2,1,0:T(8,128)S(1)}, f32[12,8,128]{2,1,0:T(8,128)S(1)}, u32[]{:S(2)}, u32[]{:S(2)}) collective-permute-start(f32[12,8,128]{2,1,0:T(8,128)S(1)} %get-tuple-element.17), channel_id=1, source_target_pairs={{16,32},{32,16},{48,64},{64,48},{80,96},{96,80},{112,128},{128,112... | collective-permute-start | bytes 147464 | tf_op jit(solution)/shard_map/ppermute | solution.py:323

commit v11 on v9

--- a/solution.py
+++ b/solution.py
@@ -11,7 +11,7 @@
 F32 = jnp.float32
 I32 = jnp.int32
 SECTORS = 16
-Z_PAIRS = [[4 * y + c, 4 * y + 2 + c] for y in range(4) for c in range(2)]
+Z_PAIRS = [[4 * y + 2 + c, 4 * y + c] for y in range(4) for c in range(2)]
 SIDES = [[4 * y + 2 * z + c for y in range(4) for c in range(2)] for z in range(2)]
 
 
@@ -135,7 +135,7 @@
     rows = zc.shape[1]
     me, band = lax.axis_index("lon"), lax.axis_index("lat")
     core = me & 1
-    across = 1 - ((me >> 1) & 1)
+    across = (me >> 1) & 1
     lane = iota((rows, 128), 1)
     outer = unfold(swapped[across, 9 * rows : 9 * rows + 8])
     outer = jnp.where(core == 0, outer, pltpu.roll(outer, 4, 1))

time: 51.4 us -> 51.3 us (level)
  no operation moved by 1% of the time
where the time goes in v11:
time: 51.3 us; the launch traced here: 51.1 us
  blocking collectives  37.3 us (73%)
  starting transfers between devices  9.83 us (19%)
  Pallas kernels  3.86 us (8%)
    all_gather x1, blocking collectives, body(): swapped = lax.all_gather(send, 'lon', axis_index_groups=Z_PAIRS)  18.6 us
    all_gather x1, blocking collectives, body(): circle = lax.all_gather(packed, 'lon', axis_index_groups=SIDES)  14 us
    ppermute x1, starting transfers between devices, body(): gb = lax.ppermute(eb, 'lat', lat_swaps)  9.83 us
    all_gather x1, blocking collectives, body(): ga = lax.all_gather(ea, ('lat', 'lon'), axis_index_groups=lat_pairs)  4.77 us
    pallas_call x1, Pallas kernels, body(): call(sweep_kernel, [((8, rows, 128), F32)], scratch_shapes=[pltpu.VMEM((8...  1.51 us
    pallas_call x1, Pallas kernels, body(): call(pack_kernel, [((9, rows, 128), F32), ((2, rows, 128), I32)], 32, scr...  1.06 us
  transfers between devices with their start and end apart: 1, of which 0 were waited for; matrix products, arithmetic and copies ran while one was open for 0% of the time, Pallas kernels for 0%

profile of v11, /device:TPU:6, one launch (start us, length us, event | category | flops | bytes accessed | tf_op | source)
XLA Modules:
  0.0 51.1 jit_solution(10921277702728474887)
XLA Ops:
  0.0 1.1 %shard_map.73 = (f32[9,24,128]{2,1,0:T(8,128)S(1)}, s32[2,24,128]{2,1,0:T(8,128)S(1)}) custom-call(f32[8,24,128]{2,1,0:T(8,128)} %bitcast.9, s32[2,24]{1,0:T(2,128)} %refs_1_.1, s32[2,24,128]{2,1,0:T(8,128)} %zc.1, f32[2,24,128]{2,1,0:T(8,128)} %zf.1, s32[2,24,128]{2,1,0:T(8,128)} %mc.1, f32[2,24,128]{2,1,0:T(8,128)} %mf.1, f32[2,24,128]{2,1,0:T(8,128)} %cp.1), custom_call_target="tpu_custom_call" | custom-call | tf_op jit(solution)/shard_map/pallas_call | solution.py:294
  1.1 14.0 %all-gather = f32[72,24,128]{2,1,0:T(8,128)S(1)} all-gather(f32[9,24,128]{2,1,0:T(8,128)S(1)} %get-tuple-element.10), channel_id=2, replica_groups={{0,1,4,5,8,9,12,13},{2,3,6,7,10,11,14,15},{16,17,20,21,24,25,28,29},{18..., dimensions={0}, use_global_device_ids=true | all-gather | bytes 995328 | tf_op jit(solution)/shard_map/all_gather | solution.py:302
  15.1 0.3 shard_map.75
  15.4 0.3 shard_map.74.keep
  15.6 0.0 copy-start
  15.6 0.0 copy-start.1
  15.7 0.0 copy-start.2
  15.7 0.0 copy-start.3
  15.7 0.0 copy-start.4
  15.7 18.6 %all-gather.1 = f32[448,128]{1,0:T(8,128)S(1)} all-gather(f32[224,128]{1,0:T(8,128)S(1)} %shard_map.75), channel_id=3, replica_groups={{2,0},{3,1},{6,4},{7,5},{10,8},{11,9},{14,12},{15,13},{18,16},{19,17},{..., dimensions={0}, use_global_device_ids=true | all-gather | bytes 344064 | tf_op jit(solution)/shard_map/all_gather | solution.py:305
  34.2 0.0 copy-done
  34.3 0.0 copy-done.1
  34.3 0.0 copy-done.2
  34.3 0.0 copy-done.3
  34.3 0.0 copy-done.4
  34.3 0.7 %shard_map.76 = (f32[15,24,128]{2,1,0:T(8,128)S(1)}, f32[12,8,128]{2,1,0:T(8,128)S(1)}, f32[12,8,128]{2,1,0:T(8,128)S(1)}) custom-call(f32[240,128]{1,0:T(8,128)S(1)} %shard_map.74.keep, f32[2,224,128]{2,1,0:T(8,128)S(1)} %bitcast.7, s32[2,24,128]{2,1,0:T(8,128)S(1)} %copy-done, f32[2,24,128]{2,1,0:T(8,128)S(1)} %copy-done.1, s32[2,24,128]{2,1,0:T(8,128)S(1)} %copy-done.2, ...), custom_call_target="tpu_custom_call" | custom-call | tf_op jit(solution)/shard_map/pallas_call | solution.py:306
  35.0 9.8 %collective-permute-start = (f32[12,8,128]{2,1,0:T(8,128)S(1)}, f32[12,8,128]{2,1,0:T(8,128)S(1)}, u32[]{:S(2)}, u32[]{:S(2)}) collective-permute-start(f32[12,8,128]{2,1,0:T(8,128)S(1)} %get-tuple-element.14), channel_id=1, source_target_pairs={{16,32},{32,16},{48,64},{64,48},{80,96},{96,80},{112,128},{128,112... | collective-permute-start | bytes 147464 | tf_op jit(solution)/shard_map/ppermute | solution.py:309
  44.9 4.8 %all-gather.2 = f32[24,8,128]{2,1,0:T(8,128)S(1)} all-gather(f32[12,8,128]{2,1,0:T(8,128)S(1)} %get-tuple-element.13), channel_id=4, replica_groups={{0,16},{1,17},{2,18},{3,19},{4,20},{5,21},{6,22},{7,23},{8,24},{9,25},{..., dimensions={0}, use_global_device_ids=true | all-gather | bytes 147456 | tf_op jit(solution)/shard_map/all_gather | solution.py:310
  49.6 0.0 collective-permute-done.gb
  49.6 1.5 %shard_map.77 = f32[8,24,128]{2,1,0:T(8,128)} custom-call(f32[15,24,128]{2,1,0:T(8,128)S(1)} %get-tuple-element.12.main, f32[2,12,8,128]{3,2,1,0:T(8,128)S(1)} %bitcast.8, f32[12,8,128]{2,1,0:T(8,128)S(1)} %collective-permute-done.gb), custom_call_target="tpu_custom_call" | custom-call | tf_op jit(solution)/shard_map/pallas_call | solution.py:311
Async XLA Ops:
  15.6 18.6 %copy-start = (s32[2,24,128]{2,1,0:T(8,128)S(1)}, s32[2,24,128]{2,1,0:T(8,128)}, u32[]{:S(2)}) copy-start(s32[2,24,128]{2,1,0:T(8,128)} %zc.1) | copy-start | bytes 73732
  15.6 18.6 %copy-start.1 = (f32[2,24,128]{2,1,0:T(8,128)S(1)}, f32[2,24,128]{2,1,0:T(8,128)}, u32[]{:S(2)}) copy-start(f32[2,24,128]{2,1,0:T(8,128)} %zf.1) | copy-start | bytes 73732
  15.7 18.6 %copy-start.2 = (s32[2,24,128]{2,1,0:T(8,128)S(1)}, s32[2,24,128]{2,1,0:T(8,128)}, u32[]{:S(2)}) copy-start(s32[2,24,128]{2,1,0:T(8,128)} %mc.1) | copy-start | bytes 73732
  15.7 18.6 %copy-start.3 = (f32[2,24,128]{2,1,0:T(8,128)S(1)}, f32[2,24,128]{2,1,0:T(8,128)}, u32[]{:S(2)}) copy-start(f32[2,24,128]{2,1,0:T(8,128)} %mf.1) | copy-start | bytes 73732
  15.7 18.6 %copy-start.4 = (f32[2,24,128]{2,1,0:T(8,128)S(1)}, f32[2,24,128]{2,1,0:T(8,128)}, u32[]{:S(2)}) copy-start(f32[2,24,128]{2,1,0:T(8,128)} %cp.1) | copy-start | bytes 73732
  35.0 14.6 %collective-permute-start = (f32[12,8,128]{2,1,0:T(8,128)S(1)}, f32[12,8,128]{2,1,0:T(8,128)S(1)}, u32[]{:S(2)}, u32[]{:S(2)}) collective-permute-start(f32[12,8,128]{2,1,0:T(8,128)S(1)} %get-tuple-element.14), channel_id=1, source_target_pairs={{16,32},{32,16},{48,64},{64,48},{80,96},{96,80},{112,128},{128,112... | collective-permute-start | bytes 147464 | tf_op jit(solution)/shard_map/ppermute | solution.py:309
